TPU v7x, 32 devices: a whole 2x2x4 slice. The times are simulated.
32 devices in a mesh: node: 4 (over y, x), space: 8 (over z, core).
Axes of the slice: x: 2, y: 2, z: 4, core: 2. Of those that a mesh axis runs over, the one named last changes fastest.
Arguments:
- start: float32 [4, 32, 64, 256], P(None, 'space'), may hold values from -6 to 6
- guess: float32 [4, 4, 32, 64, 256], P('node', None, 'space'), may hold values from -6 to 6
- heat_mask: int32 [32, 64, 256], P('space'), may hold values 0 or 1
- solid_mask: int32 [32, 64, 256], P('space'), may hold values 0 or 1
Outputs:
- iterate: float32 [4, 4, 32, 64, 256], P('node', None, 'space')
All inputs are finite; a program needn't handle non-finite values. No bound on the sum of `heat_mask` or of `solid_mask` on one device may be relied on, other than what follows from the above.
Results may differ from a plain program's by a relative error of at most 0.0001.
Values sent between devices are 32-bit elements; how exact they have to be, the bound alone decides.
No kernel may reach another device: no remote copies, remote signals or barrier semaphores. Data moves between devices by JAX's collectives and lax.ppermute only.
A program may use at most 64 MiB of HBM per device.

v0:
```python
import jax
import jax.numpy as jnp
from jax import lax
from jax.sharding import PartitionSpec as P

SWEEPS = 2
JACOBI = 3


advect_rate = 0.25
buoyancy = 0.5
heating = 1.0
diffusion = (0.5, 0.5, 0.5, 0.35)


def extended(cells, sides, width):
    for axis, dim in sides:
        count = lax.axis_size(axis)
        ends = count - 1
        head = lax.slice_in_dim(cells, 0, width, axis=dim)
        tail = lax.slice_in_dim(cells, cells.shape[dim] - width, cells.shape[dim], axis=dim)
        cells = jnp.concatenate(
            [
                lax.ppermute(tail, axis, [(i, (i + 1) % count) for i in range(ends)]),
                cells,
                lax.ppermute(head, axis, [((i + 1) % count, i) for i in range(ends)]),
            ],
            axis=dim,
        )
    return cells


def legendre_value(order, place):
    previous = 1.0
    current = place
    for degree in range(1, order):
        following = ((2 * degree + 1) * place * current - degree * previous) / (degree + 1)
        previous = current
        current = following
    return current


def radau_tables(count):

    def radau_poly(place):
        return legendre_value(count, place) - legendre_value(count - 1, place)

    samples = 4000 * count
    roots_found = []
    left_end = -1.0
    left_value = radau_poly(left_end)
    for index in range(1, samples + 1):
        right_end = -1.0 + (2.0 - 1e-07) * index / samples
        right_value = radau_poly(right_end)
        if left_value * right_value < 0.0:
            low_end = left_end
            high_end = right_end
            low_value = left_value
            for repeat in range(200):
                middle = 0.5 * (low_end + high_end)
                middle_value = radau_poly(middle)
                if low_value * middle_value <= 0.0:
                    high_end = middle
                else:
                    low_end = middle
                    low_value = middle_value
            roots_found.append(0.5 * (low_end + high_end))
        left_end = right_end
        left_value = right_value
    points = [(value + 1.0) / 2.0 for value in roots_found[: count - 1]] + [1.0]
    table = []
    for row in range(count):
        table.append([0.0] * count)
    for column in range(count):
        coefficients = [1.0]
        for other in range(count):
            if other == column:
                continue
            scale = 1.0 / (points[column] - points[other])
            widened = [0.0] * (len(coefficients) + 1)
            for index in range(len(coefficients)):
                widened[index + 1] += coefficients[index] * scale
                widened[index] -= points[other] * coefficients[index] * scale
            coefficients = widened
        for row in range(count):
            total = 0.0
            for index in range(len(coefficients)):
                total += coefficients[index] * points[row] ** (index + 1) / (index + 1)
            table[row][column] = total
    return (points, table)


def shifted(field, axis, offset):
    length = field.shape[axis]
    zero_shape = list(field.shape)
    zero_shape[axis] = abs(offset)
    zeros = jnp.zeros(zero_shape, field.dtype)
    if offset > 0:
        kept = lax.slice_in_dim(field, offset, length, axis=axis)
        return jnp.concatenate([kept, zeros], axis)
    kept = lax.slice_in_dim(field, 0, length + offset, axis=axis)
    return jnp.concatenate([zeros, kept], axis)


def neighbour_sum(padded):
    centre = padded[:, 1:-1]
    total = padded[:, 2:] + padded[:, :-2]
    total = total + shifted(centre, 2, 1) + shifted(centre, 2, -1)
    total = total + shifted(centre, 3, 1) + shifted(centre, 3, -1)
    return total


def tendency(padded, heat_mask, solid_mask):
    centre = padded[:, 1:-1]
    grad_x = (padded[:, 2:] - padded[:, :-2]) * 0.5
    grad_z = (shifted(centre, 2, 1) - shifted(centre, 2, -1)) * 0.5
    grad_y = (shifted(centre, 3, 1) - shifted(centre, 3, -1)) * 0.5
    transport = centre[0:1] * grad_x + centre[1:2] * grad_y + centre[2:3] * grad_z
    rates = jnp.asarray(diffusion, jnp.float32).reshape(4, 1, 1, 1)
    diffusive = rates * (neighbour_sum(padded) - 6.0 * centre)
    blank = jnp.zeros_like(centre[3])
    source = jnp.stack(
        [blank, blank, buoyancy * centre[3], heating * heat_mask.astype(jnp.float32)]
    )
    fluid = 1.0 - solid_mask.astype(jnp.float32)
    keeper = jnp.stack([fluid, fluid, fluid, jnp.ones_like(fluid)])
    total = (-advect_rate * transport + diffusive + source) * keeper
    return (total, diffusive)


def on_device(start, guess, heat_mask, solid_mask):
    nodes = lax.axis_size("node")
    points_list, table_list = radau_tables(nodes)
    table = jnp.asarray(table_list, jnp.float32)
    points = jnp.asarray(points_list, jnp.float32)
    me_node = lax.axis_index("node")
    point = lax.dynamic_index_in_dim(points, me_node, 0, keepdims=False)
    rates = jnp.asarray(diffusion, jnp.float32).reshape(4, 1, 1, 1)
    coupling = point * rates
    denom_field = 1.0 + 6.0 * coupling
    current = guess[0]
    for sweep in range(SWEEPS):
        padded = extended(current, (("space", 1),), 1)
        local_term, diffusive = tendency(padded, heat_mask, solid_mask)
        flat = local_term.reshape(1, nodes, -1)
        mixed = jnp.einsum(
            "os,snf->onf",
            table,
            lax.all_to_all(flat, "node", split_axis=1, concat_axis=0, tiled=True),
            precision=lax.Precision.HIGHEST,
        )
        summed = lax.all_to_all(mixed, "node", split_axis=0, concat_axis=1, tiled=True).reshape(
            local_term.shape
        )
        right = start + summed - point * diffusive
        for level in range(JACOBI):
            if level > 0:
                padded = extended(current, (("space", 1),), 1)
            current = (right + coupling * neighbour_sum(padded)) / denom_field
    return current[None]


def solution(mesh):
    in_specs = (
        P(None, "space", None, None),
        P("node", None, "space", None, None),
        P("space", None, None),
        P("space", None, None),
    )
    out_specs = P("node", None, "space", None, None)
    return jax.shard_map(
        on_device, mesh=mesh, in_specs=in_specs, out_specs=out_specs, check_vma=False
    )
```

profile of v0, /device:TPU:8, one launch (start us, length us, event | category | flops | bytes accessed | tf_op | source)
XLA Modules:
  0.0 162.3 jit_solution(4151831396317921578)
XLA Ops:
  3.1 3.6 %collective-permute-start = (f32[4,1,64,256]{3,2,1,0:T(8,128)S(1)}, f32[4,1,64,256]{3,2,1,0:T(8,128)S(1)}, u32[]{:S(2)}, u32[]{:S(2)}) collective-permute-start(f32[4,1,64,256]{3,2,1,0:T(8,128)S(1)} %get-tuple-element.52), channel_id=1, source_target_pairs={{1,0},{2,1},{3,2},{4,3},{5,4},{6,5},{7,6},{9,8},{10,9},{11,10},{12... | collective-permute-start | bytes 786440 | tf_op jit(solution)/shard_map/ppermute | solution.py:26
  11.3 2.0 %fusion.1 = (f32[4,4,64,256]{3,2,1,0:T(8,128)S(1)}, f32[4,4,64,256]{3,2,1,0:T(8,128)}) fusion(f32[1,4,64,256]{3,2,1,0:T(8,128)S(1)} %convert_bitcast_fusion, f32[1,4,64,256]{3,2,1,0:T(8,128)S(1)} %get-tuple-element.49, f32[1,4,64,256]{3,2,1,0:T(8,128)S(1)} %subtract_bitcast_fusion, f32[4,4,63,256]{3,2,1,0:T(8,128)S(1)} %get-tuple-element.56, ...), kind=kLoop, calls=%fused_computation.5 | loop fusion | flops 7077888 | bytes 9396272 | tf_op jit(solution)/shard_map/mul | solution.py:127
  14.4 18.2 %all_to_all.16 = f32[1,4,65536]{2,0,1:T(1,128)S(1)} all-to-all(f32[1,4,65536]{2,0,1:T(1,128)S(1)} %reshape.78), channel_id=1, replica_groups=mesh['node'=4,'space'=8] {'node'}, dimensions={1} | all-to-all | bytes 2097152 | tf_op jit(solution)/shard_map/all_to_all | solution.py:149
  32.6 2.3 %convolution_bitcast_fusion.1 = f32[4,1,65536]{2,0,1:T(4,128)S(1)} fusion(f32[4,4]{1,0:T(4,128)S(1)} %copy-done.10, f32[1,4,65536]{2,0,1:T(1,128)S(1)} %all_to_all.16), kind=kOutput, calls=%fused_computation.1 | convolution fusion | flops 12582912 | bytes 2097216 | tf_op jit(solution)/shard_map/os,snf->onf/dot_general | solution.py:146
  34.9 2.1 %copy.10 = f32[4,1,65536]{2,1,0:T(1,128)} copy(f32[4,1,65536]{2,0,1:T(4,128)S(1)} %convolution_bitcast_fusion.1) | data formatting | bytes 2097152 | tf_op jit(solution)/shard_map/os,snf->onf/dot_general | solution.py:146
  37.0 3.5 %all-to-all-start.1 = ((f32[4,1,65536]{2,1,0:T(1,128)}), f32[4,1,65536]{2,1,0:T(1,128)S(1)}, u32[]{:S(2)}, u32[]{:S(2)}) async-start(f32[4,1,65536]{2,1,0:T(1,128)} %copy.10), calls=%async_computation.1 | async-start | bytes 2097152 | tf_op jit(solution)/shard_map/all_to_all | solution.py:152
  42.5 12.7 %all-to-all-done.1 = f32[4,1,65536]{2,1,0:T(1,128)S(1)} async-done(((f32[4,1,65536]{2,1,0:T(1,128)}), f32[4,1,65536]{2,1,0:T(1,128)S(1)}, u32[]{:S(2)}, u32[]{:S(2)}) %all-to-all-start.1) | async-done | bytes 1048608 | tf_op jit(solution)/shard_map/all_to_all | solution.py:152
  55.3 3.0 %reduce = f32[4,65536]{1,0:T(4,128)S(1)} reduce(f32[4,1,65536]{2,1,0:T(1,128)S(1)} %all-to-all-done.1, f32[]{:T(128)} %constant.88), dimensions={1}, to_apply=%all_to_all.9.reduce_sub_computation | reduce | bytes 2097156 | tf_op jit(solution)/shard_map/all_to_all | solution.py:152
  63.4 2.6 %collective-permute-start.3 = (f32[4,1,64,256]{3,2,1,0:T(8,128)S(1)}, f32[4,1,64,256]{3,2,1,0:T(8,128)S(1)}, u32[]{:S(2)}, u32[]{:S(2)}) collective-permute-start(f32[4,1,64,256]{3,2,1,0:T(8,128)S(1)} %get-tuple-element.46), channel_id=1, source_target_pairs={{0,1},{1,2},{2,3},{3,4},{4,5},{5,6},{6,7},{8,9},{9,10},{10,11},{11... | collective-permute-start | bytes 786440 | tf_op jit(solution)/shard_map/ppermute | solution.py:24
  67.3 3.8 %collective-permute-done.3 = f32[4,1,64,256]{3,2,1,0:T(8,128)S(1)} collective-permute-done((f32[4,1,64,256]{3,2,1,0:T(8,128)S(1)}, f32[4,1,64,256]{3,2,1,0:T(8,128)S(1)}, u32[]{:S(2)}, u32[]{:S(2)}) %collective-permute-start.3) | collective-permute-done | bytes 262176 | tf_op jit(solution)/shard_map/ppermute | solution.py:24
  72.3 1.9 %collective-permute-start.4 = (f32[4,1,64,256]{3,2,1,0:T(8,128)S(1)}, f32[4,1,64,256]{3,2,1,0:T(8,128)S(1)}, u32[]{:S(2)}, u32[]{:S(2)}) collective-permute-start(f32[4,1,64,256]{3,2,1,0:T(8,128)S(1)} %get-tuple-element.39), channel_id=1, source_target_pairs={{1,0},{2,1},{3,2},{4,3},{5,4},{6,5},{7,6},{9,8},{10,9},{11,10},{12... | collective-permute-start | bytes 786440 | tf_op jit(solution)/shard_map/ppermute | solution.py:26
  74.3 2.4 %collective-permute-start.5 = (f32[4,1,64,256]{3,2,1,0:T(8,128)S(1)}, f32[4,1,64,256]{3,2,1,0:T(8,128)S(1)}, u32[]{:S(2)}, u32[]{:S(2)}) collective-permute-start(f32[4,1,64,256]{3,2,1,0:T(8,128)S(1)} %get-tuple-element.40), channel_id=1, source_target_pairs={{0,1},{1,2},{2,3},{3,4},{4,5},{5,6},{6,7},{8,9},{9,10},{10,11},{11... | collective-permute-start | bytes 786440 | tf_op jit(solution)/shard_map/ppermute | solution.py:24
  78.1 3.8 %collective-permute-done.5 = f32[4,1,64,256]{3,2,1,0:T(8,128)S(1)} collective-permute-done((f32[4,1,64,256]{3,2,1,0:T(8,128)S(1)}, f32[4,1,64,256]{3,2,1,0:T(8,128)S(1)}, u32[]{:S(2)}, u32[]{:S(2)}) %collective-permute-start.5) | collective-permute-done | bytes 262176 | tf_op jit(solution)/shard_map/ppermute | solution.py:24
  83.1 1.9 %collective-permute-start.7 = (f32[4,1,64,256]{3,2,1,0:T(8,128)S(1)}, f32[4,1,64,256]{3,2,1,0:T(8,128)S(1)}, u32[]{:S(2)}, u32[]{:S(2)}) collective-permute-start(f32[4,1,64,256]{3,2,1,0:T(8,128)S(1)} %get-tuple-element.29), channel_id=1, source_target_pairs={{0,1},{1,2},{2,3},{3,4},{4,5},{5,6},{6,7},{8,9},{9,10},{10,11},{11... | collective-permute-start | bytes 786440 | tf_op jit(solution)/shard_map/ppermute | solution.py:24
  85.1 3.6 %collective-permute-start.6 = (f32[4,1,64,256]{3,2,1,0:T(8,128)S(1)}, f32[4,1,64,256]{3,2,1,0:T(8,128)S(1)}, u32[]{:S(2)}, u32[]{:S(2)}) collective-permute-start(f32[4,1,64,256]{3,2,1,0:T(8,128)S(1)} %get-tuple-element.30), channel_id=1, source_target_pairs={{1,0},{2,1},{3,2},{4,3},{5,4},{6,5},{7,6},{9,8},{10,9},{11,10},{12... | collective-permute-start | bytes 786440 | tf_op jit(solution)/shard_map/ppermute | solution.py:26
  92.6 2.0 %fusion.3 = (f32[4,4,64,256]{3,2,1,0:T(8,128)S(1)}, f32[4,4,64,256]{3,2,1,0:T(8,128)}) fusion(f32[1,4,64,256]{3,2,1,0:T(8,128)S(1)} %convert_bitcast_fusion, f32[1,4,64,256]{3,2,1,0:T(8,128)S(1)} %copy-done.6, f32[1,4,64,256]{3,2,1,0:T(8,128)S(1)} %get-tuple-element.28, f32[4,4,63,256]{3,2,1,0:T(8,128)S(1)} %get-tuple-element.34, ...), kind=kLoop, calls=%fused_computation.7 | loop fusion | flops 7077888 | bytes 9396272 | tf_op jit(solution)/shard_map/mul | solution.py:127
  95.7 17.1 %all_to_all.17 = f32[1,4,65536]{2,0,1:T(1,128)S(1)} all-to-all(f32[1,4,65536]{2,0,1:T(1,128)S(1)} %reshape.81), channel_id=1, replica_groups=mesh['node'=4,'space'=8] {'node'}, dimensions={1} | all-to-all | bytes 2097152 | tf_op jit(solution)/shard_map/all_to_all | solution.py:149
  112.8 2.3 %convolution_bitcast_fusion = f32[4,1,65536]{2,0,1:T(4,128)S(1)} fusion(f32[4,4]{1,0:T(4,128)S(1)} %copy-done.10, f32[1,4,65536]{2,0,1:T(1,128)S(1)} %all_to_all.17), kind=kOutput, calls=%fused_computation | convolution fusion | flops 12582912 | bytes 2097216 | tf_op jit(solution)/shard_map/os,snf->onf/dot_general | solution.py:146
  116.2 17.6 %all_to_all.18 = f32[4,1,65536]{2,1,0:T(1,128)S(1)} all-to-all(f32[4,1,65536]{2,1,0:T(1,128)S(1)} %copy.11), channel_id=1, replica_groups=mesh['node'=4,'space'=8] {'node'}, dimensions={0} | all-to-all | bytes 2097152 | tf_op jit(solution)/shard_map/all_to_all | solution.py:152
  133.8 3.0 %reduce.1 = f32[4,65536]{1,0:T(4,128)S(1)} reduce(f32[4,1,65536]{2,1,0:T(1,128)S(1)} %all_to_all.18, f32[]{:T(128)} %constant.88), dimensions={1}, to_apply=%all_to_all.11.reduce_sub_computation | reduce | bytes 2097156 | tf_op jit(solution)/shard_map/all_to_all | solution.py:152
  142.0 2.4 %collective-permute-start.9 = (f32[4,1,64,256]{3,2,1,0:T(8,128)S(1)}, f32[4,1,64,256]{3,2,1,0:T(8,128)S(1)}, u32[]{:S(2)}, u32[]{:S(2)}) collective-permute-start(f32[4,1,64,256]{3,2,1,0:T(8,128)S(1)} %get-tuple-element.24), channel_id=1, source_target_pairs={{0,1},{1,2},{2,3},{3,4},{4,5},{5,6},{6,7},{8,9},{9,10},{10,11},{11... | collective-permute-start | bytes 786440 | tf_op jit(solution)/shard_map/ppermute | solution.py:24
  145.9 3.8 %collective-permute-done.9 = f32[4,1,64,256]{3,2,1,0:T(8,128)S(1)} collective-permute-done((f32[4,1,64,256]{3,2,1,0:T(8,128)S(1)}, f32[4,1,64,256]{3,2,1,0:T(8,128)S(1)}, u32[]{:S(2)}, u32[]{:S(2)}) %collective-permute-start.9) | collective-permute-done | bytes 262176 | tf_op jit(solution)/shard_map/ppermute | solution.py:24
  152.8 2.4 %collective-permute-start.11 = (f32[4,1,64,256]{3,2,1,0:T(8,128)S(1)}, f32[4,1,64,256]{3,2,1,0:T(8,128)S(1)}, u32[]{:S(2)}, u32[]{:S(2)}) collective-permute-start(f32[4,1,64,256]{3,2,1,0:T(8,128)S(1)} %get-tuple-element.14), channel_id=1, source_target_pairs={{0,1},{1,2},{2,3},{3,4},{4,5},{5,6},{6,7},{8,9},{9,10},{10,11},{11... | collective-permute-start | bytes 786440 | tf_op jit(solution)/shard_map/ppermute | solution.py:24
  156.7 3.8 %collective-permute-done.11 = f32[4,1,64,256]{3,2,1,0:T(8,128)S(1)} collective-permute-done((f32[4,1,64,256]{3,2,1,0:T(8,128)S(1)}, f32[4,1,64,256]{3,2,1,0:T(8,128)S(1)}, u32[]{:S(2)}, u32[]{:S(2)}) %collective-permute-start.11) | collective-permute-done | bytes 262176 | tf_op jit(solution)/shard_map/ppermute | solution.py:24
  (74 shorter events, 39.6 us)
Async XLA Ops:
  0.0 6.8 %copy-start = (f32[1,4,4,64,256]{4,3,2,1,0:T(8,128)S(1)}, f32[1,4,4,64,256]{4,3,2,1,0:T(8,128)}, u32[]{:S(2)}) copy-start(f32[1,4,4,64,256]{4,3,2,1,0:T(8,128)} %param.10) | copy-start | bytes 3145732
  1.2 7.9 %collective-permute-start.1 = (f32[4,1,64,256]{3,2,1,0:T(8,128)S(1)}, f32[4,1,64,256]{3,2,1,0:T(8,128)S(1)}, u32[]{:S(2)}, u32[]{:S(2)}) collective-permute-start(f32[4,1,64,256]{3,2,1,0:T(8,128)S(1)} %get-tuple-element.51), channel_id=1, source_target_pairs={{0,1},{1,2},{2,3},{3,4},{4,5},{5,6},{6,7},{8,9},{9,10},{10,11},{11... | collective-permute-start | bytes 786440 | tf_op jit(solution)/shard_map/ppermute | solution.py:24
  3.1 7.5 %collective-permute-start = (f32[4,1,64,256]{3,2,1,0:T(8,128)S(1)}, f32[4,1,64,256]{3,2,1,0:T(8,128)S(1)}, u32[]{:S(2)}, u32[]{:S(2)}) collective-permute-start(f32[4,1,64,256]{3,2,1,0:T(8,128)S(1)} %get-tuple-element.52), channel_id=1, source_target_pairs={{1,0},{2,1},{3,2},{4,3},{5,4},{6,5},{7,6},{9,8},{10,9},{11,10},{12... | collective-permute-start | bytes 786440 | tf_op jit(solution)/shard_map/ppermute | solution.py:26
  7.0 1.0 copy-start.7
  7.9 0.9 copy-start.8
  8.9 1.7 %copy-start.5 = (f32[1,4,64,256]{3,2,1,0:T(8,128)}, f32[1,4,64,256]{3,2,1,0:T(8,128)S(1)}, u32[]{:S(2)}) copy-start(f32[1,4,64,256]{3,2,1,0:T(8,128)S(1)} %subtract_bitcast_fusion) | copy-start | bytes 786436
  14.4 18.2 %copy-start.10 = (f32[4,4]{1,0:T(4,128)S(1)}, f32[4,4]{1,0:T(4,128)}, u32[]{:S(2)}) copy-start(f32[4,4]{1,0:T(4,128)} %constant.8.clone) | copy-start | bytes 196
  37.0 18.3 %all-to-all-start.1 = ((f32[4,1,65536]{2,1,0:T(1,128)}), f32[4,1,65536]{2,1,0:T(1,128)S(1)}, u32[]{:S(2)}, u32[]{:S(2)}) async-start(f32[4,1,65536]{2,1,0:T(1,128)} %copy.10), calls=%async_computation.1 | async-start | bytes 2097152 | tf_op jit(solution)/shard_map/all_to_all | solution.py:152
  40.5 0.7 copy-start.11
  58.3 1.2 copy-start.1
  58.3 1.5 copy-start.3
  61.5 5.8 %collective-permute-start.2 = (f32[4,1,64,256]{3,2,1,0:T(8,128)S(1)}, f32[4,1,64,256]{3,2,1,0:T(8,128)S(1)}, u32[]{:S(2)}, u32[]{:S(2)}) collective-permute-start(f32[4,1,64,256]{3,2,1,0:T(8,128)S(1)} %get-tuple-element.45), channel_id=1, source_target_pairs={{1,0},{2,1},{3,2},{4,3},{5,4},{6,5},{7,6},{9,8},{10,9},{11,10},{12... | collective-permute-start | bytes 786440 | tf_op jit(solution)/shard_map/ppermute | solution.py:26
  63.4 7.7 %collective-permute-start.3 = (f32[4,1,64,256]{3,2,1,0:T(8,128)S(1)}, f32[4,1,64,256]{3,2,1,0:T(8,128)S(1)}, u32[]{:S(2)}, u32[]{:S(2)}) collective-permute-start(f32[4,1,64,256]{3,2,1,0:T(8,128)S(1)} %get-tuple-element.46), channel_id=1, source_target_pairs={{0,1},{1,2},{2,3},{3,4},{4,5},{5,6},{6,7},{8,9},{9,10},{10,11},{11... | collective-permute-start | bytes 786440 | tf_op jit(solution)/shard_map/ppermute | solution.py:24
  72.3 5.8 %collective-permute-start.4 = (f32[4,1,64,256]{3,2,1,0:T(8,128)S(1)}, f32[4,1,64,256]{3,2,1,0:T(8,128)S(1)}, u32[]{:S(2)}, u32[]{:S(2)}) collective-permute-start(f32[4,1,64,256]{3,2,1,0:T(8,128)S(1)} %get-tuple-element.39), channel_id=1, source_target_pairs={{1,0},{2,1},{3,2},{4,3},{5,4},{6,5},{7,6},{9,8},{10,9},{11,10},{12... | collective-permute-start | bytes 786440 | tf_op jit(solution)/shard_map/ppermute | solution.py:26
  74.3 7.7 %collective-permute-start.5 = (f32[4,1,64,256]{3,2,1,0:T(8,128)S(1)}, f32[4,1,64,256]{3,2,1,0:T(8,128)S(1)}, u32[]{:S(2)}, u32[]{:S(2)}) collective-permute-start(f32[4,1,64,256]{3,2,1,0:T(8,128)S(1)} %get-tuple-element.40), channel_id=1, source_target_pairs={{0,1},{1,2},{2,3},{3,4},{4,5},{5,6},{6,7},{8,9},{9,10},{10,11},{11... | collective-permute-start | bytes 786440 | tf_op jit(solution)/shard_map/ppermute | solution.py:24
  83.1 7.7 %collective-permute-start.7 = (f32[4,1,64,256]{3,2,1,0:T(8,128)S(1)}, f32[4,1,64,256]{3,2,1,0:T(8,128)S(1)}, u32[]{:S(2)}, u32[]{:S(2)}) collective-permute-start(f32[4,1,64,256]{3,2,1,0:T(8,128)S(1)} %get-tuple-element.29), channel_id=1, source_target_pairs={{0,1},{1,2},{2,3},{3,4},{4,5},{5,6},{6,7},{8,9},{9,10},{10,11},{11... | collective-permute-start | bytes 786440 | tf_op jit(solution)/shard_map/ppermute | solution.py:24
  85.1 7.5 %collective-permute-start.6 = (f32[4,1,64,256]{3,2,1,0:T(8,128)S(1)}, f32[4,1,64,256]{3,2,1,0:T(8,128)S(1)}, u32[]{:S(2)}, u32[]{:S(2)}) collective-permute-start(f32[4,1,64,256]{3,2,1,0:T(8,128)S(1)} %get-tuple-element.30), channel_id=1, source_target_pairs={{1,0},{2,1},{3,2},{4,3},{5,4},{6,5},{7,6},{9,8},{10,9},{11,10},{12... | collective-permute-start | bytes 786440 | tf_op jit(solution)/shard_map/ppermute | solution.py:26
  88.9 3.7 %copy-start.6 = (f32[1,4,64,256]{3,2,1,0:T(8,128)S(1)}, f32[1,4,64,256]{3,2,1,0:T(8,128)}, u32[]{:S(2)}) copy-start(f32[1,4,64,256]{3,2,1,0:T(8,128)} %copy-done.5) | copy-start | bytes 786436
  136.9 1.2 copy-start.2
  136.9 1.5 copy-start.4
  140.1 5.8 %collective-permute-start.8 = (f32[4,1,64,256]{3,2,1,0:T(8,128)S(1)}, f32[4,1,64,256]{3,2,1,0:T(8,128)S(1)}, u32[]{:S(2)}, u32[]{:S(2)}) collective-permute-start(f32[4,1,64,256]{3,2,1,0:T(8,128)S(1)} %get-tuple-element.23), channel_id=1, source_target_pairs={{1,0},{2,1},{3,2},{4,3},{5,4},{6,5},{7,6},{9,8},{10,9},{11,10},{12... | collective-permute-start | bytes 786440 | tf_op jit(solution)/shard_map/ppermute | solution.py:26
  142.0 7.7 %collective-permute-start.9 = (f32[4,1,64,256]{3,2,1,0:T(8,128)S(1)}, f32[4,1,64,256]{3,2,1,0:T(8,128)S(1)}, u32[]{:S(2)}, u32[]{:S(2)}) collective-permute-start(f32[4,1,64,256]{3,2,1,0:T(8,128)S(1)} %get-tuple-element.24), channel_id=1, source_target_pairs={{0,1},{1,2},{2,3},{3,4},{4,5},{5,6},{6,7},{8,9},{9,10},{10,11},{11... | collective-permute-start | bytes 786440 | tf_op jit(solution)/shard_map/ppermute | solution.py:24
  150.9 5.8 %collective-permute-start.10 = (f32[4,1,64,256]{3,2,1,0:T(8,128)S(1)}, f32[4,1,64,256]{3,2,1,0:T(8,128)S(1)}, u32[]{:S(2)}, u32[]{:S(2)}) collective-permute-start(f32[4,1,64,256]{3,2,1,0:T(8,128)S(1)} %get-tuple-element.13), channel_id=1, source_target_pairs={{1,0},{2,1},{3,2},{4,3},{5,4},{6,5},{7,6},{9,8},{10,9},{11,10},{12... | collective-permute-start | bytes 786440 | tf_op jit(solution)/shard_map/ppermute | solution.py:26
  152.8 7.7 %collective-permute-start.11 = (f32[4,1,64,256]{3,2,1,0:T(8,128)S(1)}, f32[4,1,64,256]{3,2,1,0:T(8,128)S(1)}, u32[]{:S(2)}, u32[]{:S(2)}) collective-permute-start(f32[4,1,64,256]{3,2,1,0:T(8,128)S(1)} %get-tuple-element.14), channel_id=1, source_target_pairs={{0,1},{1,2},{2,3},{3,4},{4,5},{5,6},{6,7},{8,9},{9,10},{10,11},{11... | collective-permute-start | bytes 786440 | tf_op jit(solution)/shard_map/ppermute | solution.py:24
  (1 other events, 0.7 us)
where the time goes:
time: 163 us; the launch traced here: 162 us
  blocking collectives  52.9 us (32%)
  waiting for transfers between devices  37.9 us (23%)
  starting transfers between devices  32.1 us (20%)
  other arithmetic  17.5 us (11%)
  local copies, waits for them, and re-layouts  16.7 us (10%)
  matrix products  4.68 us (3%)
    all_to_all x2, blocking collectives, on_device(): lax.all_to_all(flat, 'node', split_axis=1, concat_axis=0, tiled=True)  35.3 us
    all_to_all x1, blocking collectives, on_device(): lax.all_to_all(mixed, 'node', split_axis=0, concat_axis=1, tiled=True)  17.6 us
    ppermute x6, waiting for transfers between devices, extended(): lax.ppermute(tail, axis, [(i, (i + 1) % count) for i in range(ends)])  17.1 us
    ppermute x6, starting transfers between devices, extended(): lax.ppermute(head, axis, [((i + 1) % count, i) for i in range(ends)])  15 us
    ppermute x6, starting transfers between devices, extended(): lax.ppermute(tail, axis, [(i, (i + 1) % count) for i in range(ends)])  13.6 us
    all_to_all x1, waiting for transfers between devices, on_device(): lax.all_to_all(mixed, 'node', split_axis=0, concat_axis=1, tiled=True)  12.7 us
    ppermute x6, waiting for transfers between devices, extended(): lax.ppermute(head, axis, [((i + 1) % count, i) for i in range(ends)])  8.09 us
    all_to_all x2, other arithmetic, on_device(): lax.all_to_all(mixed, 'node', split_axis=0, concat_axis=1, tiled=True)  6.08 us
  transfers between devices with their start and end apart: 13, of which 12 were waited for; matrix products, arithmetic and copies ran while one was open for 2% of the time, Pallas kernels for 0%

commit v1 on v0

v1 whole, which is shorter than its diff:
```python
import functools

import jax
import jax.numpy as jnp
import numpy as np
from jax import lax
from jax.experimental import pallas as pl
from jax.experimental.pallas import tpu as pltpu
from jax.sharding import PartitionSpec as P

SWEEPS = 2
JACOBI = 3
LANES = 128
VMEM_LIMIT = 56 << 20

advect_rate = 0.25
buoyancy = 0.5
heating = 1.0
diffusion = (0.5, 0.5, 0.5, 0.35)


def legendre_value(order, place):
    previous = 1.0
    current = place
    for degree in range(1, order):
        following = ((2 * degree + 1) * place * current - degree * previous) / (degree + 1)
        previous = current
        current = following
    return current


def radau_tables(count):

    def radau_poly(place):
        return legendre_value(count, place) - legendre_value(count - 1, place)

    samples = 4000 * count
    roots_found = []
    left_end = -1.0
    left_value = radau_poly(left_end)
    for index in range(1, samples + 1):
        right_end = -1.0 + (2.0 - 1e-07) * index / samples
        right_value = radau_poly(right_end)
        if left_value * right_value < 0.0:
            low_end = left_end
            high_end = right_end
            low_value = left_value
            for repeat in range(200):
                middle = 0.5 * (low_end + high_end)
                middle_value = radau_poly(middle)
                if low_value * middle_value <= 0.0:
                    high_end = middle
                else:
                    low_end = middle
                    low_value = middle_value
            roots_found.append(0.5 * (low_end + high_end))
        left_end = right_end
        left_value = right_value
    points = [(value + 1.0) / 2.0 for value in roots_found[: count - 1]] + [1.0]
    table = []
    for row in range(count):
        table.append([0.0] * count)
    for column in range(count):
        coefficients = [1.0]
        for other in range(count):
            if other == column:
                continue
            scale = 1.0 / (points[column] - points[other])
            widened = [0.0] * (len(coefficients) + 1)
            for index in range(len(coefficients)):
                widened[index + 1] += coefficients[index] * scale
                widened[index] -= points[other] * coefficients[index] * scale
            coefficients = widened
        for row in range(count):
            total = 0.0
            for index in range(len(coefficients)):
                total += coefficients[index] * points[row] ** (index + 1) / (index + 1)
            table[row][column] = total
    return (points, table)


def round_up(value, step):
    return -(-value // step) * step


class Geometry:
    def __init__(self, nodes, planes, depth):
        overlap = SWEEPS * JACOBI if nodes > 1 else 0
        self.nodes, self.planes, self.depth = nodes, planes, depth
        self.window = -(-(depth + 2 * overlap * (nodes - 1)) // nodes)
        step = self.window - 2 * overlap
        assert step > 0 and planes >= JACOBI
        self.offset = [min(p * step, depth - self.window) for p in range(nodes)]
        first = [0] + [p * step + overlap for p in range(1, nodes)]
        last = first[1:] + [depth]
        self.first, self.count = first, [b - a for a, b in zip(first, last)]
        self.stride = self.window + 1
        while (planes * self.stride) % 8:
            self.stride += 1
        self.rows = planes * self.stride
        self.side = round_up(JACOBI * self.stride, 8)
        self.aux_side = round_up((JACOBI - 1) * self.stride, 8)
        self.low = 8 + self.side
        self.total = self.low + self.rows + self.side + 8
        self.back = max(self.count)
        while (planes * self.back) % 8:
            self.back += 1

    def span(self, reach):
        begin = (self.low - reach * self.stride) // 8 * 8
        end = round_up(self.low + (self.planes + reach) * self.stride, 8)
        assert begin - self.stride >= 0 and end + self.stride <= self.total
        return begin, end


def pack_kernel(geo, guess_ref, out_ref):
    blank = jnp.zeros((geo.stride - geo.window, LANES), jnp.float32)
    for p in range(geo.nodes):
        for f in range(4):
            for x in range(geo.planes):
                for h in range(2):
                    at = x * geo.stride
                    out_ref[p, f, h, at : at + geo.window] = guess_ref[
                        0, f, x, geo.offset[p] : geo.offset[p] + geo.window, h * LANES : (h + 1) * LANES
                    ]
                    out_ref[p, f, h, at + geo.window : at + geo.stride] = blank


def pack_aux_kernel(geo, me_ref, start_ref, heat_ref, solid_ref, out_ref):
    blank = jnp.zeros((geo.stride - geo.window, LANES), jnp.float32)
    me = me_ref[0]
    for p in range(geo.nodes):

        @pl.when(me == p)
        def _():
            rows = slice(geo.offset[p], geo.offset[p] + geo.window)
            for x in range(geo.planes):
                for h in range(2):
                    at = x * geo.stride
                    lanes = slice(h * LANES, (h + 1) * LANES)
                    for f in range(4):
                        out_ref[f, h, at : at + geo.window] = start_ref[f, x, rows, lanes]
                    out_ref[4, h, at : at + geo.window] = heating * heat_ref[x, rows, lanes].astype(jnp.float32)
                    out_ref[5, h, at : at + geo.window] = 1.0 - solid_ref[x, rows, lanes].astype(jnp.float32)
                    for f in range(6):
                        out_ref[f, h, at + geo.window : at + geo.stride] = blank


def sweep_kernel(
    geo, last, points, table, me_ref, coef_ref, own_ref, lo_ref, hi_ref, aux_ref, auxlo_ref, auxhi_ref, mask_ref, out_ref,
    field, tend, first, base, aux, sems,
):
    n, stride, low = geo.nodes, geo.stride, geo.low
    copies = [
        pltpu.make_async_copy(own_ref, field.at[:, :, :, pl.ds(low, geo.rows)], sems.at[0]),
        pltpu.make_async_copy(lo_ref, field.at[:, :, :, pl.ds(low - geo.side, geo.side)], sems.at[1]),
        pltpu.make_async_copy(hi_ref, field.at[:, :, :, pl.ds(low + geo.rows, geo.side)], sems.at[2]),
        pltpu.make_async_copy(aux_ref, aux.at[:, :, pl.ds(low, geo.rows)], sems.at[3]),
        pltpu.make_async_copy(auxlo_ref, aux.at[:, :, pl.ds(low - geo.aux_side, geo.aux_side)], sems.at[4]),
        pltpu.make_async_copy(auxhi_ref, aux.at[:, :, pl.ds(low + geo.rows, geo.aux_side)], sems.at[5]),
    ]
    for copy in copies:
        copy.start()
    lane = lax.broadcasted_iota(jnp.int32, (8, LANES), 1)
    is_first, is_last = lane == 0, lane == LANES - 1
    for copy in copies:
        copy.wait()

    def sides(a, b):
        ra, rb = pltpu.roll(a, 1, 1), pltpu.roll(b, 1, 1)
        la, lb = pltpu.roll(a, LANES - 1, 1), pltpu.roll(b, LANES - 1, 1)
        minus = (jnp.where(is_first, 0.0, ra), jnp.where(is_first, ra, rb))
        plus = (jnp.where(is_last, lb, la), jnp.where(is_last, 0.0, lb))
        return minus, plus

    begin, end = geo.span(JACOBI - 1)

    def node_tendency(j, _):
        for r in range(begin, end, 8):
            rows = pl.ds(r, 8)
            vel = []
            for h in range(2):
                vel.append([(-0.5 * advect_rate) * field[j, f, h, rows] for f in range(3)])
            for f in range(4):
                centre = [field[j, f, h, rows] for h in range(2)]
                minus, plus = sides(centre[0], centre[1])
                for h in range(2):
                    xp, xm = field[j, f, h, pl.ds(r + stride, 8)], field[j, f, h, pl.ds(r - stride, 8)]
                    zp, zm = field[j, f, h, pl.ds(r + 1, 8)], field[j, f, h, pl.ds(r - 1, 8)]
                    near = (xp + xm) + (zp + zm) + (plus[h] + minus[h])
                    moved = vel[h][0] * (xp - xm) + vel[h][1] * (plus[h] - minus[h]) + vel[h][2] * (zp - zm)
                    total = moved + diffusion[f] * (near - 6.0 * centre[h])
                    if f == 2:
                        total = total + buoyancy * field[j, 3, h, rows]
                    if f == 3:
                        total = total + aux[4, h, rows]
                    else:
                        total = total * aux[5, h, rows]
                    tend[j, f, h, rows] = total
                    base[j, f, h, rows] = near
        return 0

    lax.fori_loop(0, n, node_tendency, 0)

    def quadrature(t, _):
        rows = pl.ds(pl.multiple_of(begin + t * 8, 8), 8)
        mask = mask_ref[rows]
        for f in range(4):
            scale = [mask * (1.0 / (1.0 + 6.0 * points[m] * diffusion[f])) for m in range(n)]
            for h in range(2):
                slopes = [tend[j, f, h, rows] for j in range(n)]
                begun = aux[f, h, rows]
                for m in range(n):
                    c = points[m] * diffusion[f]
                    total = begun + (6.0 * c) * field[m, f, h, rows]
                    for j in range(n):
                        total = total + table[m][j] * slopes[j]
                    total = total * scale[m]
                    first[m, f, h, rows] = total
                    base[m, f, h, rows] = total - (c * scale[m]) * base[m, f, h, rows]
        return 0

    lax.fori_loop(0, (end - begin) // 8, quadrature, 0)

    def relax(source, target, reach, shift):
        rbegin, rend = geo.span(reach)

        def channel(k, _):
            m, f = k // 4, k % 4
            weight = coef_ref[k]
            for r in range(rbegin, rend, 8):
                rows = pl.ds(r, 8)
                mask = mask_ref[rows] * weight
                minus, plus = sides(source[m, f, 0, rows], source[m, f, 1, rows])
                for h in range(2):
                    near = (
                        (source[m, f, h, pl.ds(r + stride, 8)] + source[m, f, h, pl.ds(r - stride, 8)])
                        + (source[m, f, h, pl.ds(r + 1, 8)] + source[m, f, h, pl.ds(r - 1, 8)])
                        + (plus[h] + minus[h])
                    )
                    target[m, f, h, pl.ds(r - shift, 8)] = base[m, f, h, rows] + mask * near
            return 0

        lax.fori_loop(0, 4 * n, channel, 0)

    relax(first, tend, 1, 0)
    if not last:
        relax(tend, out_ref, 0, low)
        return
    relax(tend, first, 0, 0)
    me = me_ref[0]
    for start in sorted({a - b for a, b in zip(geo.first, geo.offset)}):
        hit = [p for p in range(n) if geo.first[p] - geo.offset[p] == start]
        chosen = functools.reduce(jnp.logical_or, [me == p for p in hit])
        count = min(geo.back, geo.stride - start)

        @pl.when(chosen)
        def _():
            def channel(k, _):
                m, f = k // 4, k % 4
                for h in range(2):
                    for x in range(geo.planes):
                        out_ref[m, f, h, x * geo.back : x * geo.back + count] = first[
                            m, f, h, low + x * stride + start : low + x * stride + start + count
                        ]
                return 0

            lax.fori_loop(0, 4 * n, channel, 0)


def unpack_kernel(geo, in_ref, out_ref):
    for p in range(geo.nodes):
        for f in range(4):
            for x in range(geo.planes):
                for h in range(2):
                    at = x * geo.back
                    out_ref[0, f, x, geo.first[p] : geo.first[p] + geo.count[p], h * LANES : (h + 1) * LANES] = in_ref[
                        p, f, h, at : at + geo.count[p]
                    ]


def on_device(start, guess, heat_mask, solid_mask):
    n = lax.axis_size("node")
    tiles = lax.axis_size("space")
    planes, depth, width = guess.shape[2:]
    assert width == 2 * LANES
    geo = Geometry(n, planes, depth)
    points_list, table_list = radau_tables(n)
    table = [[float(np.float32(v)) for v in row] for row in table_list]
    points = [float(np.float32(v)) for v in points_list]
    me = lax.axis_index("node").reshape(1).astype(jnp.int32)
    tile = lax.axis_index("space")
    up = [(i, i + 1) for i in range(tiles - 1)]
    down = [(i + 1, i) for i in range(tiles - 1)]
    params = pltpu.CompilerParams(vmem_limit_bytes=VMEM_LIMIT)
    vmem, smem, anywhere = (
        pl.BlockSpec(memory_space=pltpu.VMEM), pl.BlockSpec(memory_space=pltpu.SMEM), pl.BlockSpec(memory_space=pl.ANY)
    )
    f32 = jnp.float32

    packed = pl.pallas_call(
        functools.partial(pack_kernel, geo), name="pack",
        out_shape=jax.ShapeDtypeStruct((n, 4, 2, geo.rows, LANES), f32),
        in_specs=[vmem], out_specs=vmem, compiler_params=params,
    )(guess)
    aux = pl.pallas_call(
        functools.partial(pack_aux_kernel, geo), name="pack_aux",
        out_shape=jax.ShapeDtypeStruct((6, 2, geo.rows, LANES), f32),
        in_specs=[smem, vmem, vmem, vmem], out_specs=vmem, compiler_params=params,
    )(me, start, heat_mask, solid_mask)
    aux_lo = lax.ppermute(aux[:, :, geo.rows - geo.aux_side :], "space", up)
    aux_hi = lax.ppermute(aux[:, :, : geo.aux_side], "space", down)

    row = np.arange(geo.total) - geo.low
    inside = (row % geo.stride) < geo.window
    plane = row // geo.stride + tile * planes
    mask = jnp.where(inside & (plane >= 0) & (plane < planes * tiles), 1.0, 0.0).astype(f32)
    mask = jnp.broadcast_to(mask[:, None], (geo.total, LANES))
    coef = jnp.asarray(
        [points[m] * d / (1.0 + 6.0 * points[m] * d) for m in range(n) for d in diffusion], f32
    )

    own = lax.all_to_all(packed, "node", split_axis=0, concat_axis=0, tiled=True)
    for sweep in range(SWEEPS):
        last = sweep == SWEEPS - 1
        lo = lax.ppermute(own[:, :, :, geo.rows - geo.side :], "space", up)
        hi = lax.ppermute(own[:, :, :, : geo.side], "space", down)
        rows = planes * geo.back if last else geo.rows
        big = pltpu.VMEM((n, 4, 2, geo.total, LANES), f32)
        own = pl.pallas_call(
            functools.partial(sweep_kernel, geo, last, points, table), name="sweep",
            out_shape=jax.ShapeDtypeStruct((n, 4, 2, rows, LANES), f32),
            in_specs=[smem, smem, anywhere, anywhere, anywhere, anywhere, anywhere, anywhere, vmem], out_specs=vmem,
            scratch_shapes=[big, big, big, big, pltpu.VMEM((6, 2, geo.total, LANES), f32), pltpu.SemaphoreType.DMA((6,))],
            compiler_params=params,
        )(me, coef, own, lo, hi, aux, aux_lo, aux_hi, mask)
    back = lax.all_to_all(own, "node", split_axis=0, concat_axis=0, tiled=True)
    return pl.pallas_call(
        functools.partial(unpack_kernel, geo), name="unpack",
        out_shape=jax.ShapeDtypeStruct((1, 4, planes, depth, width), f32),
        in_specs=[vmem], out_specs=vmem, compiler_params=params,
    )(back)


def solution(mesh):
    in_specs = (
        P(None, "space", None, None),
        P("node", None, "space", None, None),
        P("space", None, None),
        P("space", None, None),
    )
    out_specs = P("node", None, "space", None, None)
    return jax.shard_map(
        on_device, mesh=mesh, in_specs=in_specs, out_specs=out_specs, check_vma=False
    )
```

time: 163 us -> 130 us (0.80)
  Pallas kernels: 0 us -> 34.9 us
  starting transfers between devices: 32.1 us -> 13.7 us
  other arithmetic: 17.5 us -> 0.01 us
  waiting for transfers between devices: 37.9 us -> 27.3 us
  local copies, waits for them, and re-layouts: 16.7 us -> 7.03 us
  blocking collectives: 52.9 us -> 46.2 us
  matrix products: 4.68 us -> 0 us
    pallas_call x0 -> x5, Pallas kernels: none -> 34.9 us  [the longest x2 27.7 us: on_device(): pl.pallas_call(functools.partial(sweep_kernel, geo, last, points, table),...]
    ppermute x12 -> x6, starting transfers between devices: 28.6 us -> 13.7 us  [the longest x2 4.81 us: on_device(): lo = lax.ppermute(own[:, :, :, geo.rows - geo.side:], 'space', up)]
    all_to_all x1 -> x0, waiting for transfers between devices: 12.7 us -> none  [on_device(): lax.all_to_all(mixed, 'node', split_axis=0, concat_axis=1, tiled=True)]
    all_to_all x3 -> x2, blocking collectives: 52.9 us -> 46.2 us  [the longest x1 25 us: on_device(): lax.all_to_all(packed, 'node', split_axis=0, concat_axis=0, tiled=True)]
    all_to_all x2 -> x0, other arithmetic: 6.08 us -> none  [on_device(): lax.all_to_all(mixed, 'node', split_axis=0, concat_axis=1, tiled=True)]
    div x5 -> x0, other arithmetic: 4.8 us -> none  [on_device(): current = (right + coupling * neighbour_sum(padded)) / denom_field]
    mul x5 -> x0, other arithmetic: 4.8 us -> none  [the longest x2 3.96 us: tendency(): total = (-advect_rate * transport + diffusive + source) * keeper]
    dot_general x2 -> x0, matrix products: 4.68 us -> none  [on_device(): jnp.einsum('os,snf->onf', table, lax.all_to_all(flat, 'node', split_axis=...]
  transfers between devices with their start and end apart: 13 -> 6, of which waited for: 12 -> 4; matrix products, arithmetic and copies ran while one was open for 2% -> 2% of each run, Pallas kernels for 0% -> 2%
where the time goes in v1:
time: 130 us; the launch traced here: 129 us
  blocking collectives  46.2 us (36%)
  Pallas kernels  34.9 us (27%)
  waiting for transfers between devices  27.3 us (21%)
  starting transfers between devices  13.7 us (11%)
  local copies, waits for them, and re-layouts  7.03 us (5%)
    pallas_call x2, Pallas kernels, on_device(): pl.pallas_call(functools.partial(sweep_kernel, geo, last, points, table),...  27.7 us
    all_to_all x1, blocking collectives, on_device(): lax.all_to_all(packed, 'node', split_axis=0, concat_axis=0, tiled=True)  25 us
    all_to_all x1, blocking collectives, on_device(): back = lax.all_to_all(own, 'node', split_axis=0, concat_axis=0, tiled=True)  21.2 us
    ppermute x2, waiting for transfers between devices, on_device(): hi = lax.ppermute(own[:, :, :, :geo.side], 'space', down)  12.7 us
    ppermute x1, waiting for transfers between devices, on_device(): aux_hi = lax.ppermute(aux[:, :, :geo.aux_side], 'space', down)  7.09 us
    ppermute x2, starting transfers between devices, on_device(): lo = lax.ppermute(own[:, :, :, geo.rows - geo.side:], 'space', up)  4.81 us
    ppermute x2, starting transfers between devices, on_device(): hi = lax.ppermute(own[:, :, :, :geo.side], 'space', down)  3.83 us
    ppermute x2, waiting for transfers between devices, on_device(): lo = lax.ppermute(own[:, :, :, geo.rows - geo.side:], 'space', up)  3.82 us
  transfers between devices with their start and end apart: 6, of which 4 were waited for; matrix products, arithmetic and copies ran while one was open for 2% of the time, Pallas kernels for 2%

profile of v1, /device:TPU:8, one launch (start us, length us, event | category | flops | bytes accessed | tf_op | source)
XLA Modules:
  0.0 129.3 jit_solution(11334685915122179462)
XLA Ops:
  0.0 2.6 %pack.1 = f32[4,4,2,104,128]{4,3,2,1,0:T(8,128)} custom-call(f32[1,4,4,64,256]{4,3,2,1,0:T(8,128)} %guess_ref.1), custom_call_target="tpu_custom_call" | custom-call | tf_op jit(solution)/shard_map/pack/pallas_call | solution.py:301
  2.6 25.0 %all_to_all.10.own_ref = f32[4,4,2,104,128]{4,3,2,1,0:T(8,128)S(1)} all-to-all(f32[4,4,2,104,128]{4,3,2,1,0:T(8,128)} %pack.1), channel_id=1, replica_groups=mesh['node'=4,'space'=8] {'node'}, dimensions={0} | all-to-all | bytes 3407872 | tf_op jit(solution)/shard_map/all_to_all | solution.py:323
  27.6 0.2 fusion.4
  27.8 1.0 copy-done
  28.8 1.9 %collective-permute-start.1 = (f32[4,4,2,80,128]{4,3,2,1,0:T(8,128)S(1)}, f32[4,4,2,80,128]{4,3,2,1,0:T(8,128)}, u32[]{:S(2)}, u32[]{:S(2)}) collective-permute-start(f32[4,4,2,80,128]{4,3,2,1,0:T(8,128)S(1)} %get-tuple-element.7), channel_id=1, source_target_pairs={{1,0},{2,1},{3,2},{4,3},{5,4},{6,5},{7,6},{9,8},{10,9},{11,10},{12... | collective-permute-start | bytes 3932168 | tf_op jit(solution)/shard_map/ppermute | solution.py:327
  30.7 2.4 %collective-permute-start = (f32[4,4,2,80,128]{4,3,2,1,0:T(8,128)S(1)}, f32[4,4,2,80,128]{4,3,2,1,0:T(8,128)}, u32[]{:S(2)}, u32[]{:S(2)}) collective-permute-start(f32[4,4,2,80,128]{4,3,2,1,0:T(8,128)S(1)} %get-tuple-element.8), channel_id=1, source_target_pairs={{0,1},{1,2},{2,3},{3,4},{4,5},{5,6},{6,7},{8,9},{9,10},{10,11},{11... | collective-permute-start | bytes 3932168 | tf_op jit(solution)/shard_map/ppermute | solution.py:326
  33.1 0.0 copy-start.6
  33.1 2.3 %pack_aux.1.aux_ref = f32[6,2,104,128]{3,2,1,0:T(8,128)} custom-call(s32[1]{0:T(128)} %bitcast.me_ref, f32[4,4,64,256]{3,2,1,0:T(8,128)} %start_ref.1, s32[4,64,256]{2,1,0:T(8,128)} %heat_ref.1, s32[4,64,256]{2,1,0:T(8,128)} %solid_ref.1), custom_call_target="tpu_custom_call" | custom-call | tf_op jit(solution)/shard_map/pack_aux/pallas_call | solution.py:306
  35.4 2.0 %fusion.5 = (f32[6,2,56,128]{3,2,1,0:T(8,128)}, f32[6,2,56,128]{3,2,1,0:T(8,128)}) fusion(f32[6,2,104,128]{3,2,1,0:T(8,128)} %pack_aux.1.aux_ref), kind=kLoop, calls=%fused_computation.7 | loop fusion | bytes 1376256 | tf_op jit(solution)/shard_map/slice | solution.py:312
  37.4 3.1 %collective-permute-start.3 = (f32[6,2,56,128]{3,2,1,0:T(8,128)}, f32[6,2,56,128]{3,2,1,0:T(8,128)S(1)}, u32[]{:S(2)}, u32[]{:S(2)}) collective-permute-start(f32[6,2,56,128]{3,2,1,0:T(8,128)} %get-tuple-element.9), channel_id=1, source_target_pairs={{1,0},{2,1},{3,2},{4,3},{5,4},{6,5},{7,6},{9,8},{10,9},{11,10},{12... | collective-permute-start | bytes 1032200 | tf_op jit(solution)/shard_map/ppermute | solution.py:312
  40.5 1.9 %collective-permute-start.2 = (f32[6,2,56,128]{3,2,1,0:T(8,128)}, f32[6,2,56,128]{3,2,1,0:T(8,128)S(1)}, u32[]{:S(2)}, u32[]{:S(2)}) collective-permute-start(f32[6,2,56,128]{3,2,1,0:T(8,128)} %get-tuple-element.10), channel_id=1, source_target_pairs={{0,1},{1,2},{2,3},{3,4},{4,5},{5,6},{6,7},{8,9},{9,10},{10,11},{11... | collective-permute-start | bytes 1032200 | tf_op jit(solution)/shard_map/ppermute | solution.py:311
  42.5 7.1 %collective-permute-done.3.auxhi_ref = f32[6,2,56,128]{3,2,1,0:T(8,128)S(1)} collective-permute-done((f32[6,2,56,128]{3,2,1,0:T(8,128)}, f32[6,2,56,128]{3,2,1,0:T(8,128)S(1)}, u32[]{:S(2)}, u32[]{:S(2)}) %collective-permute-start.3) | collective-permute-done | bytes 344096 | tf_op jit(solution)/shard_map/ppermute | solution.py:312
  49.6 3.7 %collective-permute-done.2.auxlo_ref = f32[6,2,56,128]{3,2,1,0:T(8,128)S(1)} collective-permute-done((f32[6,2,56,128]{3,2,1,0:T(8,128)}, f32[6,2,56,128]{3,2,1,0:T(8,128)S(1)}, u32[]{:S(2)}, u32[]{:S(2)}) %collective-permute-start.2) | collective-permute-done | bytes 344096 | tf_op jit(solution)/shard_map/ppermute | solution.py:311
  53.3 0.8 broadcast_in_dim.16.mask_ref
  54.1 13.8 %sweep.2.own_ref = f32[4,4,2,104,128]{4,3,2,1,0:T(8,128)} custom-call(s32[1]{0:T(128)} %bitcast.me_ref, f32[16]{0:T(128)} %constant.26.clone.coef_ref, f32[4,4,2,104,128]{4,3,2,1,0:T(8,128)} %copy-done, f32[4,4,2,80,128]{4,3,2,1,0:T(8,128)} %collective-permute-done.lo_ref, f32[4,4,2,80,128]{4,3,2,1,0:T(8,128)} %collective-permute-done.1.hi_ref, ...), custom_call_target="tpu_custom_call" | custom-call | tf_op jit(solution)/shard_map/sweep/pallas_call | solution.py:330
  67.9 2.0 %fusion.3 = (f32[4,4,2,80,128]{4,3,2,1,0:T(8,128)S(1)}, f32[4,4,2,80,128]{4,3,2,1,0:T(8,128)S(1)}) fusion(f32[4,4,2,104,128]{4,3,2,1,0:T(8,128)} %sweep.2.own_ref), kind=kLoop, calls=%fused_computation.5 | loop fusion | bytes 5242880 | tf_op jit(solution)/shard_map/slice | solution.py:327
  69.9 1.9 %collective-permute-start.5 = (f32[4,4,2,80,128]{4,3,2,1,0:T(8,128)S(1)}, f32[4,4,2,80,128]{4,3,2,1,0:T(8,128)S(1)}, u32[]{:S(2)}, u32[]{:S(2)}) collective-permute-start(f32[4,4,2,80,128]{4,3,2,1,0:T(8,128)S(1)} %get-tuple-element.5), channel_id=1, source_target_pairs={{1,0},{2,1},{3,2},{4,3},{5,4},{6,5},{7,6},{9,8},{10,9},{11,10},{12... | collective-permute-start | bytes 3932168 | tf_op jit(solution)/shard_map/ppermute | solution.py:327
  71.8 2.4 %collective-permute-start.4 = (f32[4,4,2,80,128]{4,3,2,1,0:T(8,128)S(1)}, f32[4,4,2,80,128]{4,3,2,1,0:T(8,128)S(1)}, u32[]{:S(2)}, u32[]{:S(2)}) collective-permute-start(f32[4,4,2,80,128]{4,3,2,1,0:T(8,128)S(1)} %get-tuple-element.6), channel_id=1, source_target_pairs={{0,1},{1,2},{2,3},{3,4},{4,5},{5,6},{6,7},{8,9},{9,10},{10,11},{11... | collective-permute-start | bytes 3932168 | tf_op jit(solution)/shard_map/ppermute | solution.py:326
  74.2 12.7 %collective-permute-done.5.hi_ref = f32[4,4,2,80,128]{4,3,2,1,0:T(8,128)S(1)} collective-permute-done((f32[4,4,2,80,128]{4,3,2,1,0:T(8,128)S(1)}, f32[4,4,2,80,128]{4,3,2,1,0:T(8,128)S(1)}, u32[]{:S(2)}, u32[]{:S(2)}) %collective-permute-start.5) | collective-permute-done | bytes 1310752 | tf_op jit(solution)/shard_map/ppermute | solution.py:327
  86.9 3.8 %collective-permute-done.4.lo_ref = f32[4,4,2,80,128]{4,3,2,1,0:T(8,128)S(1)} collective-permute-done((f32[4,4,2,80,128]{4,3,2,1,0:T(8,128)S(1)}, f32[4,4,2,80,128]{4,3,2,1,0:T(8,128)S(1)}, u32[]{:S(2)}, u32[]{:S(2)}) %collective-permute-start.4) | collective-permute-done | bytes 1310752 | tf_op jit(solution)/shard_map/ppermute | solution.py:326
  90.7 1.1 copy-done.4
  91.8 13.9 %sweep.3 = f32[4,4,2,80,128]{4,3,2,1,0:T(8,128)} custom-call(s32[1]{0:T(128)} %bitcast.me_ref, f32[16]{0:T(128)} %constant.26.clone.coef_ref, f32[4,4,2,104,128]{4,3,2,1,0:T(8,128)} %sweep.2.own_ref, f32[4,4,2,80,128]{4,3,2,1,0:T(8,128)} %copy-done.4, f32[4,4,2,80,128]{4,3,2,1,0:T(8,128)} %copy-done.3, f32[6,2,104,128]{3,2,1,0:T(8,128)} %pack_aux.1.aux_ref, ...), custom_call_target="tpu_custom_call" | custom-call | tf_op jit(solution)/shard_map/sweep/pallas_call | solution.py:330
  105.7 21.2 %all_to_all.11.in_ref = f32[4,4,2,80,128]{4,3,2,1,0:T(8,128)} all-to-all(f32[4,4,2,80,128]{4,3,2,1,0:T(8,128)} %sweep.3), channel_id=1, replica_groups=mesh['node'=4,'space'=8] {'node'}, dimensions={0} | all-to-all | bytes 2621440 | tf_op jit(solution)/shard_map/all_to_all | solution.py:337
  126.9 2.4 %unpack.1 = f32[1,4,4,64,256]{4,3,2,1,0:T(8,128)} custom-call(f32[4,4,2,80,128]{4,3,2,1,0:T(8,128)} %all_to_all.11.in_ref), custom_call_target="tpu_custom_call" | custom-call | tf_op jit(solution)/shard_map/unpack/pallas_call | solution.py:338
  (14 shorter events, 0.0 us)
Async XLA Ops:
  27.6 1.2 copy-start
  28.8 24.5 %collective-permute-start.1 = (f32[4,4,2,80,128]{4,3,2,1,0:T(8,128)S(1)}, f32[4,4,2,80,128]{4,3,2,1,0:T(8,128)}, u32[]{:S(2)}, u32[]{:S(2)}) collective-permute-start(f32[4,4,2,80,128]{4,3,2,1,0:T(8,128)S(1)} %get-tuple-element.7), channel_id=1, source_target_pairs={{1,0},{2,1},{3,2},{4,3},{5,4},{6,5},{7,6},{9,8},{10,9},{11,10},{12... | collective-permute-start | bytes 3932168 | tf_op jit(solution)/shard_map/ppermute | solution.py:327
  30.7 22.6 %collective-permute-start = (f32[4,4,2,80,128]{4,3,2,1,0:T(8,128)S(1)}, f32[4,4,2,80,128]{4,3,2,1,0:T(8,128)}, u32[]{:S(2)}, u32[]{:S(2)}) collective-permute-start(f32[4,4,2,80,128]{4,3,2,1,0:T(8,128)S(1)} %get-tuple-element.8), channel_id=1, source_target_pairs={{0,1},{1,2},{2,3},{3,4},{4,5},{5,6},{6,7},{8,9},{9,10},{10,11},{11... | collective-permute-start | bytes 3932168 | tf_op jit(solution)/shard_map/ppermute | solution.py:326
  33.1 9.4 %copy-start.5 = (s32[280]{0:T(512)S(1)}, s32[280]{0:T(512)}, u32[]{:S(2)}) copy-start(s32[280]{0:T(512)} %constant.24.clone) | copy-start | bytes 3364
  33.1 9.4 %copy-start.6 = (pred[280]{0:T(512)(128)(4,1)S(1)}, pred[280]{0:T(512)(128)(4,1)}, u32[]{:S(2)}) copy-start(pred[280]{0:T(512)(128)(4,1)} %constant.25.clone) | copy-start | bytes 844
  37.4 12.2 %collective-permute-start.3 = (f32[6,2,56,128]{3,2,1,0:T(8,128)}, f32[6,2,56,128]{3,2,1,0:T(8,128)S(1)}, u32[]{:S(2)}, u32[]{:S(2)}) collective-permute-start(f32[6,2,56,128]{3,2,1,0:T(8,128)} %get-tuple-element.9), channel_id=1, source_target_pairs={{1,0},{2,1},{3,2},{4,3},{5,4},{6,5},{7,6},{9,8},{10,9},{11,10},{12... | collective-permute-start | bytes 1032200 | tf_op jit(solution)/shard_map/ppermute | solution.py:312
  40.5 12.8 %collective-permute-start.2 = (f32[6,2,56,128]{3,2,1,0:T(8,128)}, f32[6,2,56,128]{3,2,1,0:T(8,128)S(1)}, u32[]{:S(2)}, u32[]{:S(2)}) collective-permute-start(f32[6,2,56,128]{3,2,1,0:T(8,128)} %get-tuple-element.10), channel_id=1, source_target_pairs={{0,1},{1,2},{2,3},{3,4},{4,5},{5,6},{6,7},{8,9},{9,10},{10,11},{11... | collective-permute-start | bytes 1032200 | tf_op jit(solution)/shard_map/ppermute | solution.py:311
  49.6 4.5 %copy-start.1 = (f32[6,2,56,128]{3,2,1,0:T(8,128)}, f32[6,2,56,128]{3,2,1,0:T(8,128)S(1)}, u32[]{:S(2)}) copy-start(f32[6,2,56,128]{3,2,1,0:T(8,128)S(1)} %collective-permute-done.3.auxhi_ref) | copy-start | bytes 1032196
  53.3 0.8 copy-start.2
  69.9 17.0 %collective-permute-start.5 = (f32[4,4,2,80,128]{4,3,2,1,0:T(8,128)S(1)}, f32[4,4,2,80,128]{4,3,2,1,0:T(8,128)S(1)}, u32[]{:S(2)}, u32[]{:S(2)}) collective-permute-start(f32[4,4,2,80,128]{4,3,2,1,0:T(8,128)S(1)} %get-tuple-element.5), channel_id=1, source_target_pairs={{1,0},{2,1},{3,2},{4,3},{5,4},{6,5},{7,6},{9,8},{10,9},{11,10},{12... | collective-permute-start | bytes 3932168 | tf_op jit(solution)/shard_map/ppermute | solution.py:327
  71.8 18.9 %collective-permute-start.4 = (f32[4,4,2,80,128]{4,3,2,1,0:T(8,128)S(1)}, f32[4,4,2,80,128]{4,3,2,1,0:T(8,128)S(1)}, u32[]{:S(2)}, u32[]{:S(2)}) collective-permute-start(f32[4,4,2,80,128]{4,3,2,1,0:T(8,128)S(1)} %get-tuple-element.6), channel_id=1, source_target_pairs={{0,1},{1,2},{2,3},{3,4},{4,5},{5,6},{6,7},{8,9},{9,10},{10,11},{11... | collective-permute-start | bytes 3932168 | tf_op jit(solution)/shard_map/ppermute | solution.py:326
  86.9 3.8 %copy-start.3 = (f32[4,4,2,80,128]{4,3,2,1,0:T(8,128)}, f32[4,4,2,80,128]{4,3,2,1,0:T(8,128)S(1)}, u32[]{:S(2)}) copy-start(f32[4,4,2,80,128]{4,3,2,1,0:T(8,128)S(1)} %collective-permute-done.5.hi_ref) | copy-start | bytes 3932164
  90.7 1.1 copy-start.4

commit v2 on v1

v2 whole, which is shorter than its diff:
```python
import functools

import jax
import jax.numpy as jnp
import numpy as np
from jax import lax
from jax.experimental import pallas as pl
from jax.experimental.pallas import tpu as pltpu
from jax.sharding import PartitionSpec as P

SWEEPS = 2
JACOBI = 3
LANES = 128
VMEM_LIMIT = 56 << 20

advect_rate = 0.25
buoyancy = 0.5
heating = 1.0
diffusion = (0.5, 0.5, 0.5, 0.35)


def legendre_value(order, place):
    previous = 1.0
    current = place
    for degree in range(1, order):
        following = ((2 * degree + 1) * place * current - degree * previous) / (degree + 1)
        previous = current
        current = following
    return current


def radau_tables(count):

    def radau_poly(place):
        return legendre_value(count, place) - legendre_value(count - 1, place)

    samples = 4000 * count
    roots_found = []
    left_end = -1.0
    left_value = radau_poly(left_end)
    for index in range(1, samples + 1):
        right_end = -1.0 + (2.0 - 1e-07) * index / samples
        right_value = radau_poly(right_end)
        if left_value * right_value < 0.0:
            low_end = left_end
            high_end = right_end
            low_value = left_value
            for repeat in range(200):
                middle = 0.5 * (low_end + high_end)
                middle_value = radau_poly(middle)
                if low_value * middle_value <= 0.0:
                    high_end = middle
                else:
                    low_end = middle
                    low_value = middle_value
            roots_found.append(0.5 * (low_end + high_end))
        left_end = right_end
        left_value = right_value
    points = [(value + 1.0) / 2.0 for value in roots_found[: count - 1]] + [1.0]
    table = []
    for row in range(count):
        table.append([0.0] * count)
    for column in range(count):
        coefficients = [1.0]
        for other in range(count):
            if other == column:
                continue
            scale = 1.0 / (points[column] - points[other])
            widened = [0.0] * (len(coefficients) + 1)
            for index in range(len(coefficients)):
                widened[index + 1] += coefficients[index] * scale
                widened[index] -= points[other] * coefficients[index] * scale
            coefficients = widened
        for row in range(count):
            total = 0.0
            for index in range(len(coefficients)):
                total += coefficients[index] * points[row] ** (index + 1) / (index + 1)
            table[row][column] = total
    return (points, table)


def round_up(value, step):
    return -(-value // step) * step


class Geometry:
    def __init__(self, nodes, planes, depth):
        overlap = SWEEPS * JACOBI if nodes > 1 else 0
        self.nodes, self.planes, self.depth = nodes, planes, depth
        self.window = -(-(depth + 2 * overlap * (nodes - 1)) // nodes)
        step = self.window - 2 * overlap
        assert step > 0 and planes >= JACOBI
        self.offset = [min(p * step, depth - self.window) for p in range(nodes)]
        first = [0] + [p * step + overlap for p in range(1, nodes)]
        last = first[1:] + [depth]
        self.first, self.count = first, [b - a for a, b in zip(first, last)]
        self.stride = self.window + 1
        while (planes * self.stride) % 8:
            self.stride += 1
        self.rows = planes * self.stride
        self.side = round_up(JACOBI * self.stride, 8)
        self.low = 8 + self.side
        self.total = self.low + self.rows + self.side + 8
        self.back = max(self.count)
        while (planes * self.back) % 8:
            self.back += 1

    def span(self, reach):
        begin = (self.low - reach * self.stride) // 8 * 8
        end = round_up(self.low + (self.planes + reach) * self.stride, 8)
        assert begin - self.stride >= 0 and end + self.stride <= self.total
        return begin, end


def copy_all(pairs, sems):
    copies = [pltpu.make_async_copy(source, target, sems.at[i]) for i, (source, target) in enumerate(pairs)]
    for copy in copies:
        copy.start()
    for copy in copies:
        copy.wait()


def pack_kernel(geo, guess_ref, *refs):
    *outs, windows, sems = refs
    me = lax.axis_index("node")
    blank = jnp.zeros((geo.stride - geo.window, LANES), jnp.float32)
    for p in range(geo.nodes):
        for f in range(4):
            for x in range(geo.planes):
                for h in range(2):
                    at = x * geo.stride
                    windows[p, f, h, at : at + geo.window] = guess_ref[
                        0, f, x, geo.offset[p] : geo.offset[p] + geo.window, h * LANES : (h + 1) * LANES
                    ]
                    windows[p, f, h, at + geo.window : at + geo.stride] = blank
    copy_all([(windows.at[me ^ k], outs[k - 1]) for k in range(1, geo.nodes)], sems)


def send_rows(geo, odd):
    far = geo.rows - geo.side
    return pl.multiple_of(far * (1 - odd), 8), pl.multiple_of(far * odd, 8)


def halo_rows(geo, odd):
    below, above = geo.low - geo.side, geo.low + geo.rows
    return (
        pl.multiple_of(above + (below - above) * odd, 8),
        pl.multiple_of(below + (above - below) * odd, 8),
    )


def pack_own_kernel(
    geo, guess_ref, start_ref, heat_ref, solid_ref, own_ref, aux_ref, near_ref, far_ref, packed, sems
):
    me, odd = lax.axis_index("node"), lax.axis_index("space") % 2
    blank = jnp.zeros((geo.stride - geo.window, LANES), jnp.float32)
    for p in range(geo.nodes):

        @pl.when(me == p)
        def _():
            rows = slice(geo.offset[p], geo.offset[p] + geo.window)
            for x in range(geo.planes):
                for h in range(2):
                    at = x * geo.stride
                    lanes = slice(h * LANES, (h + 1) * LANES)
                    for f in range(4):
                        packed[f, h, at : at + geo.window] = guess_ref[0, f, x, rows, lanes]
                        packed[4 + f, h, at : at + geo.window] = start_ref[f, x, rows, lanes]
                    packed[8, h, at : at + geo.window] = heating * heat_ref[x, rows, lanes].astype(jnp.float32)
                    packed[9, h, at : at + geo.window] = 1.0 - solid_ref[x, rows, lanes].astype(jnp.float32)
                    for f in range(10):
                        packed[f, h, at + geo.window : at + geo.stride] = blank

    near, far = send_rows(geo, odd)
    copy_all(
        [
            (packed.at[:, :, pl.ds(far, geo.side)], far_ref),
            (packed.at[:, :, pl.ds(near, geo.side)], near_ref),
            (packed.at[pl.ds(0, 4)], own_ref),
            (packed.at[pl.ds(4, 6)], aux_ref),
        ],
        sems,
    )


def pick(index, values):
    chosen = jnp.float32(values[-1])
    for i in reversed(range(len(values) - 1)):
        chosen = jnp.where(index == i, jnp.float32(values[i]), chosen)
    return chosen


def sweep_kernel(geo, opening, tiles, points, table, aux_ref, near0_ref, far0_ref, *refs):
    n, stride, low, side = geo.nodes, geo.stride, geo.low, geo.side
    me, tile = lax.axis_index("node"), lax.axis_index("space")
    odd = tile % 2
    *refs, field, tend, first, base, aux, mask, sems = refs
    near, far = halo_rows(geo, odd)
    near_from, far_from = send_rows(geo, 1 - odd)
    own_rows, near_rows, far_rows = pl.ds(low, geo.rows), pl.ds(near, side), pl.ds(far, side)
    pairs = [
        (aux_ref, aux.at[:, :, own_rows]),
        (near0_ref.at[pl.ds(4, 6)], aux.at[:, :, near_rows]),
        (far0_ref.at[pl.ds(4, 6)], aux.at[:, :, far_rows]),
    ]
    for k in range(n):
        j = me ^ k if opening else k
        if opening and k == 0:
            sources = refs[0], near0_ref.at[pl.ds(0, 4)], far0_ref.at[pl.ds(0, 4)]
        elif opening:
            own_ref, near_ref, far_ref = refs[3 * k - 2 : 3 * k + 1]
            sources = own_ref, near_ref.at[:, :, pl.ds(near_from, side)], far_ref.at[:, :, pl.ds(far_from, side)]
        else:
            sources = [ref.at[k] for ref in refs[:3]]
        pairs += zip(sources, [field.at[j, :, :, rows] for rows in (own_rows, near_rows, far_rows)])
    copies = [pltpu.make_async_copy(source, target, sems.at[i]) for i, (source, target) in enumerate(pairs)]
    for copy in copies:
        copy.start()
    refs = refs[3 * n - 2 :] if opening else refs[3:]

    mask[...] = jnp.zeros(mask.shape, jnp.float32)
    for q in range(-JACOBI, geo.planes + JACOBI):
        there = jnp.float32(1.0)
        if q < 0:
            there = jnp.where(tile > 0, 1.0, 0.0)
        if q >= geo.planes:
            there = jnp.where(tile < tiles - 1, 1.0, 0.0)
        mask[low + q * stride : low + q * stride + geo.window] = jnp.full((geo.window, LANES), there, jnp.float32)
    lane = lax.broadcasted_iota(jnp.int32, (8, LANES), 1)
    is_first, is_last = lane == 0, lane == LANES - 1
    for copy in copies[:3]:
        copy.wait()

    def sides(a, b):
        ra, rb = pltpu.roll(a, 1, 1), pltpu.roll(b, 1, 1)
        la, lb = pltpu.roll(a, LANES - 1, 1), pltpu.roll(b, LANES - 1, 1)
        minus = (jnp.where(is_first, 0.0, ra), jnp.where(is_first, ra, rb))
        plus = (jnp.where(is_last, lb, la), jnp.where(is_last, 0.0, lb))
        return minus, plus

    begin, end = geo.span(JACOBI - 1)

    def node_tendency(k, _):
        j = me ^ k if opening else k
        for i, rows in enumerate((own_rows, near_rows, far_rows)):
            part = field.at[j, :, :, rows]
            pltpu.make_async_copy(part, part, sems.at[3 + 3 * k + i]).wait()
        for r in range(begin, end, 8):
            rows = pl.ds(r, 8)
            vel = []
            for h in range(2):
                vel.append([(-0.5 * advect_rate) * field[j, f, h, rows] for f in range(3)])
            for f in range(4):
                centre = [field[j, f, h, rows] for h in range(2)]
                minus, plus = sides(centre[0], centre[1])
                for h in range(2):
                    xp, xm = field[j, f, h, pl.ds(r + stride, 8)], field[j, f, h, pl.ds(r - stride, 8)]
                    zp, zm = field[j, f, h, pl.ds(r + 1, 8)], field[j, f, h, pl.ds(r - 1, 8)]
                    near = (xp + xm) + (zp + zm) + (plus[h] + minus[h])
                    moved = vel[h][0] * (xp - xm) + vel[h][1] * (plus[h] - minus[h]) + vel[h][2] * (zp - zm)
                    total = moved + diffusion[f] * (near - 6.0 * centre[h])
                    if f == 2:
                        total = total + buoyancy * field[j, 3, h, rows]
                    if f == 3:
                        total = total + aux[4, h, rows]
                    else:
                        total = total * aux[5, h, rows]
                    tend[j, f, h, rows] = total
                    base[j, f, h, rows] = near
        return 0

    lax.fori_loop(0, n, node_tendency, 0)

    def quadrature(t, _):
        rows = pl.ds(pl.multiple_of(begin + t * 8, 8), 8)
        inside = mask[rows]
        for f in range(4):
            scale = [inside * (1.0 / (1.0 + 6.0 * points[m] * diffusion[f])) for m in range(n)]
            for h in range(2):
                slopes = [tend[j, f, h, rows] for j in range(n)]
                begun = aux[f, h, rows]
                for m in range(n):
                    c = points[m] * diffusion[f]
                    total = begun + (6.0 * c) * field[m, f, h, rows]
                    for j in range(n):
                        total = total + table[m][j] * slopes[j]
                    total = total * scale[m]
                    first[m, f, h, rows] = total
                    base[m, f, h, rows] = total - (c * scale[m]) * base[m, f, h, rows]
        return 0

    lax.fori_loop(0, (end - begin) // 8, quadrature, 0)

    def weights(m):
        return [pick(m, [p * d / (1.0 + 6.0 * p * d) for p in points]) for d in diffusion]

    def relax_rows(source, target, m, f, r, weight, to):
        minus, plus = sides(source[m, f, 0, pl.ds(r, 8)], source[m, f, 1, pl.ds(r, 8)])
        for h in range(2):
            near = (
                (source[m, f, h, pl.ds(r + stride, 8)] + source[m, f, h, pl.ds(r - stride, 8)])
                + (source[m, f, h, pl.ds(r + 1, 8)] + source[m, f, h, pl.ds(r - 1, 8)])
                + (plus[h] + minus[h])
            )
            target[m, f, h, pl.ds(to, 8)] = base[m, f, h, pl.ds(r, 8)] + weight * near

    def relax(source, target, m, reach):
        weight = weights(m)
        for r in range(*geo.span(reach), 8):
            inside = mask[pl.ds(r, 8)]
            for f in range(4):
                relax_rows(source, target, m, f, r, inside * weight[f], r)

    def relax_second(m, _):
        relax(first, tend, m, 1)
        return 0

    lax.fori_loop(0, n, relax_second, 0)

    if opening:
        out_ref, near_ref, far_ref = refs
        near, far = send_rows(geo, odd)

        def results(m, start):
            for i, (row, count, ref) in enumerate(((far, side, far_ref), (near, side, near_ref), (0, geo.rows, out_ref))):
                part = first.at[m, :, :, pl.ds(pl.multiple_of(low + row, 8), count)]
                copy = pltpu.make_async_copy(part, ref.at[m], sems.at[3 + 3 * m + i])
                copy.start() if start else copy.wait()

        def relax_third(m, _):
            relax(tend, first, m, 0)
            results(m, True)
            return 0

        lax.fori_loop(0, n, relax_third, 0)
        for m in range(n):
            results(m, False)
        return

    done = pl.ds(0, geo.planes * geo.back)
    for start in sorted({a - b for a, b in zip(geo.first, geo.offset)}):
        hit = [p for p in range(n) if geo.first[p] - geo.offset[p] == start]
        chosen = functools.reduce(jnp.logical_or, [me == p for p in hit])

        @pl.when(chosen)
        def _():
            def relax_third(i, _):
                k = n - 1 - i
                m = me ^ k
                weight = weights(m)
                for x in range(geo.planes):
                    for o in [*range(0, geo.back - 8, 8), geo.back - 8]:
                        for f in range(4):
                            relax_rows(tend, first, m, f, low + x * stride + start + o, weight[f], x * geo.back + o)
                for other in range(n):

                    @pl.when(k == other)
                    def _():
                        pltpu.make_async_copy(first.at[m, :, :, done], refs[other], sems.at[other]).start()

                return 0

            lax.fori_loop(0, n, relax_third, 0)

    for k in range(n):
        pltpu.make_async_copy(first.at[me ^ k, :, :, done], refs[k], sems.at[k]).wait()


def unpack_kernel(geo, *refs):
    ins, (out_ref, pieces, sems) = refs[: geo.nodes], refs[geo.nodes :]
    me = lax.axis_index("node")
    copy_all([(ins[k], pieces.at[me ^ k]) for k in range(geo.nodes)], sems)
    for p in range(geo.nodes):
        for f in range(4):
            for x in range(geo.planes):
                for h in range(2):
                    at = x * geo.back
                    out_ref[0, f, x, geo.first[p] : geo.first[p] + geo.count[p], h * LANES : (h + 1) * LANES] = pieces[
                        p, f, h, at : at + geo.count[p]
                    ]


def on_device(start, guess, heat_mask, solid_mask):
    n = lax.axis_size("node")
    tiles = lax.axis_size("space")
    planes, depth, width = guess.shape[2:]
    assert width == 2 * LANES and tiles % 2 == 0 and n & (n - 1) == 0
    geo = Geometry(n, planes, depth)
    points_list, table_list = radau_tables(n)
    table = [[float(np.float32(v)) for v in row] for row in table_list]
    points = [float(np.float32(v)) for v in points_list]
    f32 = jnp.float32
    vmem, hbm = pl.BlockSpec(memory_space=pltpu.VMEM), pl.BlockSpec(memory_space=pltpu.HBM)

    def call(kernel, name, outs, ins, spec, out_spec, scratch, copies):
        return pl.pallas_call(
            kernel, name=name,
            out_shape=[jax.ShapeDtypeStruct(shape, f32) for shape in outs],
            in_specs=[spec] * len(ins), out_specs=[out_spec] * len(outs),
            scratch_shapes=[pltpu.VMEM(shape, f32) for shape in scratch] + [pltpu.SemaphoreType.DMA((copies,))],
            compiler_params=pltpu.CompilerParams(vmem_limit_bytes=VMEM_LIMIT),
        )(*ins)

    def across(k, value):
        return lax.ppermute(value, "node", [(i, i ^ k) for i in range(n)])

    chip = [(i, i ^ 1) for i in range(tiles)]
    links = [(i, i + 1) for i in range(1, tiles - 1, 2)] + [(i + 1, i) for i in range(1, tiles - 1, 2)]

    def beside(near, far):
        return lax.ppermute(near, "space", chip), lax.ppermute(far, "space", links)

    piece = (4, 2, geo.rows, LANES)
    sends = call(
        functools.partial(pack_kernel, geo), "pack", [piece] * (n - 1), (guess,), vmem, hbm, [(n,) + piece], n - 1
    )
    edge = (10, 2, geo.side, LANES)
    own, aux, near, far = call(
        functools.partial(pack_own_kernel, geo), "pack_own", [piece, (6,) + piece[1:], edge, edge],
        (guess, start, heat_mask, solid_mask), vmem, hbm, [(10,) + piece[1:]], 4,
    )
    near0, far0 = beside(near, far)

    owns = {0: own}
    wave = []
    for hops in range(1, n.bit_length()):
        group = [k for k in range(1, n) if k.bit_count() == hops]
        gated = lax.optimization_barrier([sends[k - 1] for k in group] + wave)
        wave = [across(k, value) for k, value in zip(group, gated)]
        owns.update(zip(group, wave))
    pieces = [own]
    for k in range(1, n):
        pieces += [owns[k], *beside(owns[k], owns[k])]

    big = (n, 4, 2, geo.total, LANES)
    scratch = [big, big, big, big, (6, 2, geo.total, LANES), (geo.total, LANES)]
    edge = (n, 4, 2, geo.side, LANES)
    own, near, far = call(
        functools.partial(sweep_kernel, geo, True, tiles, points, table), "sweep_opening", [(n,) + piece, edge, edge],
        (aux, near0, far0, *pieces), hbm, hbm, scratch, 3 + 3 * n,
    )
    near, far = beside(near, far)
    outs = call(
        functools.partial(sweep_kernel, geo, False, tiles, points, table), "sweep_closing",
        [(4, 2, planes * geo.back, LANES)] * n, (aux, near0, far0, own, near, far), hbm, hbm, scratch, 3 + 3 * n,
    )
    outs = [across(k, outs[k]) if k else outs[k] for k in range(n)]
    (result,) = call(
        functools.partial(unpack_kernel, geo), "unpack", [(1, 4, planes, depth, width)], outs, hbm, vmem,
        [(n, 4, 2, planes * geo.back, LANES)], n,
    )
    return result


def solution(mesh):
    in_specs = (
        P(None, "space", None, None),
        P("node", None, "space", None, None),
        P("space", None, None),
        P("space", None, None),
    )
    out_specs = P("node", None, "space", None, None)
    return jax.shard_map(
        on_device, mesh=mesh, in_specs=in_specs, out_specs=out_specs, check_vma=False
    )
```

time: 130 us -> 99.3 us (0.76)
  blocking collectives: 46.2 us -> 0 us
  waiting for transfers between devices: 27.3 us -> 43.9 us
  starting transfers between devices: 13.7 us -> 24 us
  Pallas kernels: 34.9 us -> 28.2 us
  local copies, waits for them, and re-layouts: 7.03 us -> 2.68 us
    all_to_all x2 -> x0, blocking collectives: 46.2 us -> none  [the longest x1 25 us: on_device(): lax.all_to_all(packed, 'node', split_axis=0, concat_axis=0, tiled=True)]
    ppermute x6 -> x16, waiting for transfers between devices: 27.3 us -> 43.9 us  [the longest x5 22.4 us: beside(): lax.ppermute(far, 'space', links)]
    ppermute x6 -> x16, starting transfers between devices: 13.7 us -> 24 us  [the longest x5 10.2 us: beside(): lax.ppermute(far, 'space', links)]
    pallas_call x5, Pallas kernels: 34.9 us -> 28.2 us  [call(): pl.pallas_call(kernel, name=name, out_shape=[jax.ShapeDtypeStruct(shape,...]
    slice x3 -> x0, local copies, waits for them, and re-layouts: 4.19 us -> none  [the longest x2 2.2 us: on_device(): hi = lax.ppermute(own[:, :, :, :geo.side], 'space', down)]
    unnamed x14 -> x34, local copies, waits for them, and re-layouts: 2.06 us -> 2.68 us
  transfers between devices with their start and end apart: 6 -> 16, of which waited for: 4 -> 10; matrix products, arithmetic and copies ran while one was open for 2% -> 0% of each run, Pallas kernels for 2% -> 3%
where the time goes in v2:
time: 99.3 us; the launch traced here: 99 us
  waiting for transfers between devices  43.9 us (44%)
  Pallas kernels  28.2 us (28%)
  starting transfers between devices  24 us (24%)
  local copies, waits for them, and re-layouts  2.68 us (3%)
    pallas_call x5, Pallas kernels, call(): pl.pallas_call(kernel, name=name, out_shape=[jax.ShapeDtypeStruct(shape,...  28.2 us
    ppermute x5, waiting for transfers between devices, beside(): lax.ppermute(far, 'space', links)  22.4 us
    ppermute x6, waiting for transfers between devices, across(): return lax.ppermute(value, 'node', [(i, i ^ k) for i in range(n)])  20.6 us
    ppermute x5, starting transfers between devices, beside(): lax.ppermute(far, 'space', links)  10.2 us
    ppermute x6, starting transfers between devices, across(): return lax.ppermute(value, 'node', [(i, i ^ k) for i in range(n)])  8.12 us
    ppermute x5, starting transfers between devices, beside(): lax.ppermute(near, 'space', chip)  5.64 us
    unnamed x34, local copies, waits for them, and re-layouts  2.68 us
  transfers between devices with their start and end apart: 16, of which 10 were waited for; matrix products, arithmetic and copies ran while one was open for 0% of the time, Pallas kernels for 3%

profile of v2, /device:TPU:8, one launch (start us, length us, event | category | flops | bytes accessed | tf_op | source)
XLA Modules:
  0.0 99.0 jit_solution(9388344003093106256)
XLA Ops:
  0.0 2.5 %pack.1 = (f32[4,2,104,128]{3,2,1,0:T(8,128)}, f32[4,2,104,128]{3,2,1,0:T(8,128)}, f32[4,2,104,128]{3,2,1,0:T(8,128)}) custom-call(f32[1,4,4,64,256]{4,3,2,1,0:T(8,128)} %guess_ref.3), custom_call_target="tpu_custom_call" | custom-call | tf_op jit(solution)/shard_map/pack/pallas_call | solution.py:396
  2.5 1.6 %collective-permute-start.2 = (f32[4,2,104,128]{3,2,1,0:T(8,128)}, f32[4,2,104,128]{3,2,1,0:T(8,128)S(1)}, u32[]{:S(2)}, u32[]{:S(2)}) collective-permute-start(f32[4,2,104,128]{3,2,1,0:T(8,128)} %get-tuple-element.28), channel_id=1, source_target_pairs={{0,8},{8,0},{16,24},{24,16},{1,9},{9,1},{17,25},{25,17},{2,10},{10... | collective-permute-start | bytes 1277960 | tf_op jit(solution)/shard_map/ppermute | solution.py:405
  4.1 1.5 %collective-permute-start.5 = (f32[4,2,104,128]{3,2,1,0:T(8,128)}, f32[4,2,104,128]{3,2,1,0:T(8,128)S(1)}, u32[]{:S(2)}, u32[]{:S(2)}) collective-permute-start(f32[4,2,104,128]{3,2,1,0:T(8,128)} %get-tuple-element.29), channel_id=1, source_target_pairs={{0,16},{8,24},{16,0},{24,8},{1,17},{9,25},{17,1},{25,9},{2,18},{10... | collective-permute-start | bytes 1277960 | tf_op jit(solution)/shard_map/ppermute | solution.py:405
  5.6 3.3 %pack_own.1 = (f32[4,2,104,128]{3,2,1,0:T(8,128)}, f32[6,2,104,128]{3,2,1,0:T(8,128)}, f32[10,2,80,128]{3,2,1,0:T(8,128)}, f32[10,2,80,128]{3,2,1,0:T(8,128)}) custom-call(f32[1,4,4,64,256]{4,3,2,1,0:T(8,128)} %guess_ref.3, f32[4,4,64,256]{3,2,1,0:T(8,128)} %start_ref.1, s32[4,64,256]{2,1,0:T(8,128)} %heat_ref.1, s32[4,64,256]{2,1,0:T(8,128)} %solid_ref.1), custom_call_target="tpu_custom_call" | custom-call | tf_op jit(solution)/shard_map/pack_own/pallas_call | solution.py:396
  9.0 2.4 %collective-permute-start.1 = (f32[10,2,80,128]{3,2,1,0:T(8,128)}, f32[10,2,80,128]{3,2,1,0:T(8,128)S(1)}, u32[]{:S(2)}, u32[]{:S(2)}) collective-permute-start(f32[10,2,80,128]{3,2,1,0:T(8,128)} %get-tuple-element.24), channel_id=1, source_target_pairs={{1,2},{3,4},{5,6},{2,1},{4,3},{6,5},{9,10},{11,12},{13,14},{10,9},... | collective-permute-start | bytes 2457608 | tf_op jit(solution)/shard_map/ppermute | solution.py:411
  11.5 2.9 %collective-permute-done.2.refs_1_ = f32[4,2,104,128]{3,2,1,0:T(8,128)S(1)} collective-permute-done((f32[4,2,104,128]{3,2,1,0:T(8,128)}, f32[4,2,104,128]{3,2,1,0:T(8,128)S(1)}, u32[]{:S(2)}, u32[]{:S(2)}) %collective-permute-start.2) | collective-permute-done | bytes 426016 | tf_op jit(solution)/shard_map/ppermute | solution.py:405
  15.6 1.5 %collective-permute-start.8 = (f32[4,2,104,128]{3,2,1,0:T(8,128)S(1)}, f32[4,2,104,128]{3,2,1,0:T(8,128)S(1)}, u32[]{:S(2)}, u32[]{:S(2)}) collective-permute-start(f32[4,2,104,128]{3,2,1,0:T(8,128)S(1)} %copy-done.16), channel_id=1, source_target_pairs={{0,24},{8,16},{16,8},{24,0},{1,25},{9,17},{17,9},{25,1},{2,26},{10... | collective-permute-start | bytes 1277960 | tf_op jit(solution)/shard_map/ppermute | solution.py:405
  17.1 1.9 %collective-permute-start.4 = (f32[4,2,104,128]{3,2,1,0:T(8,128)S(1)}, f32[4,2,104,128]{3,2,1,0:T(8,128)S(1)}, u32[]{:S(2)}, u32[]{:S(2)}) collective-permute-start(f32[4,2,104,128]{3,2,1,0:T(8,128)S(1)} %collective-permute-done.2.refs_1_), channel_id=1, source_target_pairs={{1,2},{3,4},{5,6},{2,1},{4,3},{6,5},{9,10},{11,12},{13,14},{10,9},... | collective-permute-start | bytes 1277960 | tf_op jit(solution)/shard_map/ppermute | solution.py:411
  19.0 1.7 %collective-permute-start.3 = (f32[4,2,104,128]{3,2,1,0:T(8,128)S(1)}, f32[4,2,104,128]{3,2,1,0:T(8,128)S(1)}, u32[]{:S(2)}, u32[]{:S(2)}) collective-permute-start(f32[4,2,104,128]{3,2,1,0:T(8,128)S(1)} %collective-permute-done.2.refs_1_), channel_id=1, source_target_pairs={{0,1},{1,0},{2,3},{3,2},{4,5},{5,4},{6,7},{7,6},{8,9},{9,8},{10,11... | collective-permute-start | bytes 1277960 | tf_op jit(solution)/shard_map/ppermute | solution.py:411
  20.7 2.0 %collective-permute-start.7 = (f32[4,2,104,128]{3,2,1,0:T(8,128)S(1)}, f32[4,2,104,128]{3,2,1,0:T(8,128)S(1)}, u32[]{:S(2)}, u32[]{:S(2)}) collective-permute-start(f32[4,2,104,128]{3,2,1,0:T(8,128)S(1)} %collective-permute-done.5.refs_4_), channel_id=1, source_target_pairs={{1,2},{3,4},{5,6},{2,1},{4,3},{6,5},{9,10},{11,12},{13,14},{10,9},... | collective-permute-start | bytes 1277960 | tf_op jit(solution)/shard_map/ppermute | solution.py:411
  22.9 1.5 %collective-permute-start.6 = (f32[4,2,104,128]{3,2,1,0:T(8,128)S(1)}, f32[4,2,104,128]{3,2,1,0:T(8,128)S(1)}, u32[]{:S(2)}, u32[]{:S(2)}) collective-permute-start(f32[4,2,104,128]{3,2,1,0:T(8,128)S(1)} %collective-permute-done.5.refs_4_), channel_id=1, source_target_pairs={{0,1},{1,0},{2,3},{3,2},{4,5},{5,4},{6,7},{7,6},{8,9},{9,8},{10,11... | collective-permute-start | bytes 1277960 | tf_op jit(solution)/shard_map/ppermute | solution.py:411
  24.4 2.4 %collective-permute-done.8.refs_7_ = f32[4,2,104,128]{3,2,1,0:T(8,128)S(1)} collective-permute-done((f32[4,2,104,128]{3,2,1,0:T(8,128)S(1)}, f32[4,2,104,128]{3,2,1,0:T(8,128)S(1)}, u32[]{:S(2)}, u32[]{:S(2)}) %collective-permute-start.8) | collective-permute-done | bytes 426016 | tf_op jit(solution)/shard_map/ppermute | solution.py:405
  26.8 1.9 %collective-permute-start.10 = (f32[4,2,104,128]{3,2,1,0:T(8,128)S(1)}, f32[4,2,104,128]{3,2,1,0:T(8,128)S(1)}, u32[]{:S(2)}, u32[]{:S(2)}) collective-permute-start(f32[4,2,104,128]{3,2,1,0:T(8,128)S(1)} %collective-permute-done.8.refs_7_), channel_id=1, source_target_pairs={{1,2},{3,4},{5,6},{2,1},{4,3},{6,5},{9,10},{11,12},{13,14},{10,9},... | collective-permute-start | bytes 1277960 | tf_op jit(solution)/shard_map/ppermute | solution.py:411
  28.8 1.7 %collective-permute-start.9 = (f32[4,2,104,128]{3,2,1,0:T(8,128)S(1)}, f32[4,2,104,128]{3,2,1,0:T(8,128)S(1)}, u32[]{:S(2)}, u32[]{:S(2)}) collective-permute-start(f32[4,2,104,128]{3,2,1,0:T(8,128)S(1)} %collective-permute-done.8.refs_7_), channel_id=1, source_target_pairs={{0,1},{1,0},{2,3},{3,2},{4,5},{5,4},{6,7},{7,6},{8,9},{9,8},{10,11... | collective-permute-start | bytes 1277960 | tf_op jit(solution)/shard_map/ppermute | solution.py:411
  30.5 1.5 %collective-permute-done.7.refs_6_ = f32[4,2,104,128]{3,2,1,0:T(8,128)S(1)} collective-permute-done((f32[4,2,104,128]{3,2,1,0:T(8,128)S(1)}, f32[4,2,104,128]{3,2,1,0:T(8,128)S(1)}, u32[]{:S(2)}, u32[]{:S(2)}) %collective-permute-start.7) | collective-permute-done | bytes 426016 | tf_op jit(solution)/shard_map/ppermute | solution.py:411
  32.0 4.6 %collective-permute-done.10.refs_9_ = f32[4,2,104,128]{3,2,1,0:T(8,128)S(1)} collective-permute-done((f32[4,2,104,128]{3,2,1,0:T(8,128)S(1)}, f32[4,2,104,128]{3,2,1,0:T(8,128)S(1)}, u32[]{:S(2)}, u32[]{:S(2)}) %collective-permute-start.10) | collective-permute-done | bytes 426016 | tf_op jit(solution)/shard_map/ppermute | solution.py:411
  37.5 10.3 %sweep_opening.1 = (f32[4,4,2,104,128]{4,3,2,1,0:T(8,128)}, f32[4,4,2,80,128]{4,3,2,1,0:T(8,128)}, f32[4,4,2,80,128]{4,3,2,1,0:T(8,128)}) custom-call(f32[6,2,104,128]{3,2,1,0:T(8,128)} %get-tuple-element.22.aux_ref, f32[10,2,80,128]{3,2,1,0:T(8,128)} %copy-done, f32[10,2,80,128]{3,2,1,0:T(8,128)} %copy-done.1, ...), custom_call_target="tpu_custom_call" | custom-call | tf_op jit(solution)/shard_map/sweep_opening/pallas_call | solution.py:396
  48.3 2.0 %collective-permute-start.12 = (f32[4,4,2,80,128]{4,3,2,1,0:T(8,128)}, f32[4,4,2,80,128]{4,3,2,1,0:T(8,128)S(1)}, u32[]{:S(2)}, u32[]{:S(2)}) collective-permute-start(f32[4,4,2,80,128]{4,3,2,1,0:T(8,128)} %get-tuple-element.34), channel_id=1, source_target_pairs={{1,2},{3,4},{5,6},{2,1},{4,3},{6,5},{9,10},{11,12},{13,14},{10,9},... | collective-permute-start | bytes 3932168 | tf_op jit(solution)/shard_map/ppermute | solution.py:411
  51.2 16.2 %collective-permute-done.12.refs_2_ = f32[4,4,2,80,128]{4,3,2,1,0:T(8,128)S(1)} collective-permute-done((f32[4,4,2,80,128]{4,3,2,1,0:T(8,128)}, f32[4,4,2,80,128]{4,3,2,1,0:T(8,128)S(1)}, u32[]{:S(2)}, u32[]{:S(2)}) %collective-permute-start.12) | collective-permute-done | bytes 1310752 | tf_op jit(solution)/shard_map/ppermute | solution.py:411
  68.5 9.7 %sweep_closing.1 = (f32[4,2,80,128]{3,2,1,0:T(8,128)}, f32[4,2,80,128]{3,2,1,0:T(8,128)}, f32[4,2,80,128]{3,2,1,0:T(8,128)}, f32[4,2,80,128]{3,2,1,0:T(8,128)}) custom-call(f32[6,2,104,128]{3,2,1,0:T(8,128)} %get-tuple-element.22.aux_ref, f32[10,2,80,128]{3,2,1,0:T(8,128)} %copy-done, f32[10,2,80,128]{3,2,1,0:T(8,128)} %copy-done.1, ...), custom_call_target="tpu_custom_call" | custom-call | tf_op jit(solution)/shard_map/sweep_closing/pallas_call | solution.py:396
  79.9 1.9 %collective-permute-start.15 = (f32[4,2,80,128]{3,2,1,0:T(8,128)}, f32[4,2,80,128]{3,2,1,0:T(8,128)S(1)}, u32[]{:S(2)}, u32[]{:S(2)}) collective-permute-start(f32[4,2,80,128]{3,2,1,0:T(8,128)} %get-tuple-element.38), channel_id=1, source_target_pairs={{0,24},{8,16},{16,8},{24,0},{1,25},{9,17},{17,9},{25,1},{2,26},{10... | collective-permute-start | bytes 983048 | tf_op jit(solution)/shard_map/ppermute | solution.py:405
  81.8 7.3 %collective-permute-done.13.refs_1_ = f32[4,2,80,128]{3,2,1,0:T(8,128)S(1)} collective-permute-done((f32[4,2,80,128]{3,2,1,0:T(8,128)}, f32[4,2,80,128]{3,2,1,0:T(8,128)S(1)}, u32[]{:S(2)}, u32[]{:S(2)}) %collective-permute-start.13) | collective-permute-done | bytes 327712 | tf_op jit(solution)/shard_map/ppermute | solution.py:405
  89.1 6.8 %collective-permute-done.15.refs_3_ = f32[4,2,80,128]{3,2,1,0:T(8,128)S(1)} collective-permute-done((f32[4,2,80,128]{3,2,1,0:T(8,128)}, f32[4,2,80,128]{3,2,1,0:T(8,128)S(1)}, u32[]{:S(2)}, u32[]{:S(2)}) %collective-permute-start.15) | collective-permute-done | bytes 327712 | tf_op jit(solution)/shard_map/ppermute | solution.py:405
  96.6 2.4 %unpack.1 = f32[1,4,4,64,256]{4,3,2,1,0:T(8,128)} custom-call(f32[4,2,80,128]{3,2,1,0:T(8,128)} %get-tuple-element.35.refs_0_, f32[4,2,80,128]{3,2,1,0:T(8,128)} %copy-done.13, f32[4,2,80,128]{3,2,1,0:T(8,128)} %copy-done.14, f32[4,2,80,128]{3,2,1,0:T(8,128)} %copy-done.15), custom_call_target="tpu_custom_call" | custom-call | tf_op jit(solution)/shard_map/unpack/pallas_call | solution.py:396
  (47 shorter events, 7.2 us)
Async XLA Ops:
  2.5 13.1 %copy-start.16 = (f32[4,2,104,128]{3,2,1,0:T(8,128)S(1)}, f32[4,2,104,128]{3,2,1,0:T(8,128)}, u32[]{:S(2)}) copy-start(f32[4,2,104,128]{3,2,1,0:T(8,128)} %get-tuple-element.31) | copy-start | bytes 1277956
  2.5 11.8 %collective-permute-start.2 = (f32[4,2,104,128]{3,2,1,0:T(8,128)}, f32[4,2,104,128]{3,2,1,0:T(8,128)S(1)}, u32[]{:S(2)}, u32[]{:S(2)}) collective-permute-start(f32[4,2,104,128]{3,2,1,0:T(8,128)} %get-tuple-element.28), channel_id=1, source_target_pairs={{0,8},{8,0},{16,24},{24,16},{1,9},{9,1},{17,25},{25,17},{2,10},{10... | collective-permute-start | bytes 1277960 | tf_op jit(solution)/shard_map/ppermute | solution.py:405
  4.1 11.5 %collective-permute-start.5 = (f32[4,2,104,128]{3,2,1,0:T(8,128)}, f32[4,2,104,128]{3,2,1,0:T(8,128)S(1)}, u32[]{:S(2)}, u32[]{:S(2)}) collective-permute-start(f32[4,2,104,128]{3,2,1,0:T(8,128)} %get-tuple-element.29), channel_id=1, source_target_pairs={{0,16},{8,24},{16,0},{24,8},{1,17},{9,25},{17,1},{25,9},{2,18},{10... | collective-permute-start | bytes 1277960 | tf_op jit(solution)/shard_map/ppermute | solution.py:405
  8.9 11.8 %collective-permute-start = (f32[10,2,80,128]{3,2,1,0:T(8,128)}, f32[10,2,80,128]{3,2,1,0:T(8,128)S(1)}, u32[]{:S(2)}, u32[]{:S(2)}) collective-permute-start(f32[10,2,80,128]{3,2,1,0:T(8,128)} %get-tuple-element.23), channel_id=1, source_target_pairs={{0,1},{1,0},{2,3},{3,2},{4,5},{5,4},{6,7},{7,6},{8,9},{9,8},{10,11... | collective-permute-start | bytes 2457608 | tf_op jit(solution)/shard_map/ppermute | solution.py:411
  9.0 13.9 %collective-permute-start.1 = (f32[10,2,80,128]{3,2,1,0:T(8,128)}, f32[10,2,80,128]{3,2,1,0:T(8,128)S(1)}, u32[]{:S(2)}, u32[]{:S(2)}) collective-permute-start(f32[10,2,80,128]{3,2,1,0:T(8,128)} %get-tuple-element.24), channel_id=1, source_target_pairs={{1,2},{3,4},{5,6},{2,1},{4,3},{6,5},{9,10},{11,12},{13,14},{10,9},... | collective-permute-start | bytes 2457608 | tf_op jit(solution)/shard_map/ppermute | solution.py:411
  14.3 22.2 %copy-start.4 = (f32[4,2,104,128]{3,2,1,0:T(8,128)}, f32[4,2,104,128]{3,2,1,0:T(8,128)S(1)}, u32[]{:S(2)}) copy-start(f32[4,2,104,128]{3,2,1,0:T(8,128)S(1)} %collective-permute-done.2.refs_1_) | copy-start | bytes 1277956
  15.6 21.0 %copy-start.5 = (f32[4,2,104,128]{3,2,1,0:T(8,128)}, f32[4,2,104,128]{3,2,1,0:T(8,128)S(1)}, u32[]{:S(2)}) copy-start(f32[4,2,104,128]{3,2,1,0:T(8,128)S(1)} %collective-permute-done.5.refs_4_) | copy-start | bytes 1277956
  15.6 11.3 %collective-permute-start.8 = (f32[4,2,104,128]{3,2,1,0:T(8,128)S(1)}, f32[4,2,104,128]{3,2,1,0:T(8,128)S(1)}, u32[]{:S(2)}, u32[]{:S(2)}) collective-permute-start(f32[4,2,104,128]{3,2,1,0:T(8,128)S(1)} %copy-done.16), channel_id=1, source_target_pairs={{0,24},{8,16},{16,8},{24,0},{1,25},{9,17},{17,9},{25,1},{2,26},{10... | collective-permute-start | bytes 1277960 | tf_op jit(solution)/shard_map/ppermute | solution.py:405
  17.1 11.7 %collective-permute-start.4 = (f32[4,2,104,128]{3,2,1,0:T(8,128)S(1)}, f32[4,2,104,128]{3,2,1,0:T(8,128)S(1)}, u32[]{:S(2)}, u32[]{:S(2)}) collective-permute-start(f32[4,2,104,128]{3,2,1,0:T(8,128)S(1)} %collective-permute-done.2.refs_1_), channel_id=1, source_target_pairs={{1,2},{3,4},{5,6},{2,1},{4,3},{6,5},{9,10},{11,12},{13,14},{10,9},... | collective-permute-start | bytes 1277960 | tf_op jit(solution)/shard_map/ppermute | solution.py:411
  19.0 11.5 %collective-permute-start.3 = (f32[4,2,104,128]{3,2,1,0:T(8,128)S(1)}, f32[4,2,104,128]{3,2,1,0:T(8,128)S(1)}, u32[]{:S(2)}, u32[]{:S(2)}) collective-permute-start(f32[4,2,104,128]{3,2,1,0:T(8,128)S(1)} %collective-permute-done.2.refs_1_), channel_id=1, source_target_pairs={{0,1},{1,0},{2,3},{3,2},{4,5},{5,4},{6,7},{7,6},{8,9},{9,8},{10,11... | collective-permute-start | bytes 1277960 | tf_op jit(solution)/shard_map/ppermute | solution.py:411
  20.7 15.9 %copy-start = (f32[10,2,80,128]{3,2,1,0:T(8,128)}, f32[10,2,80,128]{3,2,1,0:T(8,128)S(1)}, u32[]{:S(2)}) copy-start(f32[10,2,80,128]{3,2,1,0:T(8,128)S(1)} %collective-permute-done.near0_ref) | copy-start | bytes 2457604
  20.7 11.3 %collective-permute-start.7 = (f32[4,2,104,128]{3,2,1,0:T(8,128)S(1)}, f32[4,2,104,128]{3,2,1,0:T(8,128)S(1)}, u32[]{:S(2)}, u32[]{:S(2)}) collective-permute-start(f32[4,2,104,128]{3,2,1,0:T(8,128)S(1)} %collective-permute-done.5.refs_4_), channel_id=1, source_target_pairs={{1,2},{3,4},{5,6},{2,1},{4,3},{6,5},{9,10},{11,12},{13,14},{10,9},... | collective-permute-start | bytes 1277960 | tf_op jit(solution)/shard_map/ppermute | solution.py:411
  22.9 13.7 %copy-start.1 = (f32[10,2,80,128]{3,2,1,0:T(8,128)}, f32[10,2,80,128]{3,2,1,0:T(8,128)S(1)}, u32[]{:S(2)}) copy-start(f32[10,2,80,128]{3,2,1,0:T(8,128)S(1)} %collective-permute-done.1.far0_ref) | copy-start | bytes 2457604
  22.9 9.1 %collective-permute-start.6 = (f32[4,2,104,128]{3,2,1,0:T(8,128)S(1)}, f32[4,2,104,128]{3,2,1,0:T(8,128)S(1)}, u32[]{:S(2)}, u32[]{:S(2)}) collective-permute-start(f32[4,2,104,128]{3,2,1,0:T(8,128)S(1)} %collective-permute-done.5.refs_4_), channel_id=1, source_target_pairs={{0,1},{1,0},{2,3},{3,2},{4,5},{5,4},{6,7},{7,6},{8,9},{9,8},{10,11... | collective-permute-start | bytes 1277960 | tf_op jit(solution)/shard_map/ppermute | solution.py:411
  26.8 9.8 %copy-start.6 = (f32[4,2,104,128]{3,2,1,0:T(8,128)}, f32[4,2,104,128]{3,2,1,0:T(8,128)S(1)}, u32[]{:S(2)}) copy-start(f32[4,2,104,128]{3,2,1,0:T(8,128)S(1)} %collective-permute-done.8.refs_7_) | copy-start | bytes 1277956
  26.8 9.7 %collective-permute-start.10 = (f32[4,2,104,128]{3,2,1,0:T(8,128)S(1)}, f32[4,2,104,128]{3,2,1,0:T(8,128)S(1)}, u32[]{:S(2)}, u32[]{:S(2)}) collective-permute-start(f32[4,2,104,128]{3,2,1,0:T(8,128)S(1)} %collective-permute-done.8.refs_7_), channel_id=1, source_target_pairs={{1,2},{3,4},{5,6},{2,1},{4,3},{6,5},{9,10},{11,12},{13,14},{10,9},... | collective-permute-start | bytes 1277960 | tf_op jit(solution)/shard_map/ppermute | solution.py:411
  28.8 7.9 %copy-start.7 = (f32[4,2,104,128]{3,2,1,0:T(8,128)}, f32[4,2,104,128]{3,2,1,0:T(8,128)S(1)}, u32[]{:S(2)}) copy-start(f32[4,2,104,128]{3,2,1,0:T(8,128)S(1)} %collective-permute-done.4.refs_3_) | copy-start | bytes 1277956
  28.8 7.8 %collective-permute-start.9 = (f32[4,2,104,128]{3,2,1,0:T(8,128)S(1)}, f32[4,2,104,128]{3,2,1,0:T(8,128)S(1)}, u32[]{:S(2)}, u32[]{:S(2)}) collective-permute-start(f32[4,2,104,128]{3,2,1,0:T(8,128)S(1)} %collective-permute-done.8.refs_7_), channel_id=1, source_target_pairs={{0,1},{1,0},{2,3},{3,2},{4,5},{5,4},{6,7},{7,6},{8,9},{9,8},{10,11... | collective-permute-start | bytes 1277960 | tf_op jit(solution)/shard_map/ppermute | solution.py:411
  47.8 3.4 %collective-permute-start.11 = (f32[4,4,2,80,128]{4,3,2,1,0:T(8,128)}, f32[4,4,2,80,128]{4,3,2,1,0:T(8,128)S(1)}, u32[]{:S(2)}, u32[]{:S(2)}) collective-permute-start(f32[4,4,2,80,128]{4,3,2,1,0:T(8,128)} %get-tuple-element.33), channel_id=1, source_target_pairs={{0,1},{1,0},{2,3},{3,2},{4,5},{5,4},{6,7},{7,6},{8,9},{9,8},{10,11... | collective-permute-start | bytes 3932168 | tf_op jit(solution)/shard_map/ppermute | solution.py:411
  48.3 19.1 %collective-permute-start.12 = (f32[4,4,2,80,128]{4,3,2,1,0:T(8,128)}, f32[4,4,2,80,128]{4,3,2,1,0:T(8,128)S(1)}, u32[]{:S(2)}, u32[]{:S(2)}) collective-permute-start(f32[4,4,2,80,128]{4,3,2,1,0:T(8,128)} %get-tuple-element.34), channel_id=1, source_target_pairs={{1,2},{3,4},{5,6},{2,1},{4,3},{6,5},{9,10},{11,12},{13,14},{10,9},... | collective-permute-start | bytes 3932168 | tf_op jit(solution)/shard_map/ppermute | solution.py:411
  51.2 16.3 %copy-start.2 = (f32[4,4,2,80,128]{4,3,2,1,0:T(8,128)}, f32[4,4,2,80,128]{4,3,2,1,0:T(8,128)S(1)}, u32[]{:S(2)}) copy-start(f32[4,4,2,80,128]{4,3,2,1,0:T(8,128)S(1)} %collective-permute-done.11.refs_1_) | copy-start | bytes 3932164
  78.3 10.8 %collective-permute-start.13 = (f32[4,2,80,128]{3,2,1,0:T(8,128)}, f32[4,2,80,128]{3,2,1,0:T(8,128)S(1)}, u32[]{:S(2)}, u32[]{:S(2)}) collective-permute-start(f32[4,2,80,128]{3,2,1,0:T(8,128)} %get-tuple-element.36), channel_id=1, source_target_pairs={{0,8},{8,0},{16,24},{24,16},{1,9},{9,1},{17,25},{25,17},{2,10},{10... | collective-permute-start | bytes 983048 | tf_op jit(solution)/shard_map/ppermute | solution.py:405
  78.9 10.2 %collective-permute-start.14 = (f32[4,2,80,128]{3,2,1,0:T(8,128)}, f32[4,2,80,128]{3,2,1,0:T(8,128)S(1)}, u32[]{:S(2)}, u32[]{:S(2)}) collective-permute-start(f32[4,2,80,128]{3,2,1,0:T(8,128)} %get-tuple-element.37), channel_id=1, source_target_pairs={{0,16},{8,24},{16,0},{24,8},{1,17},{9,25},{17,1},{25,9},{2,18},{10... | collective-permute-start | bytes 983048 | tf_op jit(solution)/shard_map/ppermute | solution.py:405
  79.9 16.0 %collective-permute-start.15 = (f32[4,2,80,128]{3,2,1,0:T(8,128)}, f32[4,2,80,128]{3,2,1,0:T(8,128)S(1)}, u32[]{:S(2)}, u32[]{:S(2)}) collective-permute-start(f32[4,2,80,128]{3,2,1,0:T(8,128)} %get-tuple-element.38), channel_id=1, source_target_pairs={{0,24},{8,16},{16,8},{24,0},{1,25},{9,17},{17,9},{25,1},{2,26},{10... | collective-permute-start | bytes 983048 | tf_op jit(solution)/shard_map/ppermute | solution.py:405
  (9 other events, 32.4 us)

commit v3 on v2

v3 whole, which is shorter than its diff:
```python
import functools
import math

import jax
import jax.numpy as jnp
import numpy as np
from jax import lax
from jax.experimental import pallas as pl
from jax.experimental.pallas import tpu as pltpu
from jax.sharding import PartitionSpec as P

SWEEPS = 2
JACOBI = 3
LANES = 128
VMEM_SLACK = 2 << 20

advect_rate = 0.25
buoyancy = 0.5
heating = 1.0
diffusion = (0.5, 0.5, 0.5, 0.35)


def legendre_value(order, place):
    previous = 1.0
    current = place
    for degree in range(1, order):
        following = ((2 * degree + 1) * place * current - degree * previous) / (degree + 1)
        previous = current
        current = following
    return current


def radau_tables(count):

    def radau_poly(place):
        return legendre_value(count, place) - legendre_value(count - 1, place)

    samples = 4000 * count
    roots_found = []
    left_end = -1.0
    left_value = radau_poly(left_end)
    for index in range(1, samples + 1):
        right_end = -1.0 + (2.0 - 1e-07) * index / samples
        right_value = radau_poly(right_end)
        if left_value * right_value < 0.0:
            low_end = left_end
            high_end = right_end
            low_value = left_value
            for repeat in range(200):
                middle = 0.5 * (low_end + high_end)
                middle_value = radau_poly(middle)
                if low_value * middle_value <= 0.0:
                    high_end = middle
                else:
                    low_end = middle
                    low_value = middle_value
            roots_found.append(0.5 * (low_end + high_end))
        left_end = right_end
        left_value = right_value
    points = [(value + 1.0) / 2.0 for value in roots_found[: count - 1]] + [1.0]
    table = []
    for row in range(count):
        table.append([0.0] * count)
    for column in range(count):
        coefficients = [1.0]
        for other in range(count):
            if other == column:
                continue
            scale = 1.0 / (points[column] - points[other])
            widened = [0.0] * (len(coefficients) + 1)
            for index in range(len(coefficients)):
                widened[index + 1] += coefficients[index] * scale
                widened[index] -= points[other] * coefficients[index] * scale
            coefficients = widened
        for row in range(count):
            total = 0.0
            for index in range(len(coefficients)):
                total += coefficients[index] * points[row] ** (index + 1) / (index + 1)
            table[row][column] = total
    return (points, table)


def size_of(shape):
    return math.prod(getattr(shape, "shape", shape))


def round_up(value, step):
    return -(-value // step) * step


class Geometry:
    def __init__(self, nodes, planes, depth):
        overlap = SWEEPS * JACOBI if nodes > 1 else 0
        self.nodes, self.planes, self.depth = nodes, planes, depth
        self.window = -(-(depth + 2 * overlap * (nodes - 1)) // nodes)
        step = self.window - 2 * overlap
        assert step > 0 and planes >= JACOBI
        self.offset = [min(p * step, depth - self.window) for p in range(nodes)]
        first = [0] + [p * step + overlap for p in range(1, nodes)]
        last = first[1:] + [depth]
        self.first, self.count = first, [b - a for a, b in zip(first, last)]
        self.stride = self.window + 1
        while (planes * self.stride) % 8:
            self.stride += 1
        self.rows = planes * self.stride
        self.side = round_up(JACOBI * self.stride, 8)
        self.low = 8 + self.side
        self.total = self.low + self.rows + self.side + 8
        self.back = max(self.count)
        while (planes * self.back) % 8:
            self.back += 1

    def trims(self, closing, reach):
        packed, cuts = 0, []
        for d in range(1, reach + 1):
            cut = closing * JACOBI + d
            cuts.append((d, cut, packed, self.window - cut))
            packed += self.window - cut
        return cuts, round_up(packed, 8)

    def mixed(self):
        row, parts = 0, []
        for f in range(10):
            cuts, count = self.trims(False, JACOBI if f < 4 else JACOBI - 1)
            for h in range(2):
                parts.append((f, h, cuts, row))
                row += count
        self.mixed_rows = row
        return parts

    def span(self, reach):
        begin = (self.low - reach * self.stride) // 8 * 8
        end = round_up(self.low + (self.planes + reach) * self.stride, 8)
        assert begin - self.stride >= 0 and end + self.stride <= self.total
        return begin, end

    def early(self, upper):
        begin, end = self.span(JACOBI - 1)
        second_begin, second_end = self.span(JACOBI - 2)
        if upper:
            end = (self.low + (self.planes - 1) * self.stride) // 8 * 8
            second_end = (end - self.stride) // 8 * 8
        else:
            begin = round_up(self.low + self.stride, 8)
            second_begin = round_up(begin + self.stride, 8)
        return (begin, end), (second_begin, second_end)

    def late(self, upper):
        rest = []
        for whole, part in zip((self.span(JACOBI - 1), self.span(JACOBI - 2)), self.early(upper)):
            rest.append((part[1], whole[1]) if upper else (whole[0], part[0]))
        return rest


def copy_all(pairs, sems):
    copies = [pltpu.make_async_copy(source, target, sems.at[i]) for i, (source, target) in enumerate(pairs)]
    for copy in copies:
        copy.start()
    for copy in copies:
        copy.wait()


def pack_kernel(geo, guess_ref, *refs):
    *outs, windows, sems = refs
    me = lax.axis_index("node")
    blank = jnp.zeros((geo.stride - geo.window, LANES), jnp.float32)
    for p in range(geo.nodes):
        for f in range(4):
            for x in range(geo.planes):
                for h in range(2):
                    at = x * geo.stride
                    windows[p, f, h, at : at + geo.window] = guess_ref[
                        0, f, x, geo.offset[p] : geo.offset[p] + geo.window, h * LANES : (h + 1) * LANES
                    ]
                    windows[p, f, h, at + geo.window : at + geo.stride] = blank
    copy_all([(windows.at[me ^ k], outs[k - 1]) for k in range(1, geo.nodes)], sems)


def send_rows(geo, odd):
    far = geo.rows - geo.side
    return pl.multiple_of(far * (1 - odd), 8), pl.multiple_of(far * odd, 8)


def each_place(me, odd, body):
    for upper in (False, True):
        for lowest in (False, True):
            pl.when((odd == int(upper)) & ((me == 0) == lowest))(functools.partial(body, upper, lowest))


def trim(geo, cuts, upper, lowest, source, at, target, to=0):
    for d, cut, packed, count in cuts:
        plane = geo.planes - d if upper else d - 1
        row = at + plane * geo.stride + (0 if lowest else cut)
        target[to + packed : to + packed + count] = source[row : row + count]


def place(geo, cuts, upper, lowest, source, target, start=0):
    for d, cut, packed, count in cuts:
        plane = geo.planes - 1 + d if upper else -d
        row = geo.low + plane * geo.stride + (0 if lowest else cut)
        target[row : row + count] = source[start + packed : start + packed + count]


def trim_kernel(geo, own_ref, far_ref):
    def body(upper, lowest):
        for f in range(4):
            for h in range(2):
                trim(geo, geo.trims(False, JACOBI)[0], upper, lowest, own_ref.at[f, h], 0, far_ref.at[f, h])

    each_place(lax.axis_index("node"), lax.axis_index("space") % 2, body)


def halo_rows(geo, odd):
    below, above = geo.low - geo.side, geo.low + geo.rows
    return (
        pl.multiple_of(above + (below - above) * odd, 8),
        pl.multiple_of(below + (above - below) * odd, 8),
    )


def pack_own_kernel(
    geo, guess_hbm, start_hbm, heat_hbm, solid_hbm, own_ref, aux_ref, near_ref, far_ref,
    guess_ref, start_ref, heat_ref, solid_ref, packed, sems,
):
    me, odd = lax.axis_index("node"), lax.axis_index("space") % 2
    copy_all(
        [(guess_hbm, guess_ref), (start_hbm, start_ref), (heat_hbm, heat_ref), (solid_hbm, solid_ref)], sems
    )
    blank = jnp.zeros((geo.stride - geo.window, LANES), jnp.float32)
    for p in range(geo.nodes):

        @pl.when(me == p)
        def _():
            rows = slice(geo.offset[p], geo.offset[p] + geo.window)
            for x in range(geo.planes):
                for h in range(2):
                    at = x * geo.stride
                    lanes = slice(h * LANES, (h + 1) * LANES)
                    for f in range(4):
                        packed[f, h, at : at + geo.window] = guess_ref[0, f, x, rows, lanes]
                        packed[4 + f, h, at : at + geo.window] = start_ref[f, x, rows, lanes]
                    packed[8, h, at : at + geo.window] = heating * heat_ref[x, rows, lanes].astype(jnp.float32)
                    packed[9, h, at : at + geo.window] = 1.0 - solid_ref[x, rows, lanes].astype(jnp.float32)
                    for f in range(10):
                        packed[f, h, at + geo.window : at + geo.stride] = blank

    near, far = send_rows(geo, odd)
    copies = [
        pltpu.make_async_copy(packed.at[:, :, pl.ds(near, geo.side)], near_ref, sems.at[0]),
        pltpu.make_async_copy(packed.at[pl.ds(0, 4)], own_ref, sems.at[1]),
        pltpu.make_async_copy(packed.at[pl.ds(4, 6)], aux_ref, sems.at[2]),
    ]
    for copy in copies:
        copy.start()

    def body(upper, lowest):
        for f, h, cuts, row in geo.mixed():
            trim(geo, cuts, upper, lowest, packed.at[f, h], 0, far_ref, row)

    each_place(me, odd, body)
    for copy in copies:
        copy.wait()


def pick(index, values):
    chosen = jnp.float32(values[-1])
    for i in reversed(range(len(values) - 1)):
        chosen = jnp.where(index == i, jnp.float32(values[i]), chosen)
    return chosen


def lane_sides(a, b):
    lane = lax.broadcasted_iota(jnp.int32, (8, LANES), 1)
    is_first, is_last = lane == 0, lane == LANES - 1
    ra, rb = pltpu.roll(a, 1, 1), pltpu.roll(b, 1, 1)
    la, lb = pltpu.roll(a, LANES - 1, 1), pltpu.roll(b, LANES - 1, 1)
    minus = (jnp.where(is_first, 0.0, ra), jnp.where(is_first, ra, rb))
    plus = (jnp.where(is_last, lb, la), jnp.where(is_last, 0.0, lb))
    return minus, plus


class Steps:
    def __init__(self, geo, points, table, aux, mask, field, tend, base, first):
        self.geo, self.points, self.table = geo, points, table
        self.aux, self.mask, self.field, self.tend, self.base, self.first = aux, mask, field, tend, base, first

    def slopes(self, j, begin, end):
        field, aux, stride = self.field, self.aux, self.geo.stride
        for r in range(begin, end, 8):
            rows = pl.ds(r, 8)
            vel = []
            for h in range(2):
                vel.append([(-0.5 * advect_rate) * field[j, f, h, rows] for f in range(3)])
            for f in range(4):
                centre = [field[j, f, h, rows] for h in range(2)]
                minus, plus = lane_sides(centre[0], centre[1])
                for h in range(2):
                    xp, xm = field[j, f, h, pl.ds(r + stride, 8)], field[j, f, h, pl.ds(r - stride, 8)]
                    zp, zm = field[j, f, h, pl.ds(r + 1, 8)], field[j, f, h, pl.ds(r - 1, 8)]
                    near = (xp + xm) + (zp + zm) + (plus[h] + minus[h])
                    moved = vel[h][0] * (xp - xm) + vel[h][1] * (plus[h] - minus[h]) + vel[h][2] * (zp - zm)
                    total = moved + diffusion[f] * (near - 6.0 * centre[h])
                    if f == 2:
                        total = total + buoyancy * field[j, 3, h, rows]
                    if f == 3:
                        total = total + aux[4, h, rows]
                    else:
                        total = total * aux[5, h, rows]
                    self.tend[j, f, h, rows] = total
                    self.base[j, f, h, rows] = near

    def quadrature(self, begin, end):
        n, points, table = self.geo.nodes, self.points, self.table

        def body(t, _):
            rows = pl.ds(pl.multiple_of(t * 8, 8), 8)
            inside = self.mask[rows]
            for f in range(4):
                scale = [inside * (1.0 / (1.0 + 6.0 * points[m] * diffusion[f])) for m in range(n)]
                for h in range(2):
                    slopes = [self.tend[j, f, h, rows] for j in range(n)]
                    begun = self.aux[f, h, rows]
                    for m in range(n):
                        c = points[m] * diffusion[f]
                        total = begun + (6.0 * c) * self.field[m, f, h, rows]
                        for j in range(n):
                            total = total + table[m][j] * slopes[j]
                        total = total * scale[m]
                        self.first[m, f, h, rows] = total
                        self.base[m, f, h, rows] = total - (c * scale[m]) * self.base[m, f, h, rows]
            return 0

        lax.fori_loop(begin // 8, end // 8, body, 0)

    def weights(self, m):
        return [pick(m, [p * d / (1.0 + 6.0 * p * d) for p in self.points]) for d in diffusion]

    def relax_rows(self, source, target, m, f, r, weight, to):
        stride = self.geo.stride
        minus, plus = lane_sides(source[m, f, 0, pl.ds(r, 8)], source[m, f, 1, pl.ds(r, 8)])
        for h in range(2):
            near = (
                (source[m, f, h, pl.ds(r + stride, 8)] + source[m, f, h, pl.ds(r - stride, 8)])
                + (source[m, f, h, pl.ds(r + 1, 8)] + source[m, f, h, pl.ds(r - 1, 8)])
                + (plus[h] + minus[h])
            )
            target[m, f, h, pl.ds(to, 8)] = self.base[m, f, h, pl.ds(r, 8)] + weight * near

    def relax(self, source, target, m, begin, end):
        weight = self.weights(m)
        for r in range(begin, end, 8):
            inside = self.mask[pl.ds(r, 8)]
            for f in range(4):
                self.relax_rows(source, target, m, f, r, inside * weight[f], r)


def each_node(count, body):
    def step(i, _):
        body(i)
        return 0

    lax.fori_loop(0, count, step, 0)


def by_side(odd, body):
    for upper in (False, True):
        pl.when(odd == int(upper))(functools.partial(body, upper))


def start_kernel(geo, opening, tiles, points, table, *refs):
    n, low, side = geo.nodes, geo.low, geo.side
    me, tile = lax.axis_index("node"), lax.axis_index("space")
    odd = tile % 2
    near, far = halo_rows(geo, odd)
    near_from, _ = send_rows(geo, 1 - odd)
    own_rows, near_rows, far_rows = pl.ds(low, geo.rows), pl.ds(near, side), pl.ds(far, side)
    pairs = []
    if opening:
        aux_ref, near0_ref, far0_ref, own0_ref, *rest, aux, mask, field, tend, base, first, sems = refs
        pairs = [(aux_ref, aux.at[:, :, own_rows]), (near0_ref.at[pl.ds(4, 6)], aux.at[:, :, near_rows])]
        fars = []
        for k in range(n):
            sources = own0_ref, near0_ref.at[pl.ds(0, 4)]
            if k:
                own_ref, near_ref, *rest = rest
                sources = own_ref, near_ref.at[:, :, pl.ds(near_from, side)]
            if 0 < k < n - 1:
                far_ref, *rest = rest
                fars.append(far_ref)
            pairs += zip(sources, [field.at[me ^ k, :, :, rows] for rows in (own_rows, near_rows)])
    else:
        aux, mask, own_ref, near_ref, field, tend, base, first, sems = refs
        for k in range(n):
            pairs += [(own_ref.at[k], field.at[k, :, :, own_rows]), (near_ref.at[k], field.at[k, :, :, near_rows])]
    copies = [pltpu.make_async_copy(source, target, sems.at[i]) for i, (source, target) in enumerate(pairs)]
    for copy in copies:
        copy.start()

    field[:, :, :, far_rows] = jnp.zeros((n, 4, 2, side, LANES), jnp.float32)
    if opening:
        aux[:, :, far_rows] = jnp.zeros((6, 2, side, LANES), jnp.float32)
        mask[...] = jnp.zeros(mask.shape, jnp.float32)
        for q in range(-JACOBI, geo.planes + JACOBI):
            there = jnp.float32(1.0)
            if q < 0:
                there = jnp.where(tile > 0, 1.0, 0.0)
            if q >= geo.planes:
                there = jnp.where(tile < tiles - 1, 1.0, 0.0)
            at = low + q * geo.stride
            mask[at : at + geo.window] = jnp.full((geo.window, LANES), there, jnp.float32)

        def unpack_far(upper, lowest):
            for f, h, cuts, row in geo.mixed():
                place(geo, cuts, upper, lowest, far0_ref, aux.at[f - 4, h] if f >= 4 else field.at[me, f, h], row)
            for k in range(1, n - 1):
                for f in range(4):
                    for h in range(2):
                        cuts = geo.trims(False, JACOBI)[0]
                        place(geo, cuts, upper, lowest, fars[k - 1].at[f, h], field.at[me ^ k, f, h])

        each_place(me, odd, unpack_far)
        for copy in copies[:2]:
            copy.wait()

    steps = Steps(geo, points, table, aux, mask, field, tend, base, first)
    shift = 2 if opening else 0

    def arrive(k, j):
        for i, rows in enumerate((own_rows, near_rows)):
            part = field.at[j, :, :, rows]
            pltpu.make_async_copy(part, part, sems.at[shift + 2 * k + i]).wait()

    if opening:

        def whole(k):
            arrive(k, me ^ k)
            steps.slopes(me ^ k, *geo.span(JACOBI - 1))

        each_node(n - 1, whole)
        arrive(n - 1, me ^ (n - 1))

    def early(upper):
        rows, second = geo.early(upper)
        if opening:
            steps.slopes(me ^ (n - 1), *rows)
        else:

            def part(k):
                arrive(k, k)
                steps.slopes(k, *rows)

            each_node(n, part)
        steps.quadrature(*rows)
        each_node(n, lambda m: steps.relax(first, tend, m, *second))

    by_side(odd, early)


def finish_kernel(geo, opening, points, table, aux, mask, *refs):
    n, stride, low, side = geo.nodes, geo.stride, geo.low, geo.side
    me, odd = lax.axis_index("node"), lax.axis_index("space") % 2
    far_ref = refs[4]
    field, tend, base, first, *outs, sems = refs[5:]
    steps = Steps(geo, points, table, aux, mask, field, tend, base, first)

    def unpack_far(upper, lowest):
        cuts = geo.trims(not opening, JACOBI)[0]
        for f in range(4):
            for h in range(2):
                if opening:
                    place(geo, cuts, upper, lowest, far_ref.at[f, h], field.at[me ^ (n - 1), f, h])
                else:
                    for k in range(n):
                        place(geo, cuts, upper, lowest, far_ref.at[k, f, h], field.at[k, f, h])

    each_place(me, odd, unpack_far)

    def late(upper):
        rows, second = geo.late(upper)
        if opening:
            steps.slopes(me ^ (n - 1), *rows)
        else:
            each_node(n, lambda j: steps.slopes(j, *rows))
        steps.quadrature(*rows)
        each_node(n, lambda m: steps.relax(first, tend, m, *second))

    by_side(odd, late)

    if opening:
        out_ref, near_out, far_out = outs
        near_row = send_rows(geo, odd)[0]

        def results(m):
            copies = []
            for i, (row, count, ref) in enumerate(((near_row, side, near_out), (0, geo.rows, out_ref))):
                part = first.at[m, :, :, pl.ds(pl.multiple_of(low + row, 8), count)]
                copies.append(pltpu.make_async_copy(part, ref.at[m], sems.at[2 * m + i]))
            return copies

        def third(m):
            steps.relax(tend, first, m, *geo.span(0))
            for copy in results(m):
                copy.start()

            def pack_far(upper, lowest):
                for f in range(4):
                    for h in range(2):
                        cuts = geo.trims(True, JACOBI)[0]
                        trim(geo, cuts, upper, lowest, first.at[m, f, h], low, far_out.at[m, f, h])

            each_place(me, odd, pack_far)

        each_node(n, third)
        for m in range(n):
            for copy in results(m):
                copy.wait()
        return

    done = pl.ds(0, geo.planes * geo.back)
    for start in sorted({a - b for a, b in zip(geo.first, geo.offset)}):
        hit = [p for p in range(n) if geo.first[p] - geo.offset[p] == start]
        chosen = functools.reduce(jnp.logical_or, [me == p for p in hit])

        @pl.when(chosen)
        def _():
            def third(i):
                k = n - 1 - i
                m = me ^ k
                weight = steps.weights(m)
                for x in range(geo.planes):
                    for o in [*range(0, geo.back - 8, 8), geo.back - 8]:
                        for f in range(4):
                            r = low + x * stride + start + o
                            steps.relax_rows(tend, first, m, f, r, weight[f], x * geo.back + o)
                for other in range(n):

                    @pl.when(k == other)
                    def _():
                        pltpu.make_async_copy(first.at[m, :, :, done], outs[other], sems.at[other]).start()

            each_node(n, third)

    for k in range(n):
        pltpu.make_async_copy(first.at[me ^ k, :, :, done], outs[k], sems.at[k]).wait()


def unpack_kernel(geo, *refs):
    ins, (out_ref, pieces, sems) = refs[: geo.nodes], refs[geo.nodes :]
    me = lax.axis_index("node")
    copy_all([(ins[k], pieces.at[me ^ k]) for k in range(geo.nodes)], sems)
    for p in range(geo.nodes):
        for f in range(4):
            for x in range(geo.planes):
                for h in range(2):
                    at = x * geo.back
                    out_ref[0, f, x, geo.first[p] : geo.first[p] + geo.count[p], h * LANES : (h + 1) * LANES] = pieces[
                        p, f, h, at : at + geo.count[p]
                    ]


def on_device(start, guess, heat_mask, solid_mask):
    n = lax.axis_size("node")
    tiles = lax.axis_size("space")
    planes, depth, width = guess.shape[2:]
    assert width == 2 * LANES and tiles % 2 == 0 and n & (n - 1) == 0
    geo = Geometry(n, planes, depth)
    points_list, table_list = radau_tables(n)
    table = [[float(np.float32(v)) for v in row] for row in table_list]
    points = [float(np.float32(v)) for v in points_list]
    f32 = jnp.float32
    vmem, free = pl.BlockSpec(memory_space=pltpu.VMEM), pl.BlockSpec(memory_space=pl.ANY)

    def call(kernel, name, outs, out_specs, ins, in_specs, scratch, copies, aliases={}):
        held = list(scratch)
        semaphores = [pltpu.SemaphoreType.DMA((copies,))] if copies else []
        return pl.pallas_call(
            kernel, name=name,
            out_shape=[jax.ShapeDtypeStruct(shape, f32) for shape in outs], in_specs=in_specs, out_specs=out_specs,
            input_output_aliases=aliases,
            scratch_shapes=[a if hasattr(a, "memory_space") else pltpu.VMEM(a, f32) for a in scratch] + semaphores,
            compiler_params=pltpu.CompilerParams(vmem_limit_bytes=VMEM_SLACK + 4 * sum(map(size_of, held))),
        )(*ins)

    def across(k, value):
        return lax.ppermute(value, "node", [(i, i ^ k) for i in range(n)])

    chip = [(i, i ^ 1) for i in range(tiles)]
    links = [(i, i + 1) for i in range(1, tiles - 1, 2)] + [(i + 1, i) for i in range(1, tiles - 1, 2)]

    def beside(near, far):
        return lax.ppermute(near, "space", chip), lax.ppermute(far, "space", links)

    piece = (4, 2, geo.rows, LANES)
    sends = call(
        functools.partial(pack_kernel, geo), "pack", [piece] * (n - 1), [free] * (n - 1), (guess,), [vmem],
        [(n,) + piece], n - 1,
    )
    geo.mixed()
    masks = pltpu.VMEM(heat_mask.shape, jnp.int32)
    own, aux, near, far = call(
        functools.partial(pack_own_kernel, geo), "pack_own",
        [piece, (6,) + piece[1:], (10, 2, geo.side, LANES), (geo.mixed_rows, LANES)], [free, free, free, vmem],
        (guess, start, heat_mask, solid_mask), [pl.BlockSpec(memory_space=pltpu.HBM)] * 4,
        [guess.shape, start.shape, masks, masks, (10,) + piece[1:]], 4,
    )
    near0, far0 = beside(near, far)

    owns = {0: own}
    wave = []
    for hops in range(1, n.bit_length()):
        group = [k for k in range(1, n) if k.bit_count() == hops]
        gated = lax.optimization_barrier([sends[k - 1] for k in group] + wave)
        wave = [across(k, value) for k, value in zip(group, gated)]
        owns.update(zip(group, wave))
    pieces, specs = [own], [free]
    for k in range(1, n):
        (far,) = call(
            functools.partial(trim_kernel, geo), "trim", [(4, 2, geo.trims(False, JACOBI)[1], LANES)], [vmem],
            (owns[k],), [vmem], [], 0,
        )
        held, far = lax.optimization_barrier((owns[k], far))
        near, far = beside(held, far)
        pieces += [owns[k], near]
        specs += [free, free]
        if k < n - 1:
            pieces.append(far)
            specs.append(vmem)

    big = (n, 4, 2, geo.total, LANES)
    state, kept = [big] * 4, [(6, 2, geo.total, LANES), (geo.total, LANES)]
    sent = (n, 4, 2, geo.trims(True, JACOBI)[1], LANES)
    aux, mask, *held = call(
        functools.partial(start_kernel, geo, True, tiles, points, table), "opening_start", kept + state, [vmem] * 6,
        (aux, near0, far0, *pieces), [free, free, vmem, *specs], [], 2 + 2 * n,
    )
    aliases = {2 + i: i for i in range(4)}
    own, near, far = call(
        functools.partial(finish_kernel, geo, True, points, table), "opening_finish",
        state + [(n,) + piece, (n, 4, 2, geo.side, LANES), sent], [vmem] * 4 + [free, free, vmem],
        (aux, mask, *held, far), [vmem] * 7, [], 2 * n, aliases,
    )[4:]
    near, far = beside(near, far)
    held = call(
        functools.partial(start_kernel, geo, False, tiles, points, table), "closing_start", state, [vmem] * 4,
        (aux, mask, own, near), [vmem, vmem, free, free], [], 2 * n,
    )
    outs = call(
        functools.partial(finish_kernel, geo, False, points, table), "closing_finish",
        state + [(4, 2, planes * geo.back, LANES)] * n, [vmem] * 4 + [free] * n,
        (aux, mask, *held, far), [vmem] * 7, [], n, aliases,
    )[4:]
    outs = [across(k, outs[k]) if k else outs[k] for k in range(n)]
    (result,) = call(
        functools.partial(unpack_kernel, geo), "unpack", [(1, 4, planes, depth, width)], [vmem], outs, [free] * n,
        [(n, 4, 2, planes * geo.back, LANES)], n,
    )
    return result


def solution(mesh):
    in_specs = (
        P(None, "space", None, None),
        P("node", None, "space", None, None),
        P("space", None, None),
        P("space", None, None),
    )
    out_specs = P("node", None, "space", None, None)
    return jax.shard_map(
        on_device, mesh=mesh, in_specs=in_specs, out_specs=out_specs, check_vma=False
    )
```

time: 99.3 us -> 81.3 us (0.82)
  waiting for transfers between devices: 43.9 us -> 32.2 us
  Pallas kernels: 28.2 us -> 21.4 us
  local copies, waits for them, and re-layouts: 2.68 us -> 5.57 us
  starting transfers between devices: 24 us -> 21.5 us
    ppermute x5, waiting for transfers between devices: 22.4 us -> 10.1 us  [beside(): lax.ppermute(far, 'space', links)]
    pallas_call x5 -> x10, Pallas kernels: 28.2 us -> 21.4 us  [call(): pl.pallas_call(kernel, name=name, out_shape=[jax.ShapeDtypeStruct(shape,...]
    ppermute x5, starting transfers between devices: 5.64 us -> 1.77 us  [beside(): lax.ppermute(near, 'space', chip)]
    unnamed x34 -> x10, local copies, waits for them, and re-layouts: 2.68 us -> 5.57 us
    ppermute x5, starting transfers between devices: 10.2 us -> 11.7 us  [beside(): lax.ppermute(far, 'space', links)]
  transfers between devices with their start and end apart: 16 -> 16, of which waited for: 10 -> 9; matrix products, arithmetic and copies ran while one was open for 0% -> 0% of each run, Pallas kernels for 3% -> 13%
where the time goes in v3:
time: 81.3 us; the launch traced here: 80.9 us
  waiting for transfers between devices  32.2 us (40%)
  starting transfers between devices  21.5 us (26%)
  Pallas kernels  21.4 us (26%)
  local copies, waits for them, and re-layouts  5.57 us (7%)
    ppermute x6, waiting for transfers between devices, across(): return lax.ppermute(value, 'node', [(i, i ^ k) for i in range(n)])  21.4 us
    pallas_call x10, Pallas kernels, call(): pl.pallas_call(kernel, name=name, out_shape=[jax.ShapeDtypeStruct(shape,...  21.4 us
    ppermute x5, starting transfers between devices, beside(): lax.ppermute(far, 'space', links)  11.7 us
    ppermute x5, waiting for transfers between devices, beside(): lax.ppermute(far, 'space', links)  10.1 us
    ppermute x6, starting transfers between devices, across(): return lax.ppermute(value, 'node', [(i, i ^ k) for i in range(n)])  8.12 us
    unnamed x10, local copies, waits for them, and re-layouts  5.57 us
    ppermute x5, starting transfers between devices, beside(): lax.ppermute(near, 'space', chip)  1.77 us
  transfers between devices with their start and end apart: 16, of which 9 were waited for; matrix products, arithmetic and copies ran while one was open for 0% of the time, Pallas kernels for 13%

profile of v3, /device:TPU:8, one launch (start us, length us, event | category | flops | bytes accessed | tf_op | source)
XLA Modules:
  0.0 80.9 jit_solution(17195334940703617798)
XLA Ops:
  0.0 1.2 %copy-done = f32[1,4,4,64,256]{4,3,2,1,0:T(8,128)S(1)} copy-done((f32[1,4,4,64,256]{4,3,2,1,0:T(8,128)S(1)}, f32[1,4,4,64,256]{4,3,2,1,0:T(8,128)}, u32[]{:S(2)}) %copy-start) | copy-done | bytes 1048600
  2.1 1.6 %collective-permute-start.2 = (f32[4,2,104,128]{3,2,1,0:T(8,128)S(1)}, f32[4,2,104,128]{3,2,1,0:T(8,128)S(1)}, u32[]{:S(2)}, u32[]{:S(2)}) collective-permute-start(f32[4,2,104,128]{3,2,1,0:T(8,128)S(1)} %get-tuple-element.44), channel_id=1, source_target_pairs={{0,8},{8,0},{16,24},{24,16},{1,9},{9,1},{17,25},{25,17},{2,10},{10... | collective-permute-start | bytes 1277960 | tf_op jit(solution)/shard_map/ppermute | solution.py:585
  3.7 1.5 %collective-permute-start.5 = (f32[4,2,104,128]{3,2,1,0:T(8,128)S(1)}, f32[4,2,104,128]{3,2,1,0:T(8,128)S(1)}, u32[]{:S(2)}, u32[]{:S(2)}) collective-permute-start(f32[4,2,104,128]{3,2,1,0:T(8,128)S(1)} %get-tuple-element.47), channel_id=1, source_target_pairs={{0,16},{8,24},{16,0},{24,8},{1,17},{9,25},{17,1},{25,9},{2,18},{10... | collective-permute-start | bytes 1277960 | tf_op jit(solution)/shard_map/ppermute | solution.py:585
  5.2 1.2 %copy-done.1 = f32[1,4,4,64,256]{4,3,2,1,0:T(8,128)S(1)} copy-done((f32[1,4,4,64,256]{4,3,2,1,0:T(8,128)S(1)}, f32[1,4,4,64,256]{4,3,2,1,0:T(8,128)}, u32[]{:S(2)}) %copy-start.1) | copy-done | bytes 1048600
  6.4 1.2 %copy-done.2 = f32[4,4,64,256]{3,2,1,0:T(8,128)S(1)} copy-done((f32[4,4,64,256]{3,2,1,0:T(8,128)S(1)}, f32[4,4,64,256]{3,2,1,0:T(8,128)}, u32[]{:S(2)}) %copy-start.2) | copy-done | bytes 1048600
  10.4 1.9 %collective-permute-start.1 = (f32[1152,128]{1,0:T(8,128)S(1)}, f32[1152,128]{1,0:T(8,128)S(1)}, u32[]{:S(2)}, u32[]{:S(2)}) collective-permute-start(f32[1152,128]{1,0:T(8,128)S(1)} %get-tuple-element.40), channel_id=1, source_target_pairs={{1,2},{3,4},{5,6},{2,1},{4,3},{6,5},{9,10},{11,12},{13,14},{10,9},... | collective-permute-start | bytes 1769480 | tf_op jit(solution)/shard_map/ppermute | solution.py:591
  12.3 1.4 %collective-permute-done.2.own_ref.refs_4_ = f32[4,2,104,128]{3,2,1,0:T(8,128)S(1)} collective-permute-done((f32[4,2,104,128]{3,2,1,0:T(8,128)S(1)}, f32[4,2,104,128]{3,2,1,0:T(8,128)S(1)}, u32[]{:S(2)}, u32[]{:S(2)}) %collective-permute-start.2) | collective-permute-done | bytes 426016 | tf_op jit(solution)/shard_map/ppermute | solution.py:585
  13.7 1.2 %collective-permute-done.5.own_ref.refs_7_ = f32[4,2,104,128]{3,2,1,0:T(8,128)S(1)} collective-permute-done((f32[4,2,104,128]{3,2,1,0:T(8,128)S(1)}, f32[4,2,104,128]{3,2,1,0:T(8,128)S(1)}, u32[]{:S(2)}, u32[]{:S(2)}) %collective-permute-start.5) | collective-permute-done | bytes 426016 | tf_op jit(solution)/shard_map/ppermute | solution.py:585
  15.0 1.5 %collective-permute-start.8 = (f32[4,2,104,128]{3,2,1,0:T(8,128)S(1)}, f32[4,2,104,128]{3,2,1,0:T(8,128)S(1)}, u32[]{:S(2)}, u32[]{:S(2)}) collective-permute-start(f32[4,2,104,128]{3,2,1,0:T(8,128)S(1)} %get-tuple-element.51), channel_id=1, source_target_pairs={{0,24},{8,16},{16,8},{24,0},{1,25},{9,17},{17,9},{25,1},{2,26},{10... | collective-permute-start | bytes 1277960 | tf_op jit(solution)/shard_map/ppermute | solution.py:585
  16.5 2.5 %collective-permute-start.4 = (f32[4,2,72,128]{3,2,1,0:T(8,128)S(1)}, f32[4,2,72,128]{3,2,1,0:T(8,128)S(1)}, u32[]{:S(2)}, u32[]{:S(2)}) collective-permute-start(f32[4,2,72,128]{3,2,1,0:T(8,128)S(1)} %trim.3), channel_id=1, source_target_pairs={{1,2},{3,4},{5,6},{2,1},{4,3},{6,5},{9,10},{11,12},{13,14},{10,9},... | collective-permute-start | bytes 884744 | tf_op jit(solution)/shard_map/ppermute | solution.py:591
  19.0 3.1 %collective-permute-start.7 = (f32[4,2,72,128]{3,2,1,0:T(8,128)S(1)}, f32[4,2,72,128]{3,2,1,0:T(8,128)S(1)}, u32[]{:S(2)}, u32[]{:S(2)}) collective-permute-start(f32[4,2,72,128]{3,2,1,0:T(8,128)S(1)} %trim.4), channel_id=1, source_target_pairs={{1,2},{3,4},{5,6},{2,1},{4,3},{6,5},{9,10},{11,12},{13,14},{10,9},... | collective-permute-start | bytes 884744 | tf_op jit(solution)/shard_map/ppermute | solution.py:591
  22.1 4.6 %collective-permute-done.8.own_ref.refs_10_ = f32[4,2,104,128]{3,2,1,0:T(8,128)S(1)} collective-permute-done((f32[4,2,104,128]{3,2,1,0:T(8,128)S(1)}, f32[4,2,104,128]{3,2,1,0:T(8,128)S(1)}, u32[]{:S(2)}, u32[]{:S(2)}) %collective-permute-start.8) | collective-permute-done | bytes 426016 | tf_op jit(solution)/shard_map/ppermute | solution.py:585
  27.9 2.2 %collective-permute-start.10 = (f32[4,2,72,128]{3,2,1,0:T(8,128)S(1)}, f32[4,2,72,128]{3,2,1,0:T(8,128)S(1)}, u32[]{:S(2)}, u32[]{:S(2)}) collective-permute-start(f32[4,2,72,128]{3,2,1,0:T(8,128)S(1)} %trim.5), channel_id=1, source_target_pairs={{1,2},{3,4},{5,6},{2,1},{4,3},{6,5},{9,10},{11,12},{13,14},{10,9},... | collective-permute-start | bytes 884744 | tf_op jit(solution)/shard_map/ppermute | solution.py:591
  30.2 5.4 %opening_start.1 = (f32[6,2,280,128]{3,2,1,0:T(8,128)S(1)}, f32[280,128]{1,0:T(8,128)S(1)}, f32[4,4,2,280,128]{4,3,2,1,0:T(8,128)S(1)}, f32[4,4,2,280,128]{4,3,2...) custom-call(f32[6,2,104,128]{3,2,1,0:T(8,128)S(1)} %get-tuple-element.38.refs_0_, ...), custom_call_target="tpu_custom_call" | custom-call | tf_op jit(solution)/shard_map/opening_start/pallas_call | solution.py:576
  36.0 3.9 %opening_finish.1 = (f32[4,4,2,280,128]{4,3,2,1,0:T(8,128)S(1)}, f32[4,4,2,280,128]{4,3,2,1,0:T(8,128)S(1)}, f32[4,4,2,280,128]{4,3,2,1,0:T(8,128)S(1)}, f32[4,4...) custom-call(f32[6,2,280,128]{3,2,1,0:T(8,128)S(1)} %get-tuple-elemen, ...), custom_call_target="tpu_custom_call", output_to_operand_aliasing={{0}: (2, {}), {1}: (3, {}), {2}: (4, {}), {3}: (5, {})} | custom-call | tf_op jit(solution)/shard_map/opening_finish/pallas_call | solution.py:576
  41.0 2.0 %collective-permute-start.12 = (f32[4,4,2,64,128]{4,3,2,1,0:T(8,128)S(1)}, f32[4,4,2,64,128]{4,3,2,1,0:T(8,128)S(1)}, u32[]{:S(2)}, u32[]{:S(2)}) collective-permute-start(f32[4,4,2,64,128]{4,3,2,1,0:T(8,128)S(1)} %get-tuple-element.66), channel_id=1, source_target_pairs={{1,2},{3,4},{5,6},{2,1},{4,3},{6,5},{9,10},{11,12},{13,14},{10,9},... | collective-permute-start | bytes 3145736 | tf_op jit(solution)/shard_map/ppermute | solution.py:591
  43.6 4.2 %closing_start.1 = (f32[4,4,2,280,128]{4,3,2,1,0:T(8,128)S(1)}, f32[4,4,2,280,128]{4,3,2,1,0:T(8,128)S(1)}, f32[4,4,2,280,128]{4,3,2,1,0:T(8,128)S(1)}, f32[4,4,2,280,128]{4,3,2,1,0:T(8,128)S(1)}) custom-call(f32[6,2,280,128]{3,2,1,0:T(8,128)S(1)} %get-tuple-element.53.aux.refs_0_, f32[280,128]{1,0:T(8,128)S(1)} %get-tuple-element.54.mask.refs_1_, ...), custom_call_target="tpu_custom_call" | custom-call | tf_op jit(solution)/shard_map/closing_start/pallas_call | solution.py:576
  47.9 9.2 %collective-permute-done.12.refs_4_ = f32[4,4,2,64,128]{4,3,2,1,0:T(8,128)S(1)} collective-permute-done((f32[4,4,2,64,128]{4,3,2,1,0:T(8,128)S(1)}, f32[4,4,2,64,128]{4,3,2,1,0:T(8,128)S(1)}, u32[]{:S(2)}, u32[]{:S(2)}) %collective-permute-start.12) | collective-permute-done | bytes 1048608 | tf_op jit(solution)/shard_map/ppermute | solution.py:591
  57.1 4.5 %closing_finish.1 = (f32[4,4,2,280,128]{4,3,2,1,0:T(8,128)S(1)}, f32[4,4,2,280,128]{4,3,2,1,0:T(8,128)S(1)}, f32[4,4,2,280,128]{4,3,2,1,0:T(8,128)S(1)}, f32[4,4...) custom-call(f32[6,2,280,128]{3,2,1,0:T(8,128)S(1)} %get-tuple-elemen, ...), custom_call_target="tpu_custom_call", output_to_operand_aliasing={{0}: (2, {}), {1}: (3, {}), {2}: (4, {}), {3}: (5, {})} | custom-call | tf_op jit(solution)/shard_map/closing_finish/pallas_call | solution.py:576
  61.6 1.3 %collective-permute-start.13 = (f32[4,2,80,128]{3,2,1,0:T(8,128)S(1)}, f32[4,2,80,128]{3,2,1,0:T(8,128)S(1)}, u32[]{:S(2)}, u32[]{:S(2)}) collective-permute-start(f32[4,2,80,128]{3,2,1,0:T(8,128)S(1)} %get-tuple-element.68), channel_id=1, source_target_pairs={{0,8},{8,0},{16,24},{24,16},{1,9},{9,1},{17,25},{25,17},{2,10},{10... | collective-permute-start | bytes 983048 | tf_op jit(solution)/shard_map/ppermute | solution.py:585
  63.4 1.7 %collective-permute-start.15 = (f32[4,2,80,128]{3,2,1,0:T(8,128)S(1)}, f32[4,2,80,128]{3,2,1,0:T(8,128)S(1)}, u32[]{:S(2)}, u32[]{:S(2)}) collective-permute-start(f32[4,2,80,128]{3,2,1,0:T(8,128)S(1)} %get-tuple-element.70), channel_id=1, source_target_pairs={{0,24},{8,16},{16,8},{24,0},{1,25},{9,17},{17,9},{25,1},{2,26},{10... | collective-permute-start | bytes 983048 | tf_op jit(solution)/shard_map/ppermute | solution.py:585
  65.2 7.1 %collective-permute-done.13.refs_1_ = f32[4,2,80,128]{3,2,1,0:T(8,128)S(1)} collective-permute-done((f32[4,2,80,128]{3,2,1,0:T(8,128)S(1)}, f32[4,2,80,128]{3,2,1,0:T(8,128)S(1)}, u32[]{:S(2)}, u32[]{:S(2)}) %collective-permute-start.13) | collective-permute-done | bytes 327712 | tf_op jit(solution)/shard_map/ppermute | solution.py:585
  72.2 7.1 %collective-permute-done.14.refs_2_ = f32[4,2,80,128]{3,2,1,0:T(8,128)S(1)} collective-permute-done((f32[4,2,80,128]{3,2,1,0:T(8,128)S(1)}, f32[4,2,80,128]{3,2,1,0:T(8,128)S(1)}, u32[]{:S(2)}, u32[]{:S(2)}) %collective-permute-start.14) | collective-permute-done | bytes 327712 | tf_op jit(solution)/shard_map/ppermute | solution.py:585
  79.4 1.5 %unpack.1 = f32[1,4,4,64,256]{4,3,2,1,0:T(8,128)} custom-call(f32[4,2,80,128]{3,2,1,0:T(8,128)S(1)} %get-tuple-element.67.refs_0_, f32[4,2,80,128]{3,2,1,0:T(8,128)S(1)} %collective-permute-done.13.refs_1_, f32[4,2,80,128]{3,2,1,0:T(8,128)S(1)} %collective-permute-done.14.refs_2_, f32[4,2,80,128]{3,2,1,0:T(8,128)S(1)} %collective-permute-done.15.refs_3_), custom_call_target="tpu_custom_call" | custom-call | tf_op jit(solution)/shard_map/unpack/pallas_call | solution.py:576
  (28 shorter events, 7.6 us)
Async XLA Ops:
  0.0 1.2 %copy-start = (f32[1,4,4,64,256]{4,3,2,1,0:T(8,128)S(1)}, f32[1,4,4,64,256]{4,3,2,1,0:T(8,128)}, u32[]{:S(2)}) copy-start(f32[1,4,4,64,256]{4,3,2,1,0:T(8,128)} %guess_ref.1) | copy-start | bytes 3145732
  2.1 11.6 %collective-permute-start.2 = (f32[4,2,104,128]{3,2,1,0:T(8,128)S(1)}, f32[4,2,104,128]{3,2,1,0:T(8,128)S(1)}, u32[]{:S(2)}, u32[]{:S(2)}) collective-permute-start(f32[4,2,104,128]{3,2,1,0:T(8,128)S(1)} %get-tuple-element.44), channel_id=1, source_target_pairs={{0,8},{8,0},{16,24},{24,16},{1,9},{9,1},{17,25},{25,17},{2,10},{10... | collective-permute-start | bytes 1277960 | tf_op jit(solution)/shard_map/ppermute | solution.py:585
  3.7 11.3 %collective-permute-start.5 = (f32[4,2,104,128]{3,2,1,0:T(8,128)S(1)}, f32[4,2,104,128]{3,2,1,0:T(8,128)S(1)}, u32[]{:S(2)}, u32[]{:S(2)}) collective-permute-start(f32[4,2,104,128]{3,2,1,0:T(8,128)S(1)} %get-tuple-element.47), channel_id=1, source_target_pairs={{0,16},{8,24},{16,0},{24,8},{1,17},{9,25},{17,1},{25,9},{2,18},{10... | collective-permute-start | bytes 1277960 | tf_op jit(solution)/shard_map/ppermute | solution.py:585
  5.2 1.2 %copy-start.1 = (f32[1,4,4,64,256]{4,3,2,1,0:T(8,128)S(1)}, f32[1,4,4,64,256]{4,3,2,1,0:T(8,128)}, u32[]{:S(2)}) copy-start(f32[1,4,4,64,256]{4,3,2,1,0:T(8,128)} %guess_ref.1) | copy-start | bytes 3145732
  6.4 1.2 %copy-start.2 = (f32[4,4,64,256]{3,2,1,0:T(8,128)S(1)}, f32[4,4,64,256]{3,2,1,0:T(8,128)}, u32[]{:S(2)}) copy-start(f32[4,4,64,256]{3,2,1,0:T(8,128)} %start_hbm.1) | copy-start | bytes 3145732
  7.6 0.9 %copy-start.3 = (s32[4,64,256]{2,1,0:T(8,128)S(1)}, s32[4,64,256]{2,1,0:T(8,128)}, u32[]{:S(2)}) copy-start(s32[4,64,256]{2,1,0:T(8,128)} %heat_hbm.1) | copy-start | bytes 786436
  8.6 0.9 %copy-start.4 = (s32[4,64,256]{2,1,0:T(8,128)S(1)}, s32[4,64,256]{2,1,0:T(8,128)}, u32[]{:S(2)}) copy-start(s32[4,64,256]{2,1,0:T(8,128)} %solid_hbm.1) | copy-start | bytes 786436
  10.4 16.4 %collective-permute-start.1 = (f32[1152,128]{1,0:T(8,128)S(1)}, f32[1152,128]{1,0:T(8,128)S(1)}, u32[]{:S(2)}, u32[]{:S(2)}) collective-permute-start(f32[1152,128]{1,0:T(8,128)S(1)} %get-tuple-element.40), channel_id=1, source_target_pairs={{1,2},{3,4},{5,6},{2,1},{4,3},{6,5},{9,10},{11,12},{13,14},{10,9},... | collective-permute-start | bytes 1769480 | tf_op jit(solution)/shard_map/ppermute | solution.py:591
  15.0 11.8 %collective-permute-start.8 = (f32[4,2,104,128]{3,2,1,0:T(8,128)S(1)}, f32[4,2,104,128]{3,2,1,0:T(8,128)S(1)}, u32[]{:S(2)}, u32[]{:S(2)}) collective-permute-start(f32[4,2,104,128]{3,2,1,0:T(8,128)S(1)} %get-tuple-element.51), channel_id=1, source_target_pairs={{0,24},{8,16},{16,8},{24,0},{1,25},{9,17},{17,9},{25,1},{2,26},{10... | collective-permute-start | bytes 1277960 | tf_op jit(solution)/shard_map/ppermute | solution.py:585
  16.4 13.7 %collective-permute-start = (f32[10,2,80,128]{3,2,1,0:T(8,128)S(1)}, f32[10,2,80,128]{3,2,1,0:T(8,128)S(1)}, u32[]{:S(2)}, u32[]{:S(2)}) collective-permute-start(f32[10,2,80,128]{3,2,1,0:T(8,128)S(1)} %get-tuple-element.39), channel_id=1, source_target_pairs={{0,1},{1,0},{2,3},{3,2},{4,5},{5,4},{6,7},{7,6},{8,9},{9,8},{10,11... | collective-permute-start | bytes 2457608 | tf_op jit(solution)/shard_map/ppermute | solution.py:591
  16.5 10.9 %collective-permute-start.4 = (f32[4,2,72,128]{3,2,1,0:T(8,128)S(1)}, f32[4,2,72,128]{3,2,1,0:T(8,128)S(1)}, u32[]{:S(2)}, u32[]{:S(2)}) collective-permute-start(f32[4,2,72,128]{3,2,1,0:T(8,128)S(1)} %trim.3), channel_id=1, source_target_pairs={{1,2},{3,4},{5,6},{2,1},{4,3},{6,5},{9,10},{11,12},{13,14},{10,9},... | collective-permute-start | bytes 884744 | tf_op jit(solution)/shard_map/ppermute | solution.py:591
  19.0 8.9 %collective-permute-start.7 = (f32[4,2,72,128]{3,2,1,0:T(8,128)S(1)}, f32[4,2,72,128]{3,2,1,0:T(8,128)S(1)}, u32[]{:S(2)}, u32[]{:S(2)}) collective-permute-start(f32[4,2,72,128]{3,2,1,0:T(8,128)S(1)} %trim.4), channel_id=1, source_target_pairs={{1,2},{3,4},{5,6},{2,1},{4,3},{6,5},{9,10},{11,12},{13,14},{10,9},... | collective-permute-start | bytes 884744 | tf_op jit(solution)/shard_map/ppermute | solution.py:591
  26.7 3.4 %collective-permute-start.3 = (f32[4,2,104,128]{3,2,1,0:T(8,128)S(1)}, f32[4,2,104,128]{3,2,1,0:T(8,128)S(1)}, u32[]{:S(2)}, u32[]{:S(2)}) collective-permute-start(f32[4,2,104,128]{3,2,1,0:T(8,128)S(1)} %collective-permute-done.2.own_ref.refs_4_), channel_id=1, source_target_pairs={{0,1},{1,0},{2,3},{3,2},{4,5},{5,4},{6,7},{7,6},{8,9},{9,8},{10,11... | collective-permute-start | bytes 1277960 | tf_op jit(solution)/shard_map/ppermute | solution.py:591
  26.8 3.4 %collective-permute-start.6 = (f32[4,2,104,128]{3,2,1,0:T(8,128)S(1)}, f32[4,2,104,128]{3,2,1,0:T(8,128)S(1)}, u32[]{:S(2)}, u32[]{:S(2)}) collective-permute-start(f32[4,2,104,128]{3,2,1,0:T(8,128)S(1)} %collective-permute-done.5.own_ref.refs_7_), channel_id=1, source_target_pairs={{0,1},{1,0},{2,3},{3,2},{4,5},{5,4},{6,7},{7,6},{8,9},{9,8},{10,11... | collective-permute-start | bytes 1277960 | tf_op jit(solution)/shard_map/ppermute | solution.py:591
  27.4 2.8 %collective-permute-start.9 = (f32[4,2,104,128]{3,2,1,0:T(8,128)S(1)}, f32[4,2,104,128]{3,2,1,0:T(8,128)S(1)}, u32[]{:S(2)}, u32[]{:S(2)}) collective-permute-start(f32[4,2,104,128]{3,2,1,0:T(8,128)S(1)} %collective-permute-done.8.own_ref.refs_10_), channel_id=1, source_target_pairs={{0,1},{1,0},{2,3},{3,2},{4,5},{5,4},{6,7},{7,6},{8,9},{9,8},{10,11... | collective-permute-start | bytes 1277960 | tf_op jit(solution)/shard_map/ppermute | solution.py:591
  27.9 8.0 %collective-permute-start.10 = (f32[4,2,72,128]{3,2,1,0:T(8,128)S(1)}, f32[4,2,72,128]{3,2,1,0:T(8,128)S(1)}, u32[]{:S(2)}, u32[]{:S(2)}) collective-permute-start(f32[4,2,72,128]{3,2,1,0:T(8,128)S(1)} %trim.5), channel_id=1, source_target_pairs={{1,2},{3,4},{5,6},{2,1},{4,3},{6,5},{9,10},{11,12},{13,14},{10,9},... | collective-permute-start | bytes 884744 | tf_op jit(solution)/shard_map/ppermute | solution.py:591
  39.8 3.8 %collective-permute-start.11 = (f32[4,4,2,80,128]{4,3,2,1,0:T(8,128)S(1)}, f32[4,4,2,80,128]{4,3,2,1,0:T(8,128)S(1)}, u32[]{:S(2)}, u32[]{:S(2)}) collective-permute-start(f32[4,4,2,80,128]{4,3,2,1,0:T(8,128)S(1)} %get-tuple-element.61), channel_id=1, source_target_pairs={{0,1},{1,0},{2,3},{3,2},{4,5},{5,4},{6,7},{7,6},{8,9},{9,8},{10,11... | collective-permute-start | bytes 3932168 | tf_op jit(solution)/shard_map/ppermute | solution.py:591
  41.0 16.1 %collective-permute-start.12 = (f32[4,4,2,64,128]{4,3,2,1,0:T(8,128)S(1)}, f32[4,4,2,64,128]{4,3,2,1,0:T(8,128)S(1)}, u32[]{:S(2)}, u32[]{:S(2)}) collective-permute-start(f32[4,4,2,64,128]{4,3,2,1,0:T(8,128)S(1)} %get-tuple-element.66), channel_id=1, source_target_pairs={{1,2},{3,4},{5,6},{2,1},{4,3},{6,5},{9,10},{11,12},{13,14},{10,9},... | collective-permute-start | bytes 3145736 | tf_op jit(solution)/shard_map/ppermute | solution.py:591
  61.6 10.6 %collective-permute-start.13 = (f32[4,2,80,128]{3,2,1,0:T(8,128)S(1)}, f32[4,2,80,128]{3,2,1,0:T(8,128)S(1)}, u32[]{:S(2)}, u32[]{:S(2)}) collective-permute-start(f32[4,2,80,128]{3,2,1,0:T(8,128)S(1)} %get-tuple-element.68), channel_id=1, source_target_pairs={{0,8},{8,0},{16,24},{24,16},{1,9},{9,1},{17,25},{25,17},{2,10},{10... | collective-permute-start | bytes 983048 | tf_op jit(solution)/shard_map/ppermute | solution.py:585
  62.9 16.5 %collective-permute-start.14 = (f32[4,2,80,128]{3,2,1,0:T(8,128)S(1)}, f32[4,2,80,128]{3,2,1,0:T(8,128)S(1)}, u32[]{:S(2)}, u32[]{:S(2)}) collective-permute-start(f32[4,2,80,128]{3,2,1,0:T(8,128)S(1)} %get-tuple-element.69), channel_id=1, source_target_pairs={{0,16},{8,24},{16,0},{24,8},{1,17},{9,25},{17,1},{25,9},{2,18},{10... | collective-permute-start | bytes 983048 | tf_op jit(solution)/shard_map/ppermute | solution.py:585
  63.4 16.0 %collective-permute-start.15 = (f32[4,2,80,128]{3,2,1,0:T(8,128)S(1)}, f32[4,2,80,128]{3,2,1,0:T(8,128)S(1)}, u32[]{:S(2)}, u32[]{:S(2)}) collective-permute-start(f32[4,2,80,128]{3,2,1,0:T(8,128)S(1)} %get-tuple-element.70), channel_id=1, source_target_pairs={{0,24},{8,16},{16,8},{24,0},{1,25},{9,17},{17,9},{25,1},{2,26},{10... | collective-permute-start | bytes 983048 | tf_op jit(solution)/shard_map/ppermute | solution.py:585

commit v4 on v3

--- a/solution.py
+++ b/solution.py
@@ -116,7 +116,7 @@
             cut = closing * JACOBI + d
             cuts.append((d, cut, packed, self.window - cut))
             packed += self.window - cut
-        return cuts, round_up(packed, 8)
+        return cuts, packed
 
     def mixed(self):
         row, parts = 0, []
@@ -125,8 +125,12 @@
             for h in range(2):
                 parts.append((f, h, cuts, row))
                 row += count
-        self.mixed_rows = row
+        self.mixed_rows = round_up(row, 8)
         return parts
+
+    def fields(self, closing):
+        cuts, count = self.trims(closing, JACOBI)
+        return [(f, h, cuts, (2 * f + h) * count) for f in range(4) for h in range(2)], round_up(8 * count, 8)
 
     def span(self, reach):
         begin = (self.low - reach * self.stride) // 8 * 8
@@ -203,9 +207,8 @@
 
 def trim_kernel(geo, own_ref, far_ref):
     def body(upper, lowest):
-        for f in range(4):
-            for h in range(2):
-                trim(geo, geo.trims(False, JACOBI)[0], upper, lowest, own_ref.at[f, h], 0, far_ref.at[f, h])
+        for f, h, cuts, row in geo.fields(False)[0]:
+            trim(geo, cuts, upper, lowest, own_ref.at[f, h], 0, far_ref, row)
 
     each_place(lax.axis_index("node"), lax.axis_index("space") % 2, body)
 
@@ -413,10 +416,8 @@
             for f, h, cuts, row in geo.mixed():
                 place(geo, cuts, upper, lowest, far0_ref, aux.at[f - 4, h] if f >= 4 else field.at[me, f, h], row)
             for k in range(1, n - 1):
-                for f in range(4):
-                    for h in range(2):
-                        cuts = geo.trims(False, JACOBI)[0]
-                        place(geo, cuts, upper, lowest, fars[k - 1].at[f, h], field.at[me ^ k, f, h])
+                for f, h, cuts, row in geo.fields(False)[0]:
+                    place(geo, cuts, upper, lowest, fars[k - 1], field.at[me ^ k, f, h], row)
 
         each_place(me, odd, unpack_far)
         for copy in copies[:2]:
@@ -464,14 +465,12 @@
     steps = Steps(geo, points, table, aux, mask, field, tend, base, first)
 
     def unpack_far(upper, lowest):
-        cuts = geo.trims(not opening, JACOBI)[0]
-        for f in range(4):
-            for h in range(2):
-                if opening:
-                    place(geo, cuts, upper, lowest, far_ref.at[f, h], field.at[me ^ (n - 1), f, h])
-                else:
-                    for k in range(n):
-                        place(geo, cuts, upper, lowest, far_ref.at[k, f, h], field.at[k, f, h])
+        for f, h, cuts, row in geo.fields(not opening)[0]:
+            if opening:
+                place(geo, cuts, upper, lowest, far_ref, field.at[me ^ (n - 1), f, h], row)
+            else:
+                for k in range(n):
+                    place(geo, cuts, upper, lowest, far_ref.at[k], field.at[k, f, h], row)
 
     each_place(me, odd, unpack_far)
 
@@ -503,10 +502,8 @@
                 copy.start()
 
             def pack_far(upper, lowest):
-                for f in range(4):
-                    for h in range(2):
-                        cuts = geo.trims(True, JACOBI)[0]
-                        trim(geo, cuts, upper, lowest, first.at[m, f, h], low, far_out.at[m, f, h])
+                for f, h, cuts, row in geo.fields(True)[0]:
+                    trim(geo, cuts, upper, lowest, first.at[m, f, h], low, far_out.at[m], row)
 
             each_place(me, odd, pack_far)
 
@@ -545,17 +542,24 @@
 
 
 def unpack_kernel(geo, *refs):
-    ins, (out_ref, pieces, sems) = refs[: geo.nodes], refs[geo.nodes :]
+    ins, (out_ref, whole, sems) = refs[: geo.nodes], refs[geo.nodes :]
     me = lax.axis_index("node")
-    copy_all([(ins[k], pieces.at[me ^ k]) for k in range(geo.nodes)], sems)
-    for p in range(geo.nodes):
-        for f in range(4):
-            for x in range(geo.planes):
-                for h in range(2):
-                    at = x * geo.back
-                    out_ref[0, f, x, geo.first[p] : geo.first[p] + geo.count[p], h * LANES : (h + 1) * LANES] = pieces[
-                        p, f, h, at : at + geo.count[p]
-                    ]
+    copies = [pltpu.make_async_copy(whole.at[f], out_ref.at[0, f], sems.at[f]) for f in range(4)]
+    for f in range(4):
+        for k in range(geo.nodes):
+            for p in range(geo.nodes):
+
+                @pl.when(me == p ^ k)
+                def _():
+                    rows = slice(geo.first[p], geo.first[p] + geo.count[p])
+                    for x in range(geo.planes):
+                        for h in range(2):
+                            at = x * geo.back
+                            whole[f, x, rows, h * LANES : (h + 1) * LANES] = ins[k][f, h, at : at + geo.count[p]]
+
+        copies[f].start()
+    for copy in copies:
+        copy.wait()
 
 
 def on_device(start, guess, heat_mask, solid_mask):
@@ -615,10 +619,12 @@
     pieces, specs = [own], [free]
     for k in range(1, n):
         (far,) = call(
-            functools.partial(trim_kernel, geo), "trim", [(4, 2, geo.trims(False, JACOBI)[1], LANES)], [vmem],
+            functools.partial(trim_kernel, geo), "trim", [(geo.fields(False)[1], LANES)], [vmem],
             (owns[k],), [vmem], [], 0,
         )
-        held, far = lax.optimization_barrier((owns[k], far))
+        held = owns[k]
+        if k == n - 1:
+            held, far = lax.optimization_barrier((held, far))
         near, far = beside(held, far)
         pieces += [owns[k], near]
         specs += [free, free]
@@ -628,7 +634,7 @@
 
     big = (n, 4, 2, geo.total, LANES)
     state, kept = [big] * 4, [(6, 2, geo.total, LANES), (geo.total, LANES)]
-    sent = (n, 4, 2, geo.trims(True, JACOBI)[1], LANES)
+    sent = (n, geo.fields(True)[1], LANES)
     aux, mask, *held = call(
         functools.partial(start_kernel, geo, True, tiles, points, table), "opening_start", kept + state, [vmem] * 6,
         (aux, near0, far0, *pieces), [free, free, vmem, *specs], [], 2 + 2 * n,
@@ -651,8 +657,8 @@
     )[4:]
     outs = [across(k, outs[k]) if k else outs[k] for k in range(n)]
     (result,) = call(
-        functools.partial(unpack_kernel, geo), "unpack", [(1, 4, planes, depth, width)], [vmem], outs, [free] * n,
-        [(n, 4, 2, planes * geo.back, LANES)], n,
+        functools.partial(unpack_kernel, geo), "unpack", [(1, 4, planes, depth, width)], [free], outs, [vmem] * n,
+        [(4, planes, depth, width)], 4,
     )
     return result
 

time: 81.3 us -> 79.9 us (0.983)
  waiting for transfers between devices: 32.2 us -> 30.9 us
    ppermute x5, waiting for transfers between devices: 10.1 us -> 8.56 us  [beside(): lax.ppermute(far, 'space', links)]
  transfers between devices with their start and end apart: 16 -> 16, of which waited for: 9 -> 8; matrix products, arithmetic and copies ran while one was open for 0% -> 0% of each run, Pallas kernels for 13% -> 13%
where the time goes in v4:
time: 79.9 us; the launch traced here: 79.5 us
  waiting for transfers between devices  30.9 us (39%)
  starting transfers between devices  21.9 us (27%)
  Pallas kernels  21 us (26%)
  local copies, waits for them, and re-layouts  5.57 us (7%)
    ppermute x6, waiting for transfers between devices, across(): return lax.ppermute(value, 'node', [(i, i ^ k) for i in range(n)])  21.6 us
    pallas_call x10, Pallas kernels, call(): pl.pallas_call(kernel, name=name, out_shape=[jax.ShapeDtypeStruct(shape,...  21 us
    ppermute x5, starting transfers between devices, beside(): lax.ppermute(far, 'space', links)  12 us
    ppermute x5, waiting for transfers between devices, beside(): lax.ppermute(far, 'space', links)  8.56 us
    ppermute x6, starting transfers between devices, across(): return lax.ppermute(value, 'node', [(i, i ^ k) for i in range(n)])  8.12 us
    unnamed x10, local copies, waits for them, and re-layouts  5.57 us
    ppermute x5, starting transfers between devices, beside(): lax.ppermute(near, 'space', chip)  1.8 us
  transfers between devices with their start and end apart: 16, of which 8 were waited for; matrix products, arithmetic and copies ran while one was open for 0% of the time, Pallas kernels for 13%

profile of v4, /device:TPU:8, one launch (start us, length us, event | category | flops | bytes accessed | tf_op | source)
XLA Modules:
  0.0 79.5 jit_solution(14149860878257325110)
XLA Ops:
  0.0 1.2 %copy-done = f32[1,4,4,64,256]{4,3,2,1,0:T(8,128)S(1)} copy-done((f32[1,4,4,64,256]{4,3,2,1,0:T(8,128)S(1)}, f32[1,4,4,64,256]{4,3,2,1,0:T(8,128)}, u32[]{:S(2)}) %copy-start) | copy-done | bytes 1048600
  2.1 1.6 %collective-permute-start.2 = (f32[4,2,104,128]{3,2,1,0:T(8,128)S(1)}, f32[4,2,104,128]{3,2,1,0:T(8,128)S(1)}, u32[]{:S(2)}, u32[]{:S(2)}) collective-permute-start(f32[4,2,104,128]{3,2,1,0:T(8,128)S(1)} %get-tuple-element.40), channel_id=1, source_target_pairs={{0,8},{8,0},{16,24},{24,16},{1,9},{9,1},{17,25},{25,17},{2,10},{10... | collective-permute-start | bytes 1277960 | tf_op jit(solution)/shard_map/ppermute | solution.py:589
  3.7 1.5 %collective-permute-start.5 = (f32[4,2,104,128]{3,2,1,0:T(8,128)S(1)}, f32[4,2,104,128]{3,2,1,0:T(8,128)S(1)}, u32[]{:S(2)}, u32[]{:S(2)}) collective-permute-start(f32[4,2,104,128]{3,2,1,0:T(8,128)S(1)} %get-tuple-element.41), channel_id=1, source_target_pairs={{0,16},{8,24},{16,0},{24,8},{1,17},{9,25},{17,1},{25,9},{2,18},{10... | collective-permute-start | bytes 1277960 | tf_op jit(solution)/shard_map/ppermute | solution.py:589
  5.2 1.2 %copy-done.1 = f32[1,4,4,64,256]{4,3,2,1,0:T(8,128)S(1)} copy-done((f32[1,4,4,64,256]{4,3,2,1,0:T(8,128)S(1)}, f32[1,4,4,64,256]{4,3,2,1,0:T(8,128)}, u32[]{:S(2)}) %copy-start.1) | copy-done | bytes 1048600
  6.4 1.2 %copy-done.2 = f32[4,4,64,256]{3,2,1,0:T(8,128)S(1)} copy-done((f32[4,4,64,256]{3,2,1,0:T(8,128)S(1)}, f32[4,4,64,256]{3,2,1,0:T(8,128)}, u32[]{:S(2)}) %copy-start.2) | copy-done | bytes 1048600
  10.4 1.9 %collective-permute-start.1 = (f32[1120,128]{1,0:T(8,128)S(1)}, f32[1120,128]{1,0:T(8,128)S(1)}, u32[]{:S(2)}, u32[]{:S(2)}) collective-permute-start(f32[1120,128]{1,0:T(8,128)S(1)} %get-tuple-element.36), channel_id=1, source_target_pairs={{1,2},{3,4},{5,6},{2,1},{4,3},{6,5},{9,10},{11,12},{13,14},{10,9},... | collective-permute-start | bytes 1720328 | tf_op jit(solution)/shard_map/ppermute | solution.py:595
  12.3 1.4 %collective-permute-done.2.own_ref.refs_4_ = f32[4,2,104,128]{3,2,1,0:T(8,128)S(1)} collective-permute-done((f32[4,2,104,128]{3,2,1,0:T(8,128)S(1)}, f32[4,2,104,128]{3,2,1,0:T(8,128)S(1)}, u32[]{:S(2)}, u32[]{:S(2)}) %collective-permute-start.2) | collective-permute-done | bytes 426016 | tf_op jit(solution)/shard_map/ppermute | solution.py:589
  13.7 1.2 %collective-permute-done.5.own_ref.refs_7_ = f32[4,2,104,128]{3,2,1,0:T(8,128)S(1)} collective-permute-done((f32[4,2,104,128]{3,2,1,0:T(8,128)S(1)}, f32[4,2,104,128]{3,2,1,0:T(8,128)S(1)}, u32[]{:S(2)}, u32[]{:S(2)}) %collective-permute-start.5) | collective-permute-done | bytes 426016 | tf_op jit(solution)/shard_map/ppermute | solution.py:589
  15.0 1.5 %collective-permute-start.8 = (f32[4,2,104,128]{3,2,1,0:T(8,128)S(1)}, f32[4,2,104,128]{3,2,1,0:T(8,128)S(1)}, u32[]{:S(2)}, u32[]{:S(2)}) collective-permute-start(f32[4,2,104,128]{3,2,1,0:T(8,128)S(1)} %get-tuple-element.43), channel_id=1, source_target_pairs={{0,24},{8,16},{16,8},{24,0},{1,25},{9,17},{17,9},{25,1},{2,26},{10... | collective-permute-start | bytes 1277960 | tf_op jit(solution)/shard_map/ppermute | solution.py:589
  16.5 2.5 %collective-permute-start.4 = (f32[552,128]{1,0:T(8,128)S(1)}, f32[552,128]{1,0:T(8,128)S(1)}, u32[]{:S(2)}, u32[]{:S(2)}) collective-permute-start(f32[552,128]{1,0:T(8,128)S(1)} %trim.3), channel_id=1, source_target_pairs={{1,2},{3,4},{5,6},{2,1},{4,3},{6,5},{9,10},{11,12},{13,14},{10,9},... | collective-permute-start | bytes 847880 | tf_op jit(solution)/shard_map/ppermute | solution.py:595
  19.0 3.1 %collective-permute-start.7 = (f32[552,128]{1,0:T(8,128)S(1)}, f32[552,128]{1,0:T(8,128)S(1)}, u32[]{:S(2)}, u32[]{:S(2)}) collective-permute-start(f32[552,128]{1,0:T(8,128)S(1)} %trim.4), channel_id=1, source_target_pairs={{1,2},{3,4},{5,6},{2,1},{4,3},{6,5},{9,10},{11,12},{13,14},{10,9},... | collective-permute-start | bytes 847880 | tf_op jit(solution)/shard_map/ppermute | solution.py:595
  22.1 4.6 %collective-permute-done.8.own_ref.refs_10_ = f32[4,2,104,128]{3,2,1,0:T(8,128)S(1)} collective-permute-done((f32[4,2,104,128]{3,2,1,0:T(8,128)S(1)}, f32[4,2,104,128]{3,2,1,0:T(8,128)S(1)}, u32[]{:S(2)}, u32[]{:S(2)}) %collective-permute-start.8) | collective-permute-done | bytes 426016 | tf_op jit(solution)/shard_map/ppermute | solution.py:589
  27.5 2.5 %collective-permute-start.10 = (f32[552,128]{1,0:T(8,128)S(1)}, f32[552,128]{1,0:T(8,128)S(1)}, u32[]{:S(2)}, u32[]{:S(2)}) collective-permute-start(f32[552,128]{1,0:T(8,128)S(1)} %trim.5), channel_id=1, source_target_pairs={{1,2},{3,4},{5,6},{2,1},{4,3},{6,5},{9,10},{11,12},{13,14},{10,9},... | collective-permute-start | bytes 847880 | tf_op jit(solution)/shard_map/ppermute | solution.py:595
  30.1 5.4 %opening_start.1 = (f32[6,2,280,128]{3,2,1,0:T(8,128)S(1)}, f32[280,128]{1,0:T(8,128)S(1)}, f32[4,4,2,280,128]{4,3,2,1,0:T(8,128)S(1)}, f32[4,4,2,280,128]{4,3,2...) custom-call(f32[6,2,104,128]{3,2,1,0:T(8,128)S(1)} %get-tuple-element.34.refs_0_, ...), custom_call_target="tpu_custom_call" | custom-call | tf_op jit(solution)/shard_map/opening_start/pallas_call | solution.py:580
  35.5 3.9 %opening_finish.1 = (f32[4,4,2,280,128]{4,3,2,1,0:T(8,128)S(1)}, f32[4,4,2,280,128]{4,3,2,1,0:T(8,128)S(1)}, f32[4,4,2,280,128]{4,3,2,1,0:T(8,128)S(1)}, f32[4,4...) custom-call(f32[6,2,280,128]{3,2,1,0:T(8,128)S(1)} %get-tuple-elemen, ...), custom_call_target="tpu_custom_call", output_to_operand_aliasing={{0}: (2, {}), {1}: (3, {}), {2}: (4, {}), {3}: (5, {})} | custom-call | tf_op jit(solution)/shard_map/opening_finish/pallas_call | solution.py:580
  39.4 1.2 %collective-permute-start.11 = (f32[4,4,2,80,128]{4,3,2,1,0:T(8,128)S(1)}, f32[4,4,2,80,128]{4,3,2,1,0:T(8,128)S(1)}, u32[]{:S(2)}, u32[]{:S(2)}) collective-permute-start(f32[4,4,2,80,128]{4,3,2,1,0:T(8,128)S(1)} %get-tuple-element.53), channel_id=1, source_target_pairs={{0,1},{1,0},{2,3},{3,2},{4,5},{5,4},{6,7},{7,6},{8,9},{9,8},{10,11... | collective-permute-start | bytes 3932168 | tf_op jit(solution)/shard_map/ppermute | solution.py:595
  40.6 2.0 %collective-permute-start.12 = (f32[4,480,128]{2,1,0:T(8,128)S(1)}, f32[4,480,128]{2,1,0:T(8,128)S(1)}, u32[]{:S(2)}, u32[]{:S(2)}) collective-permute-start(f32[4,480,128]{2,1,0:T(8,128)S(1)} %get-tuple-element.58), channel_id=1, source_target_pairs={{1,2},{3,4},{5,6},{2,1},{4,3},{6,5},{9,10},{11,12},{13,14},{10,9},... | collective-permute-start | bytes 2949128 | tf_op jit(solution)/shard_map/ppermute | solution.py:595
  43.2 4.2 %closing_start.1 = (f32[4,4,2,280,128]{4,3,2,1,0:T(8,128)S(1)}, f32[4,4,2,280,128]{4,3,2,1,0:T(8,128)S(1)}, f32[4,4,2,280,128]{4,3,2,1,0:T(8,128)S(1)}, f32[4,4,2,280,128]{4,3,2,1,0:T(8,128)S(1)}) custom-call(f32[6,2,280,128]{3,2,1,0:T(8,128)S(1)} %get-tuple-element.45.aux.refs_0_, f32[280,128]{1,0:T(8,128)S(1)} %get-tuple-element.46.mask.refs_1_, ...), custom_call_target="tpu_custom_call" | custom-call | tf_op jit(solution)/shard_map/closing_start/pallas_call | solution.py:580
  47.5 8.5 %collective-permute-done.12.refs_4_ = f32[4,480,128]{2,1,0:T(8,128)S(1)} collective-permute-done((f32[4,480,128]{2,1,0:T(8,128)S(1)}, f32[4,480,128]{2,1,0:T(8,128)S(1)}, u32[]{:S(2)}, u32[]{:S(2)}) %collective-permute-start.12) | collective-permute-done | bytes 983072 | tf_op jit(solution)/shard_map/ppermute | solution.py:595
  56.0 4.5 %closing_finish.1 = (f32[4,4,2,280,128]{4,3,2,1,0:T(8,128)S(1)}, f32[4,4,2,280,128]{4,3,2,1,0:T(8,128)S(1)}, f32[4,4,2,280,128]{4,3,2,1,0:T(8,128)S(1)}, f32[4,4...) custom-call(f32[6,2,280,128]{3,2,1,0:T(8,128)S(1)} %get-tuple-elemen, ...), custom_call_target="tpu_custom_call", output_to_operand_aliasing={{0}: (2, {}), {1}: (3, {}), {2}: (4, {}), {3}: (5, {})} | custom-call | tf_op jit(solution)/shard_map/closing_finish/pallas_call | solution.py:580
  60.5 1.5 %collective-permute-start.13 = (f32[4,2,80,128]{3,2,1,0:T(8,128)S(1)}, f32[4,2,80,128]{3,2,1,0:T(8,128)S(1)}, u32[]{:S(2)}, u32[]{:S(2)}) collective-permute-start(f32[4,2,80,128]{3,2,1,0:T(8,128)S(1)} %get-tuple-element.60), channel_id=1, source_target_pairs={{0,8},{8,0},{16,24},{24,16},{1,9},{9,1},{17,25},{25,17},{2,10},{10... | collective-permute-start | bytes 983048 | tf_op jit(solution)/shard_map/ppermute | solution.py:589
  62.5 1.6 %collective-permute-start.15 = (f32[4,2,80,128]{3,2,1,0:T(8,128)S(1)}, f32[4,2,80,128]{3,2,1,0:T(8,128)S(1)}, u32[]{:S(2)}, u32[]{:S(2)}) collective-permute-start(f32[4,2,80,128]{3,2,1,0:T(8,128)S(1)} %get-tuple-element.62), channel_id=1, source_target_pairs={{0,24},{8,16},{16,8},{24,0},{1,25},{9,17},{17,9},{25,1},{2,26},{10... | collective-permute-start | bytes 983048 | tf_op jit(solution)/shard_map/ppermute | solution.py:589
  64.1 7.1 %collective-permute-done.13.refs_1_ = f32[4,2,80,128]{3,2,1,0:T(8,128)S(1)} collective-permute-done((f32[4,2,80,128]{3,2,1,0:T(8,128)S(1)}, f32[4,2,80,128]{3,2,1,0:T(8,128)S(1)}, u32[]{:S(2)}, u32[]{:S(2)}) %collective-permute-start.13) | collective-permute-done | bytes 327712 | tf_op jit(solution)/shard_map/ppermute | solution.py:589
  71.1 7.3 %collective-permute-done.14.refs_2_ = f32[4,2,80,128]{3,2,1,0:T(8,128)S(1)} collective-permute-done((f32[4,2,80,128]{3,2,1,0:T(8,128)S(1)}, f32[4,2,80,128]{3,2,1,0:T(8,128)S(1)}, u32[]{:S(2)}, u32[]{:S(2)}) %collective-permute-start.14) | collective-permute-done | bytes 327712 | tf_op jit(solution)/shard_map/ppermute | solution.py:589
  (28 shorter events, 6.7 us)
Async XLA Ops:
  0.0 1.2 %copy-start = (f32[1,4,4,64,256]{4,3,2,1,0:T(8,128)S(1)}, f32[1,4,4,64,256]{4,3,2,1,0:T(8,128)}, u32[]{:S(2)}) copy-start(f32[1,4,4,64,256]{4,3,2,1,0:T(8,128)} %guess_ref.1) | copy-start | bytes 3145732
  2.1 11.6 %collective-permute-start.2 = (f32[4,2,104,128]{3,2,1,0:T(8,128)S(1)}, f32[4,2,104,128]{3,2,1,0:T(8,128)S(1)}, u32[]{:S(2)}, u32[]{:S(2)}) collective-permute-start(f32[4,2,104,128]{3,2,1,0:T(8,128)S(1)} %get-tuple-element.40), channel_id=1, source_target_pairs={{0,8},{8,0},{16,24},{24,16},{1,9},{9,1},{17,25},{25,17},{2,10},{10... | collective-permute-start | bytes 1277960 | tf_op jit(solution)/shard_map/ppermute | solution.py:589
  3.7 11.3 %collective-permute-start.5 = (f32[4,2,104,128]{3,2,1,0:T(8,128)S(1)}, f32[4,2,104,128]{3,2,1,0:T(8,128)S(1)}, u32[]{:S(2)}, u32[]{:S(2)}) collective-permute-start(f32[4,2,104,128]{3,2,1,0:T(8,128)S(1)} %get-tuple-element.41), channel_id=1, source_target_pairs={{0,16},{8,24},{16,0},{24,8},{1,17},{9,25},{17,1},{25,9},{2,18},{10... | collective-permute-start | bytes 1277960 | tf_op jit(solution)/shard_map/ppermute | solution.py:589
  5.2 1.2 %copy-start.1 = (f32[1,4,4,64,256]{4,3,2,1,0:T(8,128)S(1)}, f32[1,4,4,64,256]{4,3,2,1,0:T(8,128)}, u32[]{:S(2)}) copy-start(f32[1,4,4,64,256]{4,3,2,1,0:T(8,128)} %guess_ref.1) | copy-start | bytes 3145732
  6.4 1.2 %copy-start.2 = (f32[4,4,64,256]{3,2,1,0:T(8,128)S(1)}, f32[4,4,64,256]{3,2,1,0:T(8,128)}, u32[]{:S(2)}) copy-start(f32[4,4,64,256]{3,2,1,0:T(8,128)} %start_hbm.1) | copy-start | bytes 3145732
  7.6 0.9 %copy-start.3 = (s32[4,64,256]{2,1,0:T(8,128)S(1)}, s32[4,64,256]{2,1,0:T(8,128)}, u32[]{:S(2)}) copy-start(s32[4,64,256]{2,1,0:T(8,128)} %heat_hbm.1) | copy-start | bytes 786436
  8.6 0.9 %copy-start.4 = (s32[4,64,256]{2,1,0:T(8,128)S(1)}, s32[4,64,256]{2,1,0:T(8,128)}, u32[]{:S(2)}) copy-start(s32[4,64,256]{2,1,0:T(8,128)} %solid_hbm.1) | copy-start | bytes 786436
  10.4 16.4 %collective-permute-start.1 = (f32[1120,128]{1,0:T(8,128)S(1)}, f32[1120,128]{1,0:T(8,128)S(1)}, u32[]{:S(2)}, u32[]{:S(2)}) collective-permute-start(f32[1120,128]{1,0:T(8,128)S(1)} %get-tuple-element.36), channel_id=1, source_target_pairs={{1,2},{3,4},{5,6},{2,1},{4,3},{6,5},{9,10},{11,12},{13,14},{10,9},... | collective-permute-start | bytes 1720328 | tf_op jit(solution)/shard_map/ppermute | solution.py:595
  15.0 11.8 %collective-permute-start.8 = (f32[4,2,104,128]{3,2,1,0:T(8,128)S(1)}, f32[4,2,104,128]{3,2,1,0:T(8,128)S(1)}, u32[]{:S(2)}, u32[]{:S(2)}) collective-permute-start(f32[4,2,104,128]{3,2,1,0:T(8,128)S(1)} %get-tuple-element.43), channel_id=1, source_target_pairs={{0,24},{8,16},{16,8},{24,0},{1,25},{9,17},{17,9},{25,1},{2,26},{10... | collective-permute-start | bytes 1277960 | tf_op jit(solution)/shard_map/ppermute | solution.py:589
  16.4 13.6 %collective-permute-start = (f32[10,2,80,128]{3,2,1,0:T(8,128)S(1)}, f32[10,2,80,128]{3,2,1,0:T(8,128)S(1)}, u32[]{:S(2)}, u32[]{:S(2)}) collective-permute-start(f32[10,2,80,128]{3,2,1,0:T(8,128)S(1)} %get-tuple-element.35), channel_id=1, source_target_pairs={{0,1},{1,0},{2,3},{3,2},{4,5},{5,4},{6,7},{7,6},{8,9},{9,8},{10,11... | collective-permute-start | bytes 2457608 | tf_op jit(solution)/shard_map/ppermute | solution.py:595
  16.5 10.9 %collective-permute-start.4 = (f32[552,128]{1,0:T(8,128)S(1)}, f32[552,128]{1,0:T(8,128)S(1)}, u32[]{:S(2)}, u32[]{:S(2)}) collective-permute-start(f32[552,128]{1,0:T(8,128)S(1)} %trim.3), channel_id=1, source_target_pairs={{1,2},{3,4},{5,6},{2,1},{4,3},{6,5},{9,10},{11,12},{13,14},{10,9},... | collective-permute-start | bytes 847880 | tf_op jit(solution)/shard_map/ppermute | solution.py:595
  19.0 8.5 %collective-permute-start.7 = (f32[552,128]{1,0:T(8,128)S(1)}, f32[552,128]{1,0:T(8,128)S(1)}, u32[]{:S(2)}, u32[]{:S(2)}) collective-permute-start(f32[552,128]{1,0:T(8,128)S(1)} %trim.4), channel_id=1, source_target_pairs={{1,2},{3,4},{5,6},{2,1},{4,3},{6,5},{9,10},{11,12},{13,14},{10,9},... | collective-permute-start | bytes 847880 | tf_op jit(solution)/shard_map/ppermute | solution.py:595
  26.7 3.3 %collective-permute-start.3 = (f32[4,2,104,128]{3,2,1,0:T(8,128)S(1)}, f32[4,2,104,128]{3,2,1,0:T(8,128)S(1)}, u32[]{:S(2)}, u32[]{:S(2)}) collective-permute-start(f32[4,2,104,128]{3,2,1,0:T(8,128)S(1)} %collective-permute-done.2.own_ref.refs_4_), channel_id=1, source_target_pairs={{0,1},{1,0},{2,3},{3,2},{4,5},{5,4},{6,7},{7,6},{8,9},{9,8},{10,11... | collective-permute-start | bytes 1277960 | tf_op jit(solution)/shard_map/ppermute | solution.py:595
  26.8 3.3 %collective-permute-start.6 = (f32[4,2,104,128]{3,2,1,0:T(8,128)S(1)}, f32[4,2,104,128]{3,2,1,0:T(8,128)S(1)}, u32[]{:S(2)}, u32[]{:S(2)}) collective-permute-start(f32[4,2,104,128]{3,2,1,0:T(8,128)S(1)} %collective-permute-done.5.own_ref.refs_7_), channel_id=1, source_target_pairs={{0,1},{1,0},{2,3},{3,2},{4,5},{5,4},{6,7},{7,6},{8,9},{9,8},{10,11... | collective-permute-start | bytes 1277960 | tf_op jit(solution)/shard_map/ppermute | solution.py:595
  27.4 2.7 %collective-permute-start.9 = (f32[4,2,104,128]{3,2,1,0:T(8,128)S(1)}, f32[4,2,104,128]{3,2,1,0:T(8,128)S(1)}, u32[]{:S(2)}, u32[]{:S(2)}) collective-permute-start(f32[4,2,104,128]{3,2,1,0:T(8,128)S(1)} %collective-permute-done.8.own_ref.refs_10_), channel_id=1, source_target_pairs={{0,1},{1,0},{2,3},{3,2},{4,5},{5,4},{6,7},{7,6},{8,9},{9,8},{10,11... | collective-permute-start | bytes 1277960 | tf_op jit(solution)/shard_map/ppermute | solution.py:595
  27.5 8.0 %collective-permute-start.10 = (f32[552,128]{1,0:T(8,128)S(1)}, f32[552,128]{1,0:T(8,128)S(1)}, u32[]{:S(2)}, u32[]{:S(2)}) collective-permute-start(f32[552,128]{1,0:T(8,128)S(1)} %trim.5), channel_id=1, source_target_pairs={{1,2},{3,4},{5,6},{2,1},{4,3},{6,5},{9,10},{11,12},{13,14},{10,9},... | collective-permute-start | bytes 847880 | tf_op jit(solution)/shard_map/ppermute | solution.py:595
  39.4 3.8 %collective-permute-start.11 = (f32[4,4,2,80,128]{4,3,2,1,0:T(8,128)S(1)}, f32[4,4,2,80,128]{4,3,2,1,0:T(8,128)S(1)}, u32[]{:S(2)}, u32[]{:S(2)}) collective-permute-start(f32[4,4,2,80,128]{4,3,2,1,0:T(8,128)S(1)} %get-tuple-element.53), channel_id=1, source_target_pairs={{0,1},{1,0},{2,3},{3,2},{4,5},{5,4},{6,7},{7,6},{8,9},{9,8},{10,11... | collective-permute-start | bytes 3932168 | tf_op jit(solution)/shard_map/ppermute | solution.py:595
  40.6 15.4 %collective-permute-start.12 = (f32[4,480,128]{2,1,0:T(8,128)S(1)}, f32[4,480,128]{2,1,0:T(8,128)S(1)}, u32[]{:S(2)}, u32[]{:S(2)}) collective-permute-start(f32[4,480,128]{2,1,0:T(8,128)S(1)} %get-tuple-element.58), channel_id=1, source_target_pairs={{1,2},{3,4},{5,6},{2,1},{4,3},{6,5},{9,10},{11,12},{13,14},{10,9},... | collective-permute-start | bytes 2949128 | tf_op jit(solution)/shard_map/ppermute | solution.py:595
  60.5 10.6 %collective-permute-start.13 = (f32[4,2,80,128]{3,2,1,0:T(8,128)S(1)}, f32[4,2,80,128]{3,2,1,0:T(8,128)S(1)}, u32[]{:S(2)}, u32[]{:S(2)}) collective-permute-start(f32[4,2,80,128]{3,2,1,0:T(8,128)S(1)} %get-tuple-element.60), channel_id=1, source_target_pairs={{0,8},{8,0},{16,24},{24,16},{1,9},{9,1},{17,25},{25,17},{2,10},{10... | collective-permute-start | bytes 983048 | tf_op jit(solution)/shard_map/ppermute | solution.py:589
  62.0 16.5 %collective-permute-start.14 = (f32[4,2,80,128]{3,2,1,0:T(8,128)S(1)}, f32[4,2,80,128]{3,2,1,0:T(8,128)S(1)}, u32[]{:S(2)}, u32[]{:S(2)}) collective-permute-start(f32[4,2,80,128]{3,2,1,0:T(8,128)S(1)} %get-tuple-element.61), channel_id=1, source_target_pairs={{0,16},{8,24},{16,0},{24,8},{1,17},{9,25},{17,1},{25,9},{2,18},{10... | collective-permute-start | bytes 983048 | tf_op jit(solution)/shard_map/ppermute | solution.py:589
  62.5 16.0 %collective-permute-start.15 = (f32[4,2,80,128]{3,2,1,0:T(8,128)S(1)}, f32[4,2,80,128]{3,2,1,0:T(8,128)S(1)}, u32[]{:S(2)}, u32[]{:S(2)}) collective-permute-start(f32[4,2,80,128]{3,2,1,0:T(8,128)S(1)} %get-tuple-element.62), channel_id=1, source_target_pairs={{0,24},{8,16},{16,8},{24,0},{1,25},{9,17},{17,9},{25,1},{2,26},{10... | collective-permute-start | bytes 983048 | tf_op jit(solution)/shard_map/ppermute | solution.py:589

commit v5 on v4

--- a/solution.py
+++ b/solution.py
@@ -347,14 +347,14 @@
                 + (source[m, f, h, pl.ds(r + 1, 8)] + source[m, f, h, pl.ds(r - 1, 8)])
                 + (plus[h] + minus[h])
             )
-            target[m, f, h, pl.ds(to, 8)] = self.base[m, f, h, pl.ds(r, 8)] + weight * near
+            target[f, h, pl.ds(to, 8)] = self.base[m, f, h, pl.ds(r, 8)] + weight * near
 
     def relax(self, source, target, m, begin, end):
         weight = self.weights(m)
         for r in range(begin, end, 8):
             inside = self.mask[pl.ds(r, 8)]
             for f in range(4):
-                self.relax_rows(source, target, m, f, r, inside * weight[f], r)
+                self.relax_rows(source, target.at[m], m, f, r, inside * weight[f], r)
 
 
 def each_node(count, body):
@@ -461,7 +461,7 @@
     n, stride, low, side = geo.nodes, geo.stride, geo.low, geo.side
     me, odd = lax.axis_index("node"), lax.axis_index("space") % 2
     far_ref = refs[4]
-    field, tend, base, first, *outs, sems = refs[5:]
+    field, tend, base, first, *outs = refs[5:]
     steps = Steps(geo, points, table, aux, mask, field, tend, base, first)
 
     def unpack_far(upper, lowest):
@@ -486,7 +486,7 @@
     by_side(odd, late)
 
     if opening:
-        out_ref, near_out, far_out = outs
+        out_ref, near_out, far_out, sems = outs
         near_row = send_rows(geo, odd)[0]
 
         def results(m):
@@ -513,32 +513,20 @@
                 copy.wait()
         return
 
-    done = pl.ds(0, geo.planes * geo.back)
     for start in sorted({a - b for a, b in zip(geo.first, geo.offset)}):
         hit = [p for p in range(n) if geo.first[p] - geo.offset[p] == start]
         chosen = functools.reduce(jnp.logical_or, [me == p for p in hit])
 
         @pl.when(chosen)
         def _():
-            def third(i):
-                k = n - 1 - i
+            for k in range(n):
                 m = me ^ k
                 weight = steps.weights(m)
                 for x in range(geo.planes):
                     for o in [*range(0, geo.back - 8, 8), geo.back - 8]:
                         for f in range(4):
                             r = low + x * stride + start + o
-                            steps.relax_rows(tend, first, m, f, r, weight[f], x * geo.back + o)
-                for other in range(n):
-
-                    @pl.when(k == other)
-                    def _():
-                        pltpu.make_async_copy(first.at[m, :, :, done], outs[other], sems.at[other]).start()
-
-            each_node(n, third)
-
-    for k in range(n):
-        pltpu.make_async_copy(first.at[me ^ k, :, :, done], outs[k], sems.at[k]).wait()
+                            steps.relax_rows(tend, outs[k], m, f, r, weight[f], x * geo.back + o)
 
 
 def unpack_kernel(geo, *refs):
@@ -652,8 +640,8 @@
     )
     outs = call(
         functools.partial(finish_kernel, geo, False, points, table), "closing_finish",
-        state + [(4, 2, planes * geo.back, LANES)] * n, [vmem] * 4 + [free] * n,
-        (aux, mask, *held, far), [vmem] * 7, [], n, aliases,
+        state + [(4, 2, planes * geo.back, LANES)] * n, [vmem] * (4 + n),
+        (aux, mask, *held, far), [vmem] * 7, [], 0, aliases,
     )[4:]
     outs = [across(k, outs[k]) if k else outs[k] for k in range(n)]
     (result,) = call(

time: 79.9 us -> 79.5 us (level)
  no operation moved by 1% of the time
where the time goes in v5:
time: 79.5 us; the launch traced here: 79.1 us
  waiting for transfers between devices  30.9 us (39%)
  starting transfers between devices  21.9 us (28%)
  Pallas kernels  20.6 us (26%)
  local copies, waits for them, and re-layouts  5.57 us (7%)
    ppermute x6, waiting for transfers between devices, across(): return lax.ppermute(value, 'node', [(i, i ^ k) for i in range(n)])  21.6 us
    pallas_call x10, Pallas kernels, call(): pl.pallas_call(kernel, name=name, out_shape=[jax.ShapeDtypeStruct(shape,...  20.6 us
    ppermute x5, starting transfers between devices, beside(): lax.ppermute(far, 'space', links)  12 us
    ppermute x5, waiting for transfers between devices, beside(): lax.ppermute(far, 'space', links)  8.56 us
    ppermute x6, starting transfers between devices, across(): return lax.ppermute(value, 'node', [(i, i ^ k) for i in range(n)])  8.12 us
    unnamed x10, local copies, waits for them, and re-layouts  5.57 us
    ppermute x5, starting transfers between devices, beside(): lax.ppermute(near, 'space', chip)  1.8 us
  transfers between devices with their start and end apart: 16, of which 8 were waited for; matrix products, arithmetic and copies ran while one was open for 0% of the time, Pallas kernels for 13%

profile of v5, /device:TPU:8, one launch (start us, length us, event | category | flops | bytes accessed | tf_op | source)
XLA Modules:
  0.0 79.1 jit_solution(9717122941214993708)
XLA Ops:
  0.0 1.2 %copy-done = f32[1,4,4,64,256]{4,3,2,1,0:T(8,128)S(1)} copy-done((f32[1,4,4,64,256]{4,3,2,1,0:T(8,128)S(1)}, f32[1,4,4,64,256]{4,3,2,1,0:T(8,128)}, u32[]{:S(2)}) %copy-start) | copy-done | bytes 1048600
  2.1 1.6 %collective-permute-start.2 = (f32[4,2,104,128]{3,2,1,0:T(8,128)S(1)}, f32[4,2,104,128]{3,2,1,0:T(8,128)S(1)}, u32[]{:S(2)}, u32[]{:S(2)}) collective-permute-start(f32[4,2,104,128]{3,2,1,0:T(8,128)S(1)} %get-tuple-element.40), channel_id=1, source_target_pairs={{0,8},{8,0},{16,24},{24,16},{1,9},{9,1},{17,25},{25,17},{2,10},{10... | collective-permute-start | bytes 1277960 | tf_op jit(solution)/shard_map/ppermute | solution.py:577
  3.7 1.5 %collective-permute-start.5 = (f32[4,2,104,128]{3,2,1,0:T(8,128)S(1)}, f32[4,2,104,128]{3,2,1,0:T(8,128)S(1)}, u32[]{:S(2)}, u32[]{:S(2)}) collective-permute-start(f32[4,2,104,128]{3,2,1,0:T(8,128)S(1)} %get-tuple-element.41), channel_id=1, source_target_pairs={{0,16},{8,24},{16,0},{24,8},{1,17},{9,25},{17,1},{25,9},{2,18},{10... | collective-permute-start | bytes 1277960 | tf_op jit(solution)/shard_map/ppermute | solution.py:577
  5.2 1.2 %copy-done.1 = f32[1,4,4,64,256]{4,3,2,1,0:T(8,128)S(1)} copy-done((f32[1,4,4,64,256]{4,3,2,1,0:T(8,128)S(1)}, f32[1,4,4,64,256]{4,3,2,1,0:T(8,128)}, u32[]{:S(2)}) %copy-start.1) | copy-done | bytes 1048600
  6.4 1.2 %copy-done.2 = f32[4,4,64,256]{3,2,1,0:T(8,128)S(1)} copy-done((f32[4,4,64,256]{3,2,1,0:T(8,128)S(1)}, f32[4,4,64,256]{3,2,1,0:T(8,128)}, u32[]{:S(2)}) %copy-start.2) | copy-done | bytes 1048600
  10.4 1.9 %collective-permute-start.1 = (f32[1120,128]{1,0:T(8,128)S(1)}, f32[1120,128]{1,0:T(8,128)S(1)}, u32[]{:S(2)}, u32[]{:S(2)}) collective-permute-start(f32[1120,128]{1,0:T(8,128)S(1)} %get-tuple-element.36), channel_id=1, source_target_pairs={{1,2},{3,4},{5,6},{2,1},{4,3},{6,5},{9,10},{11,12},{13,14},{10,9},... | collective-permute-start | bytes 1720328 | tf_op jit(solution)/shard_map/ppermute | solution.py:583
  12.3 1.4 %collective-permute-done.2.own_ref.refs_4_ = f32[4,2,104,128]{3,2,1,0:T(8,128)S(1)} collective-permute-done((f32[4,2,104,128]{3,2,1,0:T(8,128)S(1)}, f32[4,2,104,128]{3,2,1,0:T(8,128)S(1)}, u32[]{:S(2)}, u32[]{:S(2)}) %collective-permute-start.2) | collective-permute-done | bytes 426016 | tf_op jit(solution)/shard_map/ppermute | solution.py:577
  13.7 1.2 %collective-permute-done.5.own_ref.refs_7_ = f32[4,2,104,128]{3,2,1,0:T(8,128)S(1)} collective-permute-done((f32[4,2,104,128]{3,2,1,0:T(8,128)S(1)}, f32[4,2,104,128]{3,2,1,0:T(8,128)S(1)}, u32[]{:S(2)}, u32[]{:S(2)}) %collective-permute-start.5) | collective-permute-done | bytes 426016 | tf_op jit(solution)/shard_map/ppermute | solution.py:577
  15.0 1.5 %collective-permute-start.8 = (f32[4,2,104,128]{3,2,1,0:T(8,128)S(1)}, f32[4,2,104,128]{3,2,1,0:T(8,128)S(1)}, u32[]{:S(2)}, u32[]{:S(2)}) collective-permute-start(f32[4,2,104,128]{3,2,1,0:T(8,128)S(1)} %get-tuple-element.43), channel_id=1, source_target_pairs={{0,24},{8,16},{16,8},{24,0},{1,25},{9,17},{17,9},{25,1},{2,26},{10... | collective-permute-start | bytes 1277960 | tf_op jit(solution)/shard_map/ppermute | solution.py:577
  16.5 2.5 %collective-permute-start.4 = (f32[552,128]{1,0:T(8,128)S(1)}, f32[552,128]{1,0:T(8,128)S(1)}, u32[]{:S(2)}, u32[]{:S(2)}) collective-permute-start(f32[552,128]{1,0:T(8,128)S(1)} %trim.3), channel_id=1, source_target_pairs={{1,2},{3,4},{5,6},{2,1},{4,3},{6,5},{9,10},{11,12},{13,14},{10,9},... | collective-permute-start | bytes 847880 | tf_op jit(solution)/shard_map/ppermute | solution.py:583
  19.0 3.1 %collective-permute-start.7 = (f32[552,128]{1,0:T(8,128)S(1)}, f32[552,128]{1,0:T(8,128)S(1)}, u32[]{:S(2)}, u32[]{:S(2)}) collective-permute-start(f32[552,128]{1,0:T(8,128)S(1)} %trim.4), channel_id=1, source_target_pairs={{1,2},{3,4},{5,6},{2,1},{4,3},{6,5},{9,10},{11,12},{13,14},{10,9},... | collective-permute-start | bytes 847880 | tf_op jit(solution)/shard_map/ppermute | solution.py:583
  22.1 4.6 %collective-permute-done.8.own_ref.refs_10_ = f32[4,2,104,128]{3,2,1,0:T(8,128)S(1)} collective-permute-done((f32[4,2,104,128]{3,2,1,0:T(8,128)S(1)}, f32[4,2,104,128]{3,2,1,0:T(8,128)S(1)}, u32[]{:S(2)}, u32[]{:S(2)}) %collective-permute-start.8) | collective-permute-done | bytes 426016 | tf_op jit(solution)/shard_map/ppermute | solution.py:577
  27.5 2.5 %collective-permute-start.10 = (f32[552,128]{1,0:T(8,128)S(1)}, f32[552,128]{1,0:T(8,128)S(1)}, u32[]{:S(2)}, u32[]{:S(2)}) collective-permute-start(f32[552,128]{1,0:T(8,128)S(1)} %trim.5), channel_id=1, source_target_pairs={{1,2},{3,4},{5,6},{2,1},{4,3},{6,5},{9,10},{11,12},{13,14},{10,9},... | collective-permute-start | bytes 847880 | tf_op jit(solution)/shard_map/ppermute | solution.py:583
  30.1 5.4 %opening_start.1 = (f32[6,2,280,128]{3,2,1,0:T(8,128)S(1)}, f32[280,128]{1,0:T(8,128)S(1)}, f32[4,4,2,280,128]{4,3,2,1,0:T(8,128)S(1)}, f32[4,4,2,280,128]{4,3,2...) custom-call(f32[6,2,104,128]{3,2,1,0:T(8,128)S(1)} %get-tuple-element.34.refs_0_, ...), custom_call_target="tpu_custom_call" | custom-call | tf_op jit(solution)/shard_map/opening_start/pallas_call | solution.py:568
  35.5 3.9 %opening_finish.1 = (f32[4,4,2,280,128]{4,3,2,1,0:T(8,128)S(1)}, f32[4,4,2,280,128]{4,3,2,1,0:T(8,128)S(1)}, f32[4,4,2,280,128]{4,3,2,1,0:T(8,128)S(1)}, f32[4,4...) custom-call(f32[6,2,280,128]{3,2,1,0:T(8,128)S(1)} %get-tuple-elemen, ...), custom_call_target="tpu_custom_call", output_to_operand_aliasing={{0}: (2, {}), {1}: (3, {}), {2}: (4, {}), {3}: (5, {})} | custom-call | tf_op jit(solution)/shard_map/opening_finish/pallas_call | solution.py:568
  39.4 1.2 %collective-permute-start.11 = (f32[4,4,2,80,128]{4,3,2,1,0:T(8,128)S(1)}, f32[4,4,2,80,128]{4,3,2,1,0:T(8,128)S(1)}, u32[]{:S(2)}, u32[]{:S(2)}) collective-permute-start(f32[4,4,2,80,128]{4,3,2,1,0:T(8,128)S(1)} %get-tuple-element.53), channel_id=1, source_target_pairs={{0,1},{1,0},{2,3},{3,2},{4,5},{5,4},{6,7},{7,6},{8,9},{9,8},{10,11... | collective-permute-start | bytes 3932168 | tf_op jit(solution)/shard_map/ppermute | solution.py:583
  40.6 2.0 %collective-permute-start.12 = (f32[4,480,128]{2,1,0:T(8,128)S(1)}, f32[4,480,128]{2,1,0:T(8,128)S(1)}, u32[]{:S(2)}, u32[]{:S(2)}) collective-permute-start(f32[4,480,128]{2,1,0:T(8,128)S(1)} %get-tuple-element.58), channel_id=1, source_target_pairs={{1,2},{3,4},{5,6},{2,1},{4,3},{6,5},{9,10},{11,12},{13,14},{10,9},... | collective-permute-start | bytes 2949128 | tf_op jit(solution)/shard_map/ppermute | solution.py:583
  43.2 4.2 %closing_start.1 = (f32[4,4,2,280,128]{4,3,2,1,0:T(8,128)S(1)}, f32[4,4,2,280,128]{4,3,2,1,0:T(8,128)S(1)}, f32[4,4,2,280,128]{4,3,2,1,0:T(8,128)S(1)}, f32[4,4,2,280,128]{4,3,2,1,0:T(8,128)S(1)}) custom-call(f32[6,2,280,128]{3,2,1,0:T(8,128)S(1)} %get-tuple-element.45.aux.refs_0_, f32[280,128]{1,0:T(8,128)S(1)} %get-tuple-element.46.mask.refs_1_, ...), custom_call_target="tpu_custom_call" | custom-call | tf_op jit(solution)/shard_map/closing_start/pallas_call | solution.py:568
  47.5 8.5 %collective-permute-done.12.refs_4_ = f32[4,480,128]{2,1,0:T(8,128)S(1)} collective-permute-done((f32[4,480,128]{2,1,0:T(8,128)S(1)}, f32[4,480,128]{2,1,0:T(8,128)S(1)}, u32[]{:S(2)}, u32[]{:S(2)}) %collective-permute-start.12) | collective-permute-done | bytes 983072 | tf_op jit(solution)/shard_map/ppermute | solution.py:583
  56.0 4.1 %closing_finish.1 = (f32[4,4,2,280,128]{4,3,2,1,0:T(8,128)S(1)}, f32[4,4,2,280,128]{4,3,2,1,0:T(8,128)S(1)}, f32[4,4,2,280,128]{4,3,2,1,0:T(8,128)S(1)}, f32[4,4...) custom-call(f32[6,2,280,128]{3,2,1,0:T(8,128)S(1)} %get-tuple-elemen, ...), custom_call_target="tpu_custom_call", output_to_operand_aliasing={{0}: (2, {}), {1}: (3, {}), {2}: (4, {}), {3}: (5, {})} | custom-call | tf_op jit(solution)/shard_map/closing_finish/pallas_call | solution.py:568
  60.1 1.5 %collective-permute-start.13 = (f32[4,2,80,128]{3,2,1,0:T(8,128)S(1)}, f32[4,2,80,128]{3,2,1,0:T(8,128)S(1)}, u32[]{:S(2)}, u32[]{:S(2)}) collective-permute-start(f32[4,2,80,128]{3,2,1,0:T(8,128)S(1)} %get-tuple-element.60), channel_id=1, source_target_pairs={{0,8},{8,0},{16,24},{24,16},{1,9},{9,1},{17,25},{25,17},{2,10},{10... | collective-permute-start | bytes 983048 | tf_op jit(solution)/shard_map/ppermute | solution.py:577
  62.1 1.6 %collective-permute-start.15 = (f32[4,2,80,128]{3,2,1,0:T(8,128)S(1)}, f32[4,2,80,128]{3,2,1,0:T(8,128)S(1)}, u32[]{:S(2)}, u32[]{:S(2)}) collective-permute-start(f32[4,2,80,128]{3,2,1,0:T(8,128)S(1)} %get-tuple-element.62), channel_id=1, source_target_pairs={{0,24},{8,16},{16,8},{24,0},{1,25},{9,17},{17,9},{25,1},{2,26},{10... | collective-permute-start | bytes 983048 | tf_op jit(solution)/shard_map/ppermute | solution.py:577
  63.6 7.1 %collective-permute-done.13.refs_1_ = f32[4,2,80,128]{3,2,1,0:T(8,128)S(1)} collective-permute-done((f32[4,2,80,128]{3,2,1,0:T(8,128)S(1)}, f32[4,2,80,128]{3,2,1,0:T(8,128)S(1)}, u32[]{:S(2)}, u32[]{:S(2)}) %collective-permute-start.13) | collective-permute-done | bytes 327712 | tf_op jit(solution)/shard_map/ppermute | solution.py:577
  70.7 7.3 %collective-permute-done.14.refs_2_ = f32[4,2,80,128]{3,2,1,0:T(8,128)S(1)} collective-permute-done((f32[4,2,80,128]{3,2,1,0:T(8,128)S(1)}, f32[4,2,80,128]{3,2,1,0:T(8,128)S(1)}, u32[]{:S(2)}, u32[]{:S(2)}) %collective-permute-start.14) | collective-permute-done | bytes 327712 | tf_op jit(solution)/shard_map/ppermute | solution.py:577
  (28 shorter events, 6.7 us)
Async XLA Ops:
  0.0 1.2 %copy-start = (f32[1,4,4,64,256]{4,3,2,1,0:T(8,128)S(1)}, f32[1,4,4,64,256]{4,3,2,1,0:T(8,128)}, u32[]{:S(2)}) copy-start(f32[1,4,4,64,256]{4,3,2,1,0:T(8,128)} %guess_ref.1) | copy-start | bytes 3145732
  2.1 11.6 %collective-permute-start.2 = (f32[4,2,104,128]{3,2,1,0:T(8,128)S(1)}, f32[4,2,104,128]{3,2,1,0:T(8,128)S(1)}, u32[]{:S(2)}, u32[]{:S(2)}) collective-permute-start(f32[4,2,104,128]{3,2,1,0:T(8,128)S(1)} %get-tuple-element.40), channel_id=1, source_target_pairs={{0,8},{8,0},{16,24},{24,16},{1,9},{9,1},{17,25},{25,17},{2,10},{10... | collective-permute-start | bytes 1277960 | tf_op jit(solution)/shard_map/ppermute | solution.py:577
  3.7 11.3 %collective-permute-start.5 = (f32[4,2,104,128]{3,2,1,0:T(8,128)S(1)}, f32[4,2,104,128]{3,2,1,0:T(8,128)S(1)}, u32[]{:S(2)}, u32[]{:S(2)}) collective-permute-start(f32[4,2,104,128]{3,2,1,0:T(8,128)S(1)} %get-tuple-element.41), channel_id=1, source_target_pairs={{0,16},{8,24},{16,0},{24,8},{1,17},{9,25},{17,1},{25,9},{2,18},{10... | collective-permute-start | bytes 1277960 | tf_op jit(solution)/shard_map/ppermute | solution.py:577
  5.2 1.2 %copy-start.1 = (f32[1,4,4,64,256]{4,3,2,1,0:T(8,128)S(1)}, f32[1,4,4,64,256]{4,3,2,1,0:T(8,128)}, u32[]{:S(2)}) copy-start(f32[1,4,4,64,256]{4,3,2,1,0:T(8,128)} %guess_ref.1) | copy-start | bytes 3145732
  6.4 1.2 %copy-start.2 = (f32[4,4,64,256]{3,2,1,0:T(8,128)S(1)}, f32[4,4,64,256]{3,2,1,0:T(8,128)}, u32[]{:S(2)}) copy-start(f32[4,4,64,256]{3,2,1,0:T(8,128)} %start_hbm.1) | copy-start | bytes 3145732
  7.6 0.9 %copy-start.3 = (s32[4,64,256]{2,1,0:T(8,128)S(1)}, s32[4,64,256]{2,1,0:T(8,128)}, u32[]{:S(2)}) copy-start(s32[4,64,256]{2,1,0:T(8,128)} %heat_hbm.1) | copy-start | bytes 786436
  8.6 0.9 %copy-start.4 = (s32[4,64,256]{2,1,0:T(8,128)S(1)}, s32[4,64,256]{2,1,0:T(8,128)}, u32[]{:S(2)}) copy-start(s32[4,64,256]{2,1,0:T(8,128)} %solid_hbm.1) | copy-start | bytes 786436
  10.4 16.4 %collective-permute-start.1 = (f32[1120,128]{1,0:T(8,128)S(1)}, f32[1120,128]{1,0:T(8,128)S(1)}, u32[]{:S(2)}, u32[]{:S(2)}) collective-permute-start(f32[1120,128]{1,0:T(8,128)S(1)} %get-tuple-element.36), channel_id=1, source_target_pairs={{1,2},{3,4},{5,6},{2,1},{4,3},{6,5},{9,10},{11,12},{13,14},{10,9},... | collective-permute-start | bytes 1720328 | tf_op jit(solution)/shard_map/ppermute | solution.py:583
  15.0 11.8 %collective-permute-start.8 = (f32[4,2,104,128]{3,2,1,0:T(8,128)S(1)}, f32[4,2,104,128]{3,2,1,0:T(8,128)S(1)}, u32[]{:S(2)}, u32[]{:S(2)}) collective-permute-start(f32[4,2,104,128]{3,2,1,0:T(8,128)S(1)} %get-tuple-element.43), channel_id=1, source_target_pairs={{0,24},{8,16},{16,8},{24,0},{1,25},{9,17},{17,9},{25,1},{2,26},{10... | collective-permute-start | bytes 1277960 | tf_op jit(solution)/shard_map/ppermute | solution.py:577
  16.4 13.6 %collective-permute-start = (f32[10,2,80,128]{3,2,1,0:T(8,128)S(1)}, f32[10,2,80,128]{3,2,1,0:T(8,128)S(1)}, u32[]{:S(2)}, u32[]{:S(2)}) collective-permute-start(f32[10,2,80,128]{3,2,1,0:T(8,128)S(1)} %get-tuple-element.35), channel_id=1, source_target_pairs={{0,1},{1,0},{2,3},{3,2},{4,5},{5,4},{6,7},{7,6},{8,9},{9,8},{10,11... | collective-permute-start | bytes 2457608 | tf_op jit(solution)/shard_map/ppermute | solution.py:583
  16.5 10.9 %collective-permute-start.4 = (f32[552,128]{1,0:T(8,128)S(1)}, f32[552,128]{1,0:T(8,128)S(1)}, u32[]{:S(2)}, u32[]{:S(2)}) collective-permute-start(f32[552,128]{1,0:T(8,128)S(1)} %trim.3), channel_id=1, source_target_pairs={{1,2},{3,4},{5,6},{2,1},{4,3},{6,5},{9,10},{11,12},{13,14},{10,9},... | collective-permute-start | bytes 847880 | tf_op jit(solution)/shard_map/ppermute | solution.py:583
  19.0 8.5 %collective-permute-start.7 = (f32[552,128]{1,0:T(8,128)S(1)}, f32[552,128]{1,0:T(8,128)S(1)}, u32[]{:S(2)}, u32[]{:S(2)}) collective-permute-start(f32[552,128]{1,0:T(8,128)S(1)} %trim.4), channel_id=1, source_target_pairs={{1,2},{3,4},{5,6},{2,1},{4,3},{6,5},{9,10},{11,12},{13,14},{10,9},... | collective-permute-start | bytes 847880 | tf_op jit(solution)/shard_map/ppermute | solution.py:583
  26.7 3.3 %collective-permute-start.3 = (f32[4,2,104,128]{3,2,1,0:T(8,128)S(1)}, f32[4,2,104,128]{3,2,1,0:T(8,128)S(1)}, u32[]{:S(2)}, u32[]{:S(2)}) collective-permute-start(f32[4,2,104,128]{3,2,1,0:T(8,128)S(1)} %collective-permute-done.2.own_ref.refs_4_), channel_id=1, source_target_pairs={{0,1},{1,0},{2,3},{3,2},{4,5},{5,4},{6,7},{7,6},{8,9},{9,8},{10,11... | collective-permute-start | bytes 1277960 | tf_op jit(solution)/shard_map/ppermute | solution.py:583
  26.8 3.3 %collective-permute-start.6 = (f32[4,2,104,128]{3,2,1,0:T(8,128)S(1)}, f32[4,2,104,128]{3,2,1,0:T(8,128)S(1)}, u32[]{:S(2)}, u32[]{:S(2)}) collective-permute-start(f32[4,2,104,128]{3,2,1,0:T(8,128)S(1)} %collective-permute-done.5.own_ref.refs_7_), channel_id=1, source_target_pairs={{0,1},{1,0},{2,3},{3,2},{4,5},{5,4},{6,7},{7,6},{8,9},{9,8},{10,11... | collective-permute-start | bytes 1277960 | tf_op jit(solution)/shard_map/ppermute | solution.py:583
  27.4 2.7 %collective-permute-start.9 = (f32[4,2,104,128]{3,2,1,0:T(8,128)S(1)}, f32[4,2,104,128]{3,2,1,0:T(8,128)S(1)}, u32[]{:S(2)}, u32[]{:S(2)}) collective-permute-start(f32[4,2,104,128]{3,2,1,0:T(8,128)S(1)} %collective-permute-done.8.own_ref.refs_10_), channel_id=1, source_target_pairs={{0,1},{1,0},{2,3},{3,2},{4,5},{5,4},{6,7},{7,6},{8,9},{9,8},{10,11... | collective-permute-start | bytes 1277960 | tf_op jit(solution)/shard_map/ppermute | solution.py:583
  27.5 8.0 %collective-permute-start.10 = (f32[552,128]{1,0:T(8,128)S(1)}, f32[552,128]{1,0:T(8,128)S(1)}, u32[]{:S(2)}, u32[]{:S(2)}) collective-permute-start(f32[552,128]{1,0:T(8,128)S(1)} %trim.5), channel_id=1, source_target_pairs={{1,2},{3,4},{5,6},{2,1},{4,3},{6,5},{9,10},{11,12},{13,14},{10,9},... | collective-permute-start | bytes 847880 | tf_op jit(solution)/shard_map/ppermute | solution.py:583
  39.4 3.8 %collective-permute-start.11 = (f32[4,4,2,80,128]{4,3,2,1,0:T(8,128)S(1)}, f32[4,4,2,80,128]{4,3,2,1,0:T(8,128)S(1)}, u32[]{:S(2)}, u32[]{:S(2)}) collective-permute-start(f32[4,4,2,80,128]{4,3,2,1,0:T(8,128)S(1)} %get-tuple-element.53), channel_id=1, source_target_pairs={{0,1},{1,0},{2,3},{3,2},{4,5},{5,4},{6,7},{7,6},{8,9},{9,8},{10,11... | collective-permute-start | bytes 3932168 | tf_op jit(solution)/shard_map/ppermute | solution.py:583
  40.6 15.4 %collective-permute-start.12 = (f32[4,480,128]{2,1,0:T(8,128)S(1)}, f32[4,480,128]{2,1,0:T(8,128)S(1)}, u32[]{:S(2)}, u32[]{:S(2)}) collective-permute-start(f32[4,480,128]{2,1,0:T(8,128)S(1)} %get-tuple-element.58), channel_id=1, source_target_pairs={{1,2},{3,4},{5,6},{2,1},{4,3},{6,5},{9,10},{11,12},{13,14},{10,9},... | collective-permute-start | bytes 2949128 | tf_op jit(solution)/shard_map/ppermute | solution.py:583
  60.1 10.6 %collective-permute-start.13 = (f32[4,2,80,128]{3,2,1,0:T(8,128)S(1)}, f32[4,2,80,128]{3,2,1,0:T(8,128)S(1)}, u32[]{:S(2)}, u32[]{:S(2)}) collective-permute-start(f32[4,2,80,128]{3,2,1,0:T(8,128)S(1)} %get-tuple-element.60), channel_id=1, source_target_pairs={{0,8},{8,0},{16,24},{24,16},{1,9},{9,1},{17,25},{25,17},{2,10},{10... | collective-permute-start | bytes 983048 | tf_op jit(solution)/shard_map/ppermute | solution.py:577
  61.6 16.5 %collective-permute-start.14 = (f32[4,2,80,128]{3,2,1,0:T(8,128)S(1)}, f32[4,2,80,128]{3,2,1,0:T(8,128)S(1)}, u32[]{:S(2)}, u32[]{:S(2)}) collective-permute-start(f32[4,2,80,128]{3,2,1,0:T(8,128)S(1)} %get-tuple-element.61), channel_id=1, source_target_pairs={{0,16},{8,24},{16,0},{24,8},{1,17},{9,25},{17,1},{25,9},{2,18},{10... | collective-permute-start | bytes 983048 | tf_op jit(solution)/shard_map/ppermute | solution.py:577
  62.1 16.0 %collective-permute-start.15 = (f32[4,2,80,128]{3,2,1,0:T(8,128)S(1)}, f32[4,2,80,128]{3,2,1,0:T(8,128)S(1)}, u32[]{:S(2)}, u32[]{:S(2)}) collective-permute-start(f32[4,2,80,128]{3,2,1,0:T(8,128)S(1)} %get-tuple-element.62), channel_id=1, source_target_pairs={{0,24},{8,16},{16,8},{24,0},{1,25},{9,17},{17,9},{25,1},{2,26},{10... | collective-permute-start | bytes 983048 | tf_op jit(solution)/shard_map/ppermute | solution.py:577
